TPU v7x, 32 devices: a whole 2x2x4 slice. The times are simulated.
32 devices in a mesh: grp: 16 (over z, x, core), tile: 2 (over y).
Axes of the slice: x: 2, y: 2, z: 4, core: 2. Of those that a mesh axis runs over, the one named last changes fastest.
Arguments:
- spectrum: float32 [1152, 64, 256], P(None, 'tile', 'grp'), may hold values from 0.05 to 2
- matrices: bfloat16 [2, 16, 2, 1152, 1152], P('tile', 'grp'), may hold values from -0.1875 to 0.1875
- ownership: int32 [64, 256], P('tile', 'grp'), may hold values from 0 to 1
- land_mask: int32 [64, 256], P('tile', 'grp'), may hold values 0 or 1
- courant: float32 [2, 1152], replicated, may hold values from -0.45 to 0.45
- stokes_weight: bfloat16 [1152, 256], replicated, may hold values from -0.1875 to 0.1875
- ocean: float32 [4, 64, 256, 128], P(None, 'tile', 'grp'), may hold values from -6 to 6
Outputs:
- spectrum_out: float32 [1152, 64, 256], P(None, 'tile', 'grp')
- ocean_out: float32 [4, 64, 256, 128], P(None, 'tile', 'grp')
All inputs are finite; a program needn't handle non-finite values. No bound on the sum of `land_mask` on one device may be relied on, other than what follows from the above.
Results may differ from a plain program's by a relative error of at most 0.0021.
Values sent between devices are 32-bit elements; how exact they have to be, the bound alone decides.
No kernel may reach another device: no remote copies, remote signals or barrier semaphores. Data moves between devices by JAX's collectives and lax.ppermute only.
A program may use at most 128 MiB of HBM per device.

v0:
```python
import jax
import jax.numpy as jnp
from jax import lax
from jax.sharding import PartitionSpec as P

STEPS = 2


current_gain = 0.2
source_gain = 0.5
mixing_side = 0.15
mixing_depth = 0.2
rotation = 0.3
transport = 0.5


def with_halo(cells, sides, width):
    for axis, dim in sides:
        count = lax.axis_size(axis)
        ends = count - 1
        head = lax.slice_in_dim(cells, 0, width, axis=dim)
        tail = lax.slice_in_dim(cells, cells.shape[dim] - width, cells.shape[dim], axis=dim)
        cells = jnp.concatenate(
            [
                lax.ppermute(tail, axis, [(i, (i + 1) % count) for i in range(ends)]),
                cells,
                lax.ppermute(head, axis, [((i + 1) % count, i) for i in range(ends)]),
            ],
            axis=dim,
        )
    return cells


def upwind(padded, speed_x, speed_y, sea_mask):
    middle = padded[:, 1:-1, 1:-1]
    western = padded[:, 1:-1, :-2]
    eastern = padded[:, 1:-1, 2:]
    northern = padded[:, :-2, 1:-1]
    southern = padded[:, 2:, 1:-1]
    flux = jnp.maximum(speed_x, 0.0) * (middle - western) + jnp.minimum(speed_x, 0.0) * (
        eastern - middle
    )
    flux = (
        flux
        + jnp.maximum(speed_y, 0.0) * (middle - northern)
        + jnp.minimum(speed_y, 0.0) * (southern - middle)
    )
    return sea_mask[None] * (middle - flux)


def ocean_step(fields, padded, drift, sea_mask):
    northern = padded[:, :-2, 1:-1]
    southern = padded[:, 2:, 1:-1]
    western = padded[:, 1:-1, :-2]
    eastern = padded[:, 1:-1, 2:]
    lateral = northern + southern + western + eastern - 4.0 * fields
    column = jnp.pad(fields, ((0, 0), (0, 0), (0, 0), (1, 1)))
    vertical = column[..., 2:] + column[..., :-2] - 2.0 * fields
    mixing = mixing_side * lateral + mixing_depth * vertical
    tend_u = mixing[0] + rotation * (fields[1] + drift[1])
    tend_v = mixing[1] - rotation * (fields[0] + drift[0])
    grad_x = 0.5 * (eastern[2:] - western[2:])
    grad_y = 0.5 * (southern[2:] - northern[2:])
    tend_tracer = mixing[2:] - transport * (drift[0][None] * grad_x + drift[1][None] * grad_y)
    tendency = jnp.concatenate([tend_u[None], tend_v[None], tend_tracer], 0)
    return fields + sea_mask[None, :, :, None] * tendency


def local(spectrum, matrices, ownership, land_mask, courant, stokes_weight, ocean):
    sea_mask = land_mask.astype(jnp.float32)
    matrix_set = matrices.reshape(matrices.shape[2:])
    count = matrix_set.shape[0]
    bins_all = spectrum.shape[0]
    block_rows = spectrum.shape[1]
    block_cols = spectrum.shape[2]
    levels_count = ocean.shape[3]
    owner_flat = ownership.reshape(1, 1, block_rows * block_cols)
    choices_range = jnp.arange(count, dtype=jnp.int32)[:, None, None]
    profile = stokes_weight.reshape(bins_all, 2, levels_count)
    energy = spectrum
    fields = ocean
    for step in range(STEPS):
        current = fields[0:2, :, :, 0]
        speed_x = courant[0][:, None, None] + current_gain * current[0][None]
        speed_y = courant[1][:, None, None] + current_gain * current[1][None]
        padded = with_halo(energy, (("grp", 2), ("tile", 1)), 1)
        advected = upwind(padded, speed_x, speed_y, sea_mask)
        flattened = advected.astype(jnp.bfloat16).reshape(bins_all, block_rows * block_cols)
        products = jnp.einsum(
            "mab,bp->map", matrix_set, flattened, preferred_element_type=jnp.float32
        )
        select = (owner_flat == choices_range).astype(jnp.float32)
        source = jnp.sum(select * products, axis=0).reshape(bins_all, block_rows, block_cols)
        energy = sea_mask[None] * (advected + source_gain * source)
        drift = jnp.einsum(
            "brc,bkl->krcl",
            energy.astype(jnp.bfloat16),
            profile,
            preferred_element_type=jnp.float32,
        )
        padded_ocean = with_halo(fields, (("grp", 2), ("tile", 1)), 1)
        fields = ocean_step(fields, padded_ocean, drift, sea_mask)
    return (energy, fields)


def solution(mesh):
    in_specs = (
        P(None, "tile", "grp"),
        P("tile", "grp", None, None, None),
        P("tile", "grp"),
        P("tile", "grp"),
        P(),
        P(),
        P(None, "tile", "grp", None),
    )
    out_specs = (P(None, "tile", "grp"), P(None, "tile", "grp", None))
    return jax.shard_map(local, mesh=mesh, in_specs=in_specs, out_specs=out_specs, check_vma=False)
```

profile of v0, /device:TPU:20, one launch (start us, length us, event | category | flops | bytes accessed | tf_op | source)
XLA Modules:
  0.0 90.3 jit_solution(7397108664289433759)
XLA Ops:
  0.6 1.9 %fusion.92 = (f32[1152,32,1]{0,2,1:T(1,128)S(1)}, f32[1152,32,1]{0,2,1:T(1,128)S(1)}) fusion(f32[1152,32,16]{0,2,1:T(8,128)} %param.7), kind=kLoop, calls=%fused_computation.173 | loop fusion | bytes 589824 | tf_op jit(solution)/shard_map/slice | solution.py:22
  2.6 2.9 %collective-permute-start.1 = (f32[1152,32,1]{0,1,2:T(8,128)S(1)}, f32[1152,32,1]{0,1,2:T(8,128)S(1)}, u32[]{:S(2)}, u32[]{:S(2)}) collective-permute-start(f32[1152,32,1]{0,1,2:T(8,128)S(1)} %copy.138), channel_id=1, source_target_pairs={{2,0},{4,2},{6,4},{8,6},{10,8},{12,10},{14,12},{16,14},{18,16},{20... | collective-permute-start | bytes 442376 | tf_op jit(solution)/shard_map/ppermute | solution.py:27
  5.5 0.7 copy.137
  6.1 1.9 %collective-permute-start = (f32[1152,32,1]{0,1,2:T(8,128)}, f32[1152,32,1]{0,1,2:T(8,128)}, u32[]{:S(2)}, u32[]{:S(2)}) collective-permute-start(f32[1152,32,1]{0,1,2:T(8,128)} %copy.137), channel_id=1, source_target_pairs={{0,2},{2,4},{4,6},{6,8},{8,10},{10,12},{12,14},{14,16},{16,18},{18... | collective-permute-start | bytes 442376 | tf_op jit(solution)/shard_map/ppermute | solution.py:25
  8.1 1.6 %copy.90 = f32[4,32,16,128]{3,1,0,2:T(8,128)S(1)} copy(f32[4,32,16,128]{3,2,1,0:T(8,128)} %param.13) | data formatting | bytes 2097152 | tf_op args[6]
  9.6 0.6 fusion.95
  10.3 2.7 %collective-permute-start.4 = (f32[4,32,1,128]{3,1,0,2:T(8,128)}, f32[4,32,1,128]{3,1,0,2:T(8,128)}, u32[]{:S(2)}, u32[]{:S(2)}) collective-permute-start(f32[4,32,1,128]{3,1,0,2:T(8,128)} %get-tuple-element.42), channel_id=1, source_target_pairs={{0,2},{2,4},{4,6},{6,8},{8,10},{10,12},{12,14},{14,16},{16,18},{18... | collective-permute-start | bytes 196616 | tf_op jit(solution)/shard_map/ppermute | solution.py:25
  13.0 3.8 %collective-permute-start.5 = (f32[4,32,1,128]{3,1,0,2:T(8,128)}, f32[4,32,1,128]{3,1,0,2:T(8,128)}, u32[]{:S(2)}, u32[]{:S(2)}) collective-permute-start(f32[4,32,1,128]{3,1,0,2:T(8,128)} %get-tuple-element.41), channel_id=1, source_target_pairs={{2,0},{4,2},{6,4},{8,6},{10,8},{12,10},{14,12},{16,14},{18,16},{20... | collective-permute-start | bytes 196616 | tf_op jit(solution)/shard_map/ppermute | solution.py:27
  16.8 0.3 copy.130
  17.1 0.3 copy.129
  17.4 0.1 copy.89
  17.5 0.1 copy.100
  17.5 0.1 eq.13
  17.7 0.8 constant_dynamic-update-slice_fusion.4
  18.6 0.5 constant_dynamic-update-slice_fusion.6
  19.0 1.1 %constant_dynamic-update-slice_fusion.5 = (f32[4,32,17,128]{3,1,0,2:T(8,128)S(1)}, f32[4,32,18,128]{3,1,0,2:T(8,128)S(1)}) fusion(f32[4,32,17,128]{3,1,0,2:T(8,128)S(1)} %get-tuple-element.38, f32[4,32,1,128]{3,1,0,2:T(8,128)} %collective-permute-done.5, f32[4,32,18,128]{3,1,0,2:T(8,128)S(1)} %get-tuple-element.39), kind=kLoop, calls=%fused_computation.165 | loop fusion | bytes 196608 | tf_op jit(solution)/shard_map/concatenate | solution.py:23
  20.2 1.3 %collective-permute-start.6 = (f32[4,1,18,128]{3,1,0,2:T(1,128)S(1)}, f32[4,1,18,128]{3,1,0,2:T(1,128)S(1)}, u32[]{:S(2)}, u32[]{:S(2)}) collective-permute-start(f32[4,1,18,128]{3,1,0,2:T(1,128)S(1)} %get-tuple-element.33), channel_id=1, source_target_pairs={{0,1},{2,3},{4,5},{6,7},{8,9},{10,11},{12,13},{14,15},{16,17},{18,... | collective-permute-start | bytes 110600 | tf_op jit(solution)/shard_map/ppermute | solution.py:25
  21.5 4.5 %collective-permute-start.7 = (f32[4,1,18,128]{3,1,0,2:T(1,128)S(1)}, f32[4,1,18,128]{3,1,0,2:T(1,128)S(1)}, u32[]{:S(2)}, u32[]{:S(2)}) collective-permute-start(f32[4,1,18,128]{3,1,0,2:T(1,128)S(1)} %get-tuple-element.32), channel_id=1, source_target_pairs={{1,0},{3,2},{5,4},{7,6},{9,8},{11,10},{13,12},{15,14},{17,16},{19,... | collective-permute-start | bytes 110600 | tf_op jit(solution)/shard_map/ppermute | solution.py:27
  26.0 0.2 copy.95
  26.2 1.1 %copy.93 = f32[1152,32,1]{0,2,1:T(1,128)S(1)} copy(f32[1152,32,1]{0,1,2:T(8,128)} %collective-permute-done) | data formatting | bytes 294912 | tf_op jit(solution)/shard_map/ppermute | solution.py:25
  27.3 1.7 %collective-permute-start.3 = (f32[1152,1,18]{0,2,1:T(8,128)S(1)}, f32[1152,1,18]{0,2,1:T(8,128)S(1)}, u32[]{:S(2)}, u32[]{:S(2)}) collective-permute-start(f32[1152,1,18]{0,2,1:T(8,128)S(1)} %get-tuple-element.19), channel_id=1, source_target_pairs={{1,0},{3,2},{5,4},{7,6},{9,8},{11,10},{13,12},{15,14},{17,16},{19,... | collective-permute-start | bytes 248840 | tf_op jit(solution)/shard_map/ppermute | solution.py:27
  29.0 1.3 %collective-permute-start.2 = (f32[1152,1,18]{0,2,1:T(8,128)S(1)}, f32[1152,1,18]{0,2,1:T(8,128)S(1)}, u32[]{:S(2)}, u32[]{:S(2)}) collective-permute-start(f32[1152,1,18]{0,2,1:T(8,128)S(1)} %get-tuple-element.18), channel_id=1, source_target_pairs={{0,1},{2,3},{4,5},{6,7},{8,9},{10,11},{12,13},{14,15},{16,17},{18,... | collective-permute-start | bytes 248840 | tf_op jit(solution)/shard_map/ppermute | solution.py:25
  30.4 0.9 %fusion.55 = f32[4,32,16,128]{3,1,0,2:T(8,128)S(1)} fusion(f32[4,32,18,128]{3,1,0,2:T(8,128)S(1)} %get-tuple-element.50, f32[4,1,18,128]{3,1,0,2:T(1,128)S(1)} %collective-permute-done.7, f32[4,1,18,128]{3,1,0,2:T(1,128)S(1)} %collective-permute-done.6, f32[4,32,16,128]{3,1,0,2:T(8,128)S(1)} %copy.90, f32[4,32,17,128]{3,1,0,2:T(8,128)S(1)} %get-tuple-element.49, ...), kind=kLoop, calls=%fused_computation.95 | loop fusion | flops 3407872 | bytes 5447680 | tf_op jit(solution)/shard_map/add | solution.py:59
  31.3 0.3 collective-permute-done.3
  31.6 4.1 %collective-permute-done.2 = f32[1152,1,18]{0,2,1:T(8,128)S(1)} collective-permute-done((f32[1152,1,18]{0,2,1:T(8,128)S(1)}, f32[1152,1,18]{0,2,1:T(8,128)S(1)}, u32[]{:S(2)}, u32[]{:S(2)}) %collective-permute-start.2) | collective-permute-done | bytes 82976 | tf_op jit(solution)/shard_map/ppermute | solution.py:25
  35.7 3.6 %fusion.89 = (bf16[1152,32,16]{0,2,1:T(8,128)(2,1)S(1)}, f32[1152,32,16]{0,2,1:T(8,128)S(1)}) fusion(f32[1152,32,16]{0,2,1:T(8,128)S(1)} %copy-done.3, f32[1152,1,18]{0,2,1:T(8,128)S(1)} %collective-permute-done.3, f32[1152,32,1]{0,2,1:T(1,128)S(1)} %copy.95, f32[1152,32,1]{0,2,1:T(1,128)S(1)} %copy.93, f32[1152,1,18]{0,2,1:T(8,128)S(1)} %collective-permute-done.2, ...), kind=kLoop, calls=%fused_computation.171 | loop fusion | flops 16515072 | bytes 6374400 | tf_op jit(solution)/shard_map/convert_element_type | solution.py:88
  39.4 3.7 %fusion.5 = f32[1152,512]{0,1:T(8,128)S(1)} fusion(bf16[1152,512,1]{0,1,2:T(8,128)(2,1)S(1)} %bitcast.76, bf16[1,1,2,1152,1152]{4,3,2,1,0:T(8,128)(2,1)S(1)} %bitcast.82, f32[2,512]{1,0:T(2,128)S(1)} %compare_convert_fusion), kind=kOutput, calls=%fused_computation.7 | convolution fusion | flops 2719678464 | bytes 8851456 | tf_op jit(solution)/shard_map/mab,bp->map/dot_general | solution.py:89
  43.1 0.2 broadcast_multiply_fusion.1
  43.2 0.3 add_multiply_fusion.1
  43.6 0.5 fusion.38
  44.1 0.3 copy.155
  44.4 0.2 fusion.86
  44.6 0.4 fusion.75
  45.0 0.5 fusion.63
  45.5 2.9 %collective-permute-start.13 = (f32[4,32,1,128]{3,1,0,2:T(8,128)S(1)}, f32[4,32,1,128]{3,1,0,2:T(8,128)S(1)}, u32[]{:S(2)}, u32[]{:S(2)}) collective-permute-start(f32[4,32,1,128]{3,1,0,2:T(8,128)S(1)} %get-tuple-element.35), channel_id=1, source_target_pairs={{2,0},{4,2},{6,4},{8,6},{10,8},{12,10},{14,12},{16,14},{18,16},{20... | collective-permute-start | bytes 196616 | tf_op jit(solution)/shard_map/ppermute | solution.py:27
  48.4 1.9 %collective-permute-start.12 = (f32[4,32,1,128]{3,1,0,2:T(8,128)S(1)}, f32[4,32,1,128]{3,1,0,2:T(8,128)S(1)}, u32[]{:S(2)}, u32[]{:S(2)}) collective-permute-start(f32[4,32,1,128]{3,1,0,2:T(8,128)S(1)} %get-tuple-element.34), channel_id=1, source_target_pairs={{0,2},{2,4},{4,6},{6,8},{8,10},{10,12},{12,14},{14,16},{16,18},{18... | collective-permute-start | bytes 196616 | tf_op jit(solution)/shard_map/ppermute | solution.py:25
  50.4 0.2 fusion.91
  50.6 4.3 %collective-permute-done.12 = f32[4,32,1,128]{3,1,0,2:T(8,128)S(1)} collective-permute-done((f32[4,32,1,128]{3,1,0,2:T(8,128)S(1)}, f32[4,32,1,128]{3,1,0,2:T(8,128)S(1)}, u32[]{:S(2)}, u32[]{:S(2)}) %collective-permute-start.12) | collective-permute-done | bytes 65568 | tf_op jit(solution)/shard_map/ppermute | solution.py:25
  55.0 1.3 %collective-permute-start.14 = (f32[4,1,18,128]{3,1,0,2:T(1,128)S(1)}, f32[4,1,18,128]{3,1,0,2:T(1,128)S(1)}, u32[]{:S(2)}, u32[]{:S(2)}) collective-permute-start(f32[4,1,18,128]{3,1,0,2:T(1,128)S(1)} %get-tuple-element.31), channel_id=1, source_target_pairs={{0,1},{2,3},{4,5},{6,7},{8,9},{10,11},{12,13},{14,15},{16,17},{18,... | collective-permute-start | bytes 110600 | tf_op jit(solution)/shard_map/ppermute | solution.py:25
  56.3 4.5 %collective-permute-start.15 = (f32[4,1,18,128]{3,1,0,2:T(1,128)S(1)}, f32[4,1,18,128]{3,1,0,2:T(1,128)S(1)}, u32[]{:S(2)}, u32[]{:S(2)}) collective-permute-start(f32[4,1,18,128]{3,1,0,2:T(1,128)S(1)} %get-tuple-element.30), channel_id=1, source_target_pairs={{1,0},{3,2},{5,4},{7,6},{9,8},{11,10},{13,12},{15,14},{17,16},{19,... | collective-permute-start | bytes 110600 | tf_op jit(solution)/shard_map/ppermute | solution.py:27
  60.9 1.9 %collective-permute-start.9 = (f32[1152,32,1]{0,1,2:T(8,128)S(1)}, f32[1152,32,1]{0,1,2:T(8,128)S(1)}, u32[]{:S(2)}, u32[]{:S(2)}) collective-permute-start(f32[1152,32,1]{0,1,2:T(8,128)S(1)} %copy.117), channel_id=1, source_target_pairs={{2,0},{4,2},{6,4},{8,6},{10,8},{12,10},{14,12},{16,14},{18,16},{20... | collective-permute-start | bytes 442376 | tf_op jit(solution)/shard_map/ppermute | solution.py:27
  62.9 2.4 %collective-permute-start.8 = (f32[1152,32,1]{0,1,2:T(8,128)S(1)}, f32[1152,32,1]{0,1,2:T(8,128)S(1)}, u32[]{:S(2)}, u32[]{:S(2)}) collective-permute-start(f32[1152,32,1]{0,1,2:T(8,128)S(1)} %copy.115), channel_id=1, source_target_pairs={{0,2},{2,4},{4,6},{6,8},{8,10},{10,12},{12,14},{14,16},{16,18},{18... | collective-permute-start | bytes 442376 | tf_op jit(solution)/shard_map/ppermute | solution.py:25
  65.3 0.3 copy.134
  65.6 0.3 copy.133
  65.8 0.3 maximum_maximum_fusion
  66.2 0.2 copy.118
  66.4 3.9 %collective-permute-done.8 = f32[1152,32,1]{0,1,2:T(8,128)S(1)} collective-permute-done((f32[1152,32,1]{0,1,2:T(8,128)S(1)}, f32[1152,32,1]{0,1,2:T(8,128)S(1)}, u32[]{:S(2)}, u32[]{:S(2)}) %collective-permute-start.8) | collective-permute-done | bytes 147488 | tf_op jit(solution)/shard_map/ppermute | solution.py:25
  70.2 0.2 copy.116
  70.4 1.7 %collective-permute-start.11 = (f32[1152,1,18]{0,2,1:T(8,128)S(1)}, f32[1152,1,18]{0,2,1:T(8,128)S(1)}, u32[]{:S(2)}, u32[]{:S(2)}) collective-permute-start(f32[1152,1,18]{0,2,1:T(8,128)S(1)} %get-tuple-element.17), channel_id=1, source_target_pairs={{1,0},{3,2},{5,4},{7,6},{9,8},{11,10},{13,12},{15,14},{17,16},{19,... | collective-permute-start | bytes 248840 | tf_op jit(solution)/shard_map/ppermute | solution.py:27
  72.1 1.5 %collective-permute-start.10 = (f32[1152,1,18]{0,2,1:T(8,128)S(1)}, f32[1152,1,18]{0,2,1:T(8,128)S(1)}, u32[]{:S(2)}, u32[]{:S(2)}) collective-permute-start(f32[1152,1,18]{0,2,1:T(8,128)S(1)} %get-tuple-element.16), channel_id=1, source_target_pairs={{0,1},{2,3},{4,5},{6,7},{8,9},{10,11},{12,13},{14,15},{16,17},{18,... | collective-permute-start | bytes 248840 | tf_op jit(solution)/shard_map/ppermute | solution.py:25
  73.6 0.6 fusion.46
  74.3 0.2 collective-permute-done.11
  74.5 4.3 %collective-permute-done.10 = f32[1152,1,18]{0,2,1:T(8,128)S(1)} collective-permute-done((f32[1152,1,18]{0,2,1:T(8,128)S(1)}, f32[1152,1,18]{0,2,1:T(8,128)S(1)}, u32[]{:S(2)}, u32[]{:S(2)}) %collective-permute-start.10) | collective-permute-done | bytes 82976 | tf_op jit(solution)/shard_map/ppermute | solution.py:25
  78.8 3.6 %fusion.87 = (bf16[1152,32,16]{0,2,1:T(8,128)(2,1)S(1)}, f32[1152,32,16]{0,2,1:T(8,128)S(1)}) fusion(f32[1152,32,16]{0,2,1:T(8,128)S(1)} %copy-done.2, f32[1152,1,18]{0,2,1:T(8,128)S(1)} %collective-permute-done.11, f32[1152,32,1]{0,2,1:T(1,128)S(1)} %copy.118, f32[1152,32,1]{0,2,1:T(1,128)S(1)} %copy.116, f32[1152,1,18]{0,2,1:T(8,128)S(1)} %collective-permute-done.10, ...), kind=kLoop, calls=%fused_computation.170 | loop fusion | flops 16515072 | bytes 6374400 | tf_op jit(solution)/shard_map/convert_element_type | solution.py:88
  82.5 3.7 %fusion.4 = f32[1152,512]{0,1:T(8,128)S(1)} fusion(bf16[1152,512,1]{0,1,2:T(8,128)(2,1)S(1)} %bitcast.75, bf16[1,1,2,1152,1152]{4,3,2,1,0:T(8,128)(2,1)S(1)} %bitcast.84, f32[2,512]{1,0:T(2,128)S(1)} %compare_convert_fusion), kind=kOutput, calls=%fused_computation.5 | convolution fusion | flops 2719678464 | bytes 8851456 | tf_op jit(solution)/shard_map/mab,bp->map/dot_general | solution.py:89
  86.2 0.2 broadcast_multiply_fusion
  86.3 0.3 add_multiply_fusion
  86.7 0.5 fusion.36
  87.2 0.3 copy.154
  87.5 0.2 fusion.82
  87.7 0.4 copy-done.4
  88.1 0.3 fusion.68
  88.4 0.3 fusion.64
  88.7 1.6 %copy.124 = f32[4,32,16,128]{3,2,1,0:T(8,128)} copy(f32[4,32,16,128]{3,1,0,2:T(8,128)S(1)} %fusion.64) | data formatting | bytes 2097152
  (50 shorter events, 0.5 us)
Async XLA Ops:
  0.6 42.9 %copy-start = (bf16[1152,256]{1,0:T(8,128)(2,1)S(1)}, bf16[1152,256]{1,0:T(8,128)(2,1)}, u32[]{:S(2)}) copy-start(bf16[1152,256]{1,0:T(8,128)(2,1)} %param.12) | copy-start | bytes 1769476
  2.5 14.8 %copy-start.8 = (s32[32,16]{0,1:T(8,128)S(1)}, s32[32,16]{0,1:T(8,128)}, u32[]{:S(2)}) copy-start(s32[32,16]{0,1:T(8,128)} %param.10) | copy-start | bytes 6148
  2.6 14.9 %copy-start.7 = (s32[32,16]{0,1:T(8,128)S(1)}, s32[32,16]{0,1:T(8,128)}, u32[]{:S(2)}) copy-start(s32[32,16]{0,1:T(8,128)} %param.9) | copy-start | bytes 6148
  2.6 15.1 %copy-start.6 = (f32[2,1152]{1,0:T(2,128)S(1)}, f32[2,1152]{1,0:T(2,128)}, u32[]{:S(2)}) copy-start(f32[2,1152]{1,0:T(2,128)} %param.11) | copy-start | bytes 27652
  2.6 15.9 %copy-start.5 = (f32[4,32,16,128]{3,2,1,0:T(8,128)S(1)}, f32[4,32,16,128]{3,2,1,0:T(8,128)}, u32[]{:S(2)}) copy-start(f32[4,32,16,128]{3,2,1,0:T(8,128)} %param.13) | copy-start | bytes 3145732
  2.6 23.4 %collective-permute-start.1 = (f32[1152,32,1]{0,1,2:T(8,128)S(1)}, f32[1152,32,1]{0,1,2:T(8,128)S(1)}, u32[]{:S(2)}, u32[]{:S(2)}) collective-permute-start(f32[1152,32,1]{0,1,2:T(8,128)S(1)} %copy.138), channel_id=1, source_target_pairs={{2,0},{4,2},{6,4},{8,6},{10,8},{12,10},{14,12},{16,14},{18,16},{20... | collective-permute-start | bytes 442376 | tf_op jit(solution)/shard_map/ppermute | solution.py:27
  6.1 20.0 %collective-permute-start = (f32[1152,32,1]{0,1,2:T(8,128)}, f32[1152,32,1]{0,1,2:T(8,128)}, u32[]{:S(2)}, u32[]{:S(2)}) collective-permute-start(f32[1152,32,1]{0,1,2:T(8,128)} %copy.137), channel_id=1, source_target_pairs={{0,2},{2,4},{4,6},{6,8},{8,10},{10,12},{12,14},{14,16},{16,18},{18... | collective-permute-start | bytes 442376 | tf_op jit(solution)/shard_map/ppermute | solution.py:25
  10.3 7.4 %collective-permute-start.4 = (f32[4,32,1,128]{3,1,0,2:T(8,128)}, f32[4,32,1,128]{3,1,0,2:T(8,128)}, u32[]{:S(2)}, u32[]{:S(2)}) collective-permute-start(f32[4,32,1,128]{3,1,0,2:T(8,128)} %get-tuple-element.42), channel_id=1, source_target_pairs={{0,2},{2,4},{4,6},{6,8},{8,10},{10,12},{12,14},{14,16},{16,18},{18... | collective-permute-start | bytes 196616 | tf_op jit(solution)/shard_map/ppermute | solution.py:25
  13.0 6.1 %collective-permute-start.5 = (f32[4,32,1,128]{3,1,0,2:T(8,128)}, f32[4,32,1,128]{3,1,0,2:T(8,128)}, u32[]{:S(2)}, u32[]{:S(2)}) collective-permute-start(f32[4,32,1,128]{3,1,0,2:T(8,128)} %get-tuple-element.41), channel_id=1, source_target_pairs={{2,0},{4,2},{6,4},{8,6},{10,8},{12,10},{14,12},{16,14},{18,16},{20... | collective-permute-start | bytes 196616 | tf_op jit(solution)/shard_map/ppermute | solution.py:27
  18.5 8.7 %copy-start.3 = (f32[1152,32,16]{0,2,1:T(8,128)S(1)}, f32[1152,32,16]{0,2,1:T(8,128)}, u32[]{:S(2)}) copy-start(f32[1152,32,16]{0,2,1:T(8,128)} %param.7) | copy-start | bytes 7077892
  20.2 10.2 %collective-permute-start.6 = (f32[4,1,18,128]{3,1,0,2:T(1,128)S(1)}, f32[4,1,18,128]{3,1,0,2:T(1,128)S(1)}, u32[]{:S(2)}, u32[]{:S(2)}) collective-permute-start(f32[4,1,18,128]{3,1,0,2:T(1,128)S(1)} %get-tuple-element.33), channel_id=1, source_target_pairs={{0,1},{2,3},{4,5},{6,7},{8,9},{10,11},{12,13},{14,15},{16,17},{18,... | collective-permute-start | bytes 110600 | tf_op jit(solution)/shard_map/ppermute | solution.py:25
  21.5 8.9 %collective-permute-start.7 = (f32[4,1,18,128]{3,1,0,2:T(1,128)S(1)}, f32[4,1,18,128]{3,1,0,2:T(1,128)S(1)}, u32[]{:S(2)}, u32[]{:S(2)}) collective-permute-start(f32[4,1,18,128]{3,1,0,2:T(1,128)S(1)} %get-tuple-element.32), channel_id=1, source_target_pairs={{1,0},{3,2},{5,4},{7,6},{9,8},{11,10},{13,12},{15,14},{17,16},{19,... | collective-permute-start | bytes 110600 | tf_op jit(solution)/shard_map/ppermute | solution.py:27
  27.3 12.1 %slice-start = ((s8[5308416]{0:T(1024)(128)(4,1)}), s8[4194304]{0:T(1024)(128)(4,1)S(1)}, s32[]{:S(2)}) async-start(s8[5308416]{0:T(1024)(128)(4,1)} %bitcast.81), calls=%async_computation | async-start | bytes 8388608
  27.3 4.2 %collective-permute-start.3 = (f32[1152,1,18]{0,2,1:T(8,128)S(1)}, f32[1152,1,18]{0,2,1:T(8,128)S(1)}, u32[]{:S(2)}, u32[]{:S(2)}) collective-permute-start(f32[1152,1,18]{0,2,1:T(8,128)S(1)} %get-tuple-element.19), channel_id=1, source_target_pairs={{1,0},{3,2},{5,4},{7,6},{9,8},{11,10},{13,12},{15,14},{17,16},{19,... | collective-permute-start | bytes 248840 | tf_op jit(solution)/shard_map/ppermute | solution.py:27
  29.0 6.7 %collective-permute-start.2 = (f32[1152,1,18]{0,2,1:T(8,128)S(1)}, f32[1152,1,18]{0,2,1:T(8,128)S(1)}, u32[]{:S(2)}, u32[]{:S(2)}) collective-permute-start(f32[1152,1,18]{0,2,1:T(8,128)S(1)} %get-tuple-element.18), channel_id=1, source_target_pairs={{0,1},{2,3},{4,5},{6,7},{8,9},{10,11},{12,13},{14,15},{16,17},{18,... | collective-permute-start | bytes 248840 | tf_op jit(solution)/shard_map/ppermute | solution.py:25
  30.4 9.0 %slice-start.1 = ((s8[5308416]{0:T(1024)(128)(4,1)}), s8[1114112]{0:T(1024)(128)(4,1)S(1)}, s32[]{:S(2)}) async-start(s8[5308416]{0:T(1024)(128)(4,1)} %bitcast.81), calls=%async_computation.1 | async-start | bytes 2228224
  43.6 6.8 %copy-start.1 = (f32[1152,32,16]{0,2,1:T(8,128)}, f32[1152,32,16]{0,2,1:T(8,128)S(1)}, u32[]{:S(2)}) copy-start(f32[1152,32,16]{0,2,1:T(8,128)S(1)} %add_multiply_fusion.1) | copy-start | bytes 7077892
  45.5 5.1 %collective-permute-start.13 = (f32[4,32,1,128]{3,1,0,2:T(8,128)S(1)}, f32[4,32,1,128]{3,1,0,2:T(8,128)S(1)}, u32[]{:S(2)}, u32[]{:S(2)}) collective-permute-start(f32[4,32,1,128]{3,1,0,2:T(8,128)S(1)} %get-tuple-element.35), channel_id=1, source_target_pairs={{2,0},{4,2},{6,4},{8,6},{10,8},{12,10},{14,12},{16,14},{18,16},{20... | collective-permute-start | bytes 196616 | tf_op jit(solution)/shard_map/ppermute | solution.py:27
  48.4 6.5 %collective-permute-start.12 = (f32[4,32,1,128]{3,1,0,2:T(8,128)S(1)}, f32[4,32,1,128]{3,1,0,2:T(8,128)S(1)}, u32[]{:S(2)}, u32[]{:S(2)}) collective-permute-start(f32[4,32,1,128]{3,1,0,2:T(8,128)S(1)} %get-tuple-element.34), channel_id=1, source_target_pairs={{0,2},{2,4},{4,6},{6,8},{8,10},{10,12},{12,14},{14,16},{16,18},{18... | collective-permute-start | bytes 196616 | tf_op jit(solution)/shard_map/ppermute | solution.py:25
  55.0 10.9 %collective-permute-start.14 = (f32[4,1,18,128]{3,1,0,2:T(1,128)S(1)}, f32[4,1,18,128]{3,1,0,2:T(1,128)S(1)}, u32[]{:S(2)}, u32[]{:S(2)}) collective-permute-start(f32[4,1,18,128]{3,1,0,2:T(1,128)S(1)} %get-tuple-element.31), channel_id=1, source_target_pairs={{0,1},{2,3},{4,5},{6,7},{8,9},{10,11},{12,13},{14,15},{16,17},{18,... | collective-permute-start | bytes 110600 | tf_op jit(solution)/shard_map/ppermute | solution.py:25
  56.3 9.6 %collective-permute-start.15 = (f32[4,1,18,128]{3,1,0,2:T(1,128)S(1)}, f32[4,1,18,128]{3,1,0,2:T(1,128)S(1)}, u32[]{:S(2)}, u32[]{:S(2)}) collective-permute-start(f32[4,1,18,128]{3,1,0,2:T(1,128)S(1)} %get-tuple-element.30), channel_id=1, source_target_pairs={{1,0},{3,2},{5,4},{7,6},{9,8},{11,10},{13,12},{15,14},{17,16},{19,... | collective-permute-start | bytes 110600 | tf_op jit(solution)/shard_map/ppermute | solution.py:27
  60.9 5.3 %collective-permute-start.9 = (f32[1152,32,1]{0,1,2:T(8,128)S(1)}, f32[1152,32,1]{0,1,2:T(8,128)S(1)}, u32[]{:S(2)}, u32[]{:S(2)}) collective-permute-start(f32[1152,32,1]{0,1,2:T(8,128)S(1)} %copy.117), channel_id=1, source_target_pairs={{2,0},{4,2},{6,4},{8,6},{10,8},{12,10},{14,12},{16,14},{18,16},{20... | collective-permute-start | bytes 442376 | tf_op jit(solution)/shard_map/ppermute | solution.py:27
  62.9 7.4 %collective-permute-start.8 = (f32[1152,32,1]{0,1,2:T(8,128)S(1)}, f32[1152,32,1]{0,1,2:T(8,128)S(1)}, u32[]{:S(2)}, u32[]{:S(2)}) collective-permute-start(f32[1152,32,1]{0,1,2:T(8,128)S(1)} %copy.115), channel_id=1, source_target_pairs={{0,2},{2,4},{4,6},{6,8},{8,10},{10,12},{12,14},{14,16},{16,18},{18... | collective-permute-start | bytes 442376 | tf_op jit(solution)/shard_map/ppermute | solution.py:25
  65.8 4.5 %copy-start.2 = (f32[1152,32,16]{0,2,1:T(8,128)S(1)}, f32[1152,32,16]{0,2,1:T(8,128)}, u32[]{:S(2)}) copy-start(f32[1152,32,16]{0,2,1:T(8,128)} %copy-done.1) | copy-start | bytes 7077892
  70.4 12.0 %slice-start.2 = ((s8[5308416]{0:T(1024)(128)(4,1)}), s8[4194304]{0:T(1024)(128)(4,1)S(1)}, s32[]{:S(2)}) async-start(s8[5308416]{0:T(1024)(128)(4,1)} %bitcast.83), calls=%async_computation.2 | async-start | bytes 8388608
  70.4 4.0 %collective-permute-start.11 = (f32[1152,1,18]{0,2,1:T(8,128)S(1)}, f32[1152,1,18]{0,2,1:T(8,128)S(1)}, u32[]{:S(2)}, u32[]{:S(2)}) collective-permute-start(f32[1152,1,18]{0,2,1:T(8,128)S(1)} %get-tuple-element.17), channel_id=1, source_target_pairs={{1,0},{3,2},{5,4},{7,6},{9,8},{11,10},{13,12},{15,14},{17,16},{19,... | collective-permute-start | bytes 248840 | tf_op jit(solution)/shard_map/ppermute | solution.py:27
  72.1 6.6 %collective-permute-start.10 = (f32[1152,1,18]{0,2,1:T(8,128)S(1)}, f32[1152,1,18]{0,2,1:T(8,128)S(1)}, u32[]{:S(2)}, u32[]{:S(2)}) collective-permute-start(f32[1152,1,18]{0,2,1:T(8,128)S(1)} %get-tuple-element.16), channel_id=1, source_target_pairs={{0,1},{2,3},{4,5},{6,7},{8,9},{10,11},{12,13},{14,15},{16,17},{18,... | collective-permute-start | bytes 248840 | tf_op jit(solution)/shard_map/ppermute | solution.py:25
  73.6 8.8 %slice-start.3 = ((s8[5308416]{0:T(1024)(128)(4,1)}), s8[1114112]{0:T(1024)(128)(4,1)S(1)}, s32[]{:S(2)}) async-start(s8[5308416]{0:T(1024)(128)(4,1)} %bitcast.83), calls=%async_computation.3 | async-start | bytes 2228224
  86.7 1.4 %copy-start.4 = (f32[1152,32,16]{0,2,1:T(8,128)}, f32[1152,32,16]{0,2,1:T(8,128)S(1)}, u32[]{:S(2)}) copy-start(f32[1152,32,16]{0,2,1:T(8,128)S(1)} %add_multiply_fusion) | copy-start | bytes 7077892
where the time goes:
time: 90.9 us; the launch traced here: 90.3 us
  starting transfers between devices  38.2 us (42%)
  waiting for transfers between devices  17.1 us (19%)
  local copies, waits for them, and re-layouts  13 us (14%)
  other arithmetic  12.2 us (13%)
  matrix products  8.46 us (9%)
  between operations  1.27 us (1%)
    ppermute x8, starting transfers between devices, with_halo(): lax.ppermute(head, axis, [((i + 1) % count, i) for i in range(ends)])  23.9 us
    ppermute x8, waiting for transfers between devices, with_halo(): lax.ppermute(tail, axis, [(i, (i + 1) % count) for i in range(ends)])  16.6 us
    ppermute x8, starting transfers between devices, with_halo(): lax.ppermute(tail, axis, [(i, (i + 1) % count) for i in range(ends)])  14.3 us
    dot_general x2, matrix products, local(): jnp.einsum('mab,bp->map', matrix_set, flattened, preferred_element_type=j...  7.43 us
    convert_element_type x2, other arithmetic, local(): advected.astype(jnp.bfloat16).reshape(bins_all, block_rows * block_cols)  7.27 us
    unnamed x33, local copies, waits for them, and re-layouts  5.69 us
    slice x4, local copies, waits for them, and re-layouts, with_halo(): lax.slice_in_dim(cells, cells.shape[dim] - width, cells.shape[dim], axis=...  2.12 us
  transfers between devices with their start and end apart: 16, of which 6 were waited for; matrix products, arithmetic and copies ran while one was open for 11% of the time, Pallas kernels for 0%

commit v1 on v0

v1 whole, which is shorter than its diff:
```python
import functools

import jax
import jax.numpy as jnp
from jax import lax
from jax.experimental import pallas as pl
from jax.experimental.pallas import tpu as pltpu
from jax.sharding import PartitionSpec as P

STEPS = 2

current_gain = 0.2
source_gain = 0.5
mixing_side = 0.15
mixing_depth = 0.2
rotation = 0.3
transport = 0.5

LANES = 128
VMEM = pltpu.VMEM
F32 = jnp.float32
BF16 = jnp.bfloat16


def lane_chunks(width):
    return range(0, width, LANES)


def spread(columns, r, cols):
    return jnp.broadcast_to(columns[:, r : r + 1], (cols, LANES))


def pick(flag, yes, no):
    return jnp.where(flag, yes, no)


def pack_borders(dims, e_ref, o_ref, odd_col, odd_row, col_refs, row_refs):
    rows, cols, bins, levels, fields = dims
    points = rows * cols

    def column(c, to_ref):
        start = cols + c
        for k in lane_chunks(bins):
            to_ref[:, k : k + LANES] = e_ref[k // LANES, pl.ds(start, rows, stride=cols), :]
        for q in range(fields):
            to_ref[:, bins + q * levels : bins + (q + 1) * levels] = o_ref[
                q, pl.ds(start, rows, stride=cols), :
            ]

    def row(r, to_ref):
        start = pl.multiple_of(cols + r * cols, cols)
        for k in lane_chunks(bins):
            to_ref[:, k : k + LANES] = e_ref[k // LANES, pl.ds(start, cols), :]
        for q in range(fields):
            to_ref[:, bins + q * levels : bins + (q + 1) * levels] = o_ref[q, pl.ds(start, cols), :]

    for index, to_ref in enumerate(col_refs):
        near = odd_col if index == 0 else 1 - odd_col
        column((cols - 1) * (1 - near), to_ref)
    for index, to_ref in enumerate(row_refs):
        near = odd_row if index == 0 else 1 - odd_row
        row((rows - 1) * (1 - near), to_ref)


def clear_ends(dims, e_ref, o_ref):
    rows, cols, bins, levels, fields = dims
    points = rows * cols
    for start in (0, cols + points):
        for k in range(bins // LANES):
            e_ref[k, start : start + cols, :] = jnp.zeros((cols, LANES), F32)
        for q in range(fields):
            o_ref[q, start : start + cols, :] = jnp.zeros((cols, levels), F32)


def first_kernel(dims, n_col, n_row, parity_ref, e_hbm, o_hbm, *refs):
    rows, cols, bins, levels, fields = dims
    points = rows * cols
    e_ref, o_ref = refs[:2]
    col_refs = refs[2 : 2 + n_col]
    row_refs = refs[2 + n_col : 2 + n_col + n_row]
    sems = refs[-1]
    copies = []
    for k in range(bins // LANES):
        copies.append(
            pltpu.make_async_copy(
                e_hbm.at[:, pl.ds(k * LANES, LANES)],
                e_ref.at[k, pl.ds(cols, points), :],
                sems.at[k],
            )
        )
    for q in range(fields):
        copies.append(
            pltpu.make_async_copy(
                o_hbm.at[q], o_ref.at[q, pl.ds(cols, points), :], sems.at[bins // LANES + q]
            )
        )
    for copy in copies:
        copy.start()
    clear_ends(dims, e_ref, o_ref)
    for copy in copies:
        copy.wait()
    pack_borders(dims, e_ref, o_ref, parity_ref[0], parity_ref[1], col_refs, row_refs)


def advect_rows(dims, e_ref, o_ref, mask_ref, courant_ref, adv_ref):
    rows, cols, bins, levels, fields = dims
    col_id = lax.broadcasted_iota(jnp.int32, (cols, LANES), 0)
    west_end = col_id == 0
    east_end = col_id == cols - 1

    def body(r, _):
        at = pl.multiple_of(r * cols, cols)
        here = pl.multiple_of(cols + r * cols, cols)
        after = pl.multiple_of(2 * cols + r * cols, cols)
        sea = mask_ref[pl.ds(at, cols), :]
        drift_x = jnp.broadcast_to(current_gain * o_ref[0, pl.ds(here, cols), 0:1], (cols, LANES))
        drift_y = jnp.broadcast_to(current_gain * o_ref[1, pl.ds(here, cols), 0:1], (cols, LANES))
        for k in lane_chunks(bins):
            lanes = slice(k, k + LANES)
            mid = e_ref[k // LANES, pl.ds(here, cols), :]
            north = e_ref[k // LANES, pl.ds(at, cols), :]
            south = e_ref[k // LANES, pl.ds(after, cols), :]
            west = jnp.where(west_end, 0.0, pltpu.roll(mid, 1, axis=0))
            east = jnp.where(east_end, 0.0, pltpu.roll(mid, cols - 1, axis=0))
            speed_x = courant_ref[0:1, lanes] + drift_x
            speed_y = courant_ref[1:2, lanes] + drift_y
            flux = speed_x * jnp.where(speed_x > 0, mid - west, east - mid)
            flux = flux + speed_y * jnp.where(speed_y > 0, mid - north, south - mid)
            adv_ref[k // LANES, pl.ds(at, cols), :] = sea * (mid - flux)
        return 0

    lax.fori_loop(0, rows, body, 0)


def advect_first_kernel(
    dims, e_ref, o_ref, mask_t, owner_t, courant_ref, m_hbm, w_hbm,
    adv_ref, mask_ref, owner_ref, m_ref, w_ref, sems,
):
    rows, cols, bins, levels, fields = dims
    copies = [
        pltpu.make_async_copy(m_hbm, m_ref, sems.at[0]),
        pltpu.make_async_copy(w_hbm, w_ref, sems.at[1]),
    ]
    for copy in copies:
        copy.start()
    mask = mask_t[...].astype(F32)
    owner = owner_t[...]
    for r in range(rows):
        mask_ref[r * cols : (r + 1) * cols, :] = spread(mask, r, cols)
        owner_ref[r * cols : (r + 1) * cols, :] = spread(owner, r, cols)
    advect_rows(dims, e_ref, o_ref, mask_ref, courant_ref, adv_ref)
    for copy in copies:
        copy.wait()


def advect_kernel(dims, e_ref, o_ref, mask_ref, courant_ref, adv_ref):
    advect_rows(dims, e_ref, o_ref, mask_ref, courant_ref, adv_ref)


def fix_borders(dims, west, east, north, south, o_ref, mask_ref, courant_ref, adv_ref):
    rows, cols, bins, levels, fields = dims
    points = rows * cols

    def column(c, halo, sign):
        sea = mask_ref[pl.ds(c, rows, stride=cols), :]
        speed = o_ref[0, pl.ds(cols + c, rows, stride=cols), :]
        speed = jnp.broadcast_to(current_gain * speed[:, 0:1], (rows, LANES))
        for k in lane_chunks(bins):
            lanes = slice(k, k + LANES)
            flow = jnp.maximum(sign * (courant_ref[0:1, lanes] + speed), 0.0)
            spots = pl.ds(c, rows, stride=cols)
            adv_ref[k // LANES, spots, :] = (
                adv_ref[k // LANES, spots, :] + sea * flow * halo(lanes)
            )

    def row(r, halo, sign):
        sea = mask_ref[r * cols : (r + 1) * cols, :]
        speed = o_ref[1, cols + r * cols : 2 * cols + r * cols, 0:1]
        speed = jnp.broadcast_to(current_gain * speed, (cols, LANES))
        for k in lane_chunks(bins):
            lanes = slice(k, k + LANES)
            flow = jnp.maximum(sign * (courant_ref[1:2, lanes] + speed), 0.0)
            spots = slice(r * cols, (r + 1) * cols)
            adv_ref[k // LANES, spots, :] = (
                adv_ref[k // LANES, spots, :] + sea * flow * halo(lanes)
            )

    column(0, west, 1.0)
    column(cols - 1, east, -1.0)
    row(0, north, 1.0)
    row(rows - 1, south, -1.0)


def ocean_rows(dims, o_ref, mask_ref, drift_ref, out_ref, out_at):
    rows, cols, bins, levels, fields = dims
    col_id = lax.broadcasted_iota(jnp.int32, (cols, levels), 0)
    west_end = col_id == 0
    east_end = col_id == cols - 1
    level_id = lax.broadcasted_iota(jnp.int32, (cols, levels), 1)
    top = level_id == 0
    bottom = level_id == levels - 1

    def body(r, _):
        at = pl.multiple_of(r * cols, cols)
        here = pl.multiple_of(cols + r * cols, cols)
        after = pl.multiple_of(2 * cols + r * cols, cols)
        sea = mask_ref[pl.ds(at, cols), :]
        drift = [drift_ref[k, pl.ds(at, cols), :] for k in range(2)]
        mid = [o_ref[q, pl.ds(here, cols), :] for q in range(fields)]
        for q in range(fields):
            own = mid[q]
            at_north = o_ref[q, pl.ds(at, cols), :]
            at_south = o_ref[q, pl.ds(after, cols), :]
            at_west = jnp.where(west_end, 0.0, pltpu.roll(own, 1, axis=0))
            at_east = jnp.where(east_end, 0.0, pltpu.roll(own, cols - 1, axis=0))
            above = jnp.where(top, 0.0, pltpu.roll(own, 1, axis=1))
            below = jnp.where(bottom, 0.0, pltpu.roll(own, levels - 1, axis=1))
            lateral = at_north + at_south + at_west + at_east - 4.0 * own
            mixing = mixing_side * lateral + mixing_depth * (below + above - 2.0 * own)
            if q == 0:
                tend = mixing + rotation * (mid[1] + drift[1])
            elif q == 1:
                tend = mixing - rotation * (mid[0] + drift[0])
            else:
                grad = drift[0] * (at_east - at_west) + drift[1] * (at_south - at_north)
                tend = mixing - (0.5 * transport) * grad
            out_ref[q, pl.ds(pl.multiple_of(out_at + r * cols, cols), cols), :] = own + sea * tend
        return 0

    lax.fori_loop(0, rows, body, 0)


def ocean_borders(dims, west, east, north, south, mask_ref, drift_ref, out_ref, out_at):
    rows, cols, bins, levels, fields = dims

    def border(start, count, stride, halo, along, sign):
        def spots(base):
            return pl.ds(base + start, count, stride=stride)

        sea = mask_ref[spots(0), :]
        shear = (sign * 0.5 * transport) * drift_ref[along, spots(0), :]
        for q in range(fields):
            value = halo(slice(bins + q * levels, bins + (q + 1) * levels))
            gain = mixing_side if q < 2 else mixing_side + shear
            out_ref[q, spots(out_at), :] = out_ref[q, spots(out_at), :] + sea * (gain * value)

    border(0, rows, cols, west, 0, 1.0)
    border(cols - 1, rows, cols, east, 0, -1.0)
    border(0, cols, 1, north, 1, 1.0)
    border((rows - 1) * cols, cols, 1, south, 1, -1.0)


def step_kernel(dims, mats, n_col, n_row, last, parity_ref, adv_old, o_in, mask_ref, owner_ref,
                courant_ref, m_ref, w_ref, *refs):
    rows, cols, bins, levels, fields = dims
    points = rows * cols
    got_col = refs[:n_col]
    got_row = refs[n_col : n_col + n_row]
    adv_in, *rest = refs[n_col + n_row :]
    if last:
        e_hbm, o_hbm, low_ref, drift_ref, e_ref, o_ref, sems = rest
    else:
        e_ref, o_ref = rest[:2]
        col_refs = rest[2 : 2 + n_col]
        row_refs = rest[2 + n_col : 2 + n_col + n_row]
        low_ref, drift_ref = rest[2 + n_col + n_row :]
    pad = 0 if last else cols
    odd_col = parity_ref[0] == 1
    odd_row = parity_ref[1] == 1

    def halo(got, odd, before):
        first = got[0]
        second = got[1] if len(got) > 1 else None

        def read(lanes):
            def take(ref):
                return 0.0 if ref is None else ref[:, lanes]

            if before:
                return jnp.where(odd, take(first), take(second))
            return jnp.where(odd, take(second), take(first))

        return read

    west = halo(got_col, odd_col, True)
    east = halo(got_col, odd_col, False)
    north = halo(got_row, odd_row, True)
    south = halo(got_row, odd_row, False)

    fix_borders(dims, west, east, north, south, o_in, mask_ref, courant_ref, adv_in)

    def mask_low(r, _):
        at = pl.multiple_of(r * cols, cols)
        owner = owner_ref[pl.ds(at, cols), :]
        for k in lane_chunks(bins):
            value = adv_in[k // LANES, pl.ds(at, cols), :]
            for m in range(mats):
                low_ref[pl.ds(at, cols), m * bins + k : m * bins + k + LANES] = jnp.where(
                    owner == m, value, 0.0
                ).astype(BF16)
        return 0

    lax.fori_loop(0, rows, mask_low, 0)
    weights = jnp.concatenate([m_ref[m] for m in range(mats)], axis=1)
    source = lax.dot_general(
        low_ref[...], weights, (((1,), (1,)), ((), ())), preferred_element_type=F32
    )
    for k in lane_chunks(bins):
        lanes = slice(k, k + LANES)
        for r in range(rows):
            at = slice(r * cols, (r + 1) * cols)
            energy = mask_ref[at, :] * (adv_in[k // LANES, at, :] + source_gain * source[at, lanes])
            if last:
                e_ref[at, lanes] = energy
            else:
                e_ref[k // LANES, cols + r * cols : 2 * cols + r * cols, :] = energy
            low_ref[at, lanes] = energy.astype(BF16)
    if last:
        e_copy = pltpu.make_async_copy(e_ref, e_hbm, sems.at[0])
        e_copy.start()
    drift = jnp.dot(low_ref[:, 0:bins], w_ref[...], preferred_element_type=F32)
    for k in range(2):
        drift_ref[k] = drift[:, k * levels : (k + 1) * levels]
    ocean_rows(dims, o_in, mask_ref, drift_ref, o_ref, pad)
    ocean_borders(dims, west, east, north, south, mask_ref, drift_ref, o_ref, pad)
    if last:
        o_copy = pltpu.make_async_copy(o_ref, o_hbm, sems.at[1])
        o_copy.start()
        e_copy.wait()
        o_copy.wait()
    else:
        clear_ends(dims, e_ref, o_ref)
        pack_borders(dims, e_ref, o_ref, parity_ref[0], parity_ref[1], col_refs, row_refs)


def swap_pairs(values, axis):
    count = lax.axis_size(axis)
    got = []
    for index, value in enumerate(values):
        pairs = []
        for i in range(index, count - 1, 2):
            pairs += [(i, i + 1), (i + 1, i)]
        got.append(lax.ppermute(value, axis, pairs))
    return got


def local(spectrum, matrices, ownership, land_mask, courant, stokes_weight, ocean):
    bins, rows, cols = spectrum.shape
    fields, _, _, levels = ocean.shape
    mats = matrices.shape[2]
    points = rows * cols
    dims = (rows, cols, bins, levels, fields)
    n_col = 2 if lax.axis_size("grp") > 2 else 1
    n_row = 2 if lax.axis_size("tile") > 2 else 1
    e0 = jnp.transpose(spectrum, (1, 2, 0)).reshape(points, bins)
    o0 = ocean.reshape(fields, points, levels)
    m0 = matrices.reshape(mats, bins, bins)
    mask_t = land_mask.T
    owner_t = ownership.T
    parity = jnp.stack([lax.axis_index("grp") % 2, lax.axis_index("tile") % 2]).astype(jnp.int32)

    vmem = pl.BlockSpec(memory_space=VMEM)
    smem = pl.BlockSpec(memory_space=pltpu.SMEM)
    anys = pl.BlockSpec(memory_space=pl.ANY)
    chunks = bins // LANES
    e_pad = VMEM((chunks, points + 2 * cols, LANES), F32)
    o_pad = VMEM((fields, points + 2 * cols, levels), F32)
    wide = bins + fields * levels
    borders = [VMEM((rows, wide), F32)] * n_col + [VMEM((cols, wide), F32)] * n_row
    n_all = n_col + n_row

    def params(mib):
        return pltpu.CompilerParams(vmem_limit_bytes=mib * 2**20)

    def exchange(sent):
        return swap_pairs(sent[:n_col], "grp") + swap_pairs(sent[n_col:], "tile")

    e, o, *sent = pl.pallas_call(
        functools.partial(first_kernel, dims, n_col, n_row),
        out_shape=[e_pad, o_pad] + borders,
        in_specs=[smem, anys, anys],
        out_specs=[vmem] * (2 + n_all),
        scratch_shapes=[pltpu.SemaphoreType.DMA((chunks + fields,))],
        compiler_params=params(8),
        name="first",
    )(parity, e0, o0)
    got = exchange(sent)
    adv, mask, owner, m, w = pl.pallas_call(
        functools.partial(advect_first_kernel, dims),
        out_shape=[
            VMEM((chunks, points, LANES), F32),
            VMEM((points, LANES), F32),
            VMEM((points, LANES), jnp.int32),
            VMEM((mats, bins, bins), BF16),
            VMEM(stokes_weight.shape, BF16),
        ],
        in_specs=[vmem] * 5 + [anys] * 2,
        out_specs=[vmem] * 5,
        scratch_shapes=[pltpu.SemaphoreType.DMA((2,))],
        compiler_params=params(16),
        name="advect_first",
    )(e, o, mask_t, owner_t, courant, m0, stokes_weight)
    for step in range(STEPS):
        last = step == STEPS - 1
        scratch = [VMEM((points, mats * bins), BF16), VMEM((2, points, levels), F32)]
        if last:
            out_shape = [
                jax.ShapeDtypeStruct((points, bins), F32),
                jax.ShapeDtypeStruct((fields, points, levels), F32),
            ]
            out_specs = [anys, anys]
            scratch += [
                VMEM((points, bins), F32),
                VMEM((fields, points, levels), F32),
                pltpu.SemaphoreType.DMA((2,)),
            ]
        else:
            out_shape = [e_pad, o_pad] + borders
            out_specs = [vmem] * (2 + n_all)
        out = pl.pallas_call(
            functools.partial(step_kernel, dims, mats, n_col, n_row, last),
            out_shape=[VMEM(adv.shape, F32)] + out_shape,
            in_specs=[smem] + [vmem] * (7 + n_all),
            out_specs=[vmem] + out_specs,
            input_output_aliases={1: 0},
            scratch_shapes=scratch,
            compiler_params=params(40),
            name="step_last" if last else "step",
        )(parity, adv, o, mask, owner, courant, m, w, *got)
        if last:
            _, energy, fields_out = out
        else:
            _, e, o, *sent = out
            got = exchange(sent)
            adv = pl.pallas_call(
                functools.partial(advect_kernel, dims),
                out_shape=VMEM((chunks, points, LANES), F32),
                in_specs=[vmem] * 4,
                out_specs=vmem,
                compiler_params=params(16),
                name="advect",
            )(e, o, mask, courant)
    energy = jnp.transpose(energy.reshape(rows, cols, bins), (2, 0, 1))
    return energy, fields_out.reshape(ocean.shape)


def solution(mesh):
    in_specs = (
        P(None, "tile", "grp"),
        P("tile", "grp", None, None, None),
        P("tile", "grp"),
        P("tile", "grp"),
        P(),
        P(),
        P(None, "tile", "grp", None),
    )
    out_specs = (P(None, "tile", "grp"), P(None, "tile", "grp", None))
    return jax.shard_map(local, mesh=mesh, in_specs=in_specs, out_specs=out_specs, check_vma=False)
```

time: 90.9 us -> 44.7 us (0.49)
  the two profiles are of different devices: /device:TPU:20 before, /device:TPU:25 now
where the time goes in v1:
time: 44.7 us; the launch traced here: 44.5 us
  Pallas kernels  26.5 us (59%)
  starting transfers between devices  8.23 us (18%)
  local copies, waits for them, and re-layouts  5.41 us (12%)
  waiting for transfers between devices  3.51 us (8%)
  between operations  0.76 us (2%)
    pallas_call x2, Pallas kernels, local(): pl.pallas_call(functools.partial(step_kernel, dims, mats, n_col, n_row, l...  17.6 us
    ppermute x6, starting transfers between devices, swap_pairs(): got.append(lax.ppermute(value, axis, pairs))  8.23 us
    unnamed x14, local copies, waits for them, and re-layouts  5.41 us
    pallas_call x1, Pallas kernels, local(): pl.pallas_call(functools.partial(advect_first_kernel, dims), out_shape=[V...  4.28 us
    ppermute x6, waiting for transfers between devices, swap_pairs(): got.append(lax.ppermute(value, axis, pairs))  3.51 us
    pallas_call x1, Pallas kernels, local(): pl.pallas_call(functools.partial(advect_kernel, dims), out_shape=VMEM((ch...  3.46 us
    pallas_call x1, Pallas kernels, local(): pl.pallas_call(functools.partial(first_kernel, dims, n_col, n_row), out_s...  1.16 us
  transfers between devices with their start and end apart: 6, of which 2 were waited for; matrix products, arithmetic and copies ran while one was open for 0% of the time, Pallas kernels for 17%

profile of v1, /device:TPU:25, one launch (start us, length us, event | category | flops | bytes accessed | tf_op | source)
XLA Modules:
  0.0 44.5 jit_solution(15754626168601019998)
XLA Ops:
  0.6 0.0 copy-start.4
  0.6 0.0 copy-start.5
  0.7 0.0 copy-start.6
  0.7 0.1 pad_add_fusion.parity_ref
  0.8 0.0 copy-start.1
  0.8 1.7 %copy-done.1 = f32[1152,32,16]{0,2,1:T(8,128)S(1)} copy-done((f32[1152,32,16]{0,2,1:T(8,128)S(1)}, f32[1152,32,16]{0,2,1:T(8,128)}, u32[]{:S(2)}) %copy-start.1) | copy-done | bytes 2359320
  2.4 0.0 copy-start.2
  2.4 1.2 %copy-done.2 = f32[4,32,16,128]{3,2,1,0:T(8,128)S(1)} copy-done((f32[4,32,16,128]{3,2,1,0:T(8,128)S(1)}, f32[4,32,16,128]{3,2,1,0:T(8,128)}, u32[]{:S(2)}) %copy-start.2) | copy-done | bytes 1048600
  3.6 0.0 copy-start.3
  3.6 1.2 %first.1 = (f32[9,544,128]{2,1,0:T(8,128)S(1)}, f32[4,544,128]{2,1,0:T(8,128)S(1)}, f32[32,1664]{1,0:T(8,128)S(1)}, f32[32,1664]{1,0:T(8,128)S(1)}, f32[16,1664]{1,0:T(8,128)S(1)}) custom-call(s32[2]{0:T(128)S(1)} %pad_add_fusion.parity_ref, f32[512,1152]{1,0:T(8,128)S(1)} %bitcast.14, f32[4,512,128]{2,1,0:T(8,128)S(1)} %bitcast.15), custom_call_target="tpu_custom_call" | custom-call | tf_op jit(solution)/shard_map/first/pallas_call | solution.py:378
  4.8 0.7 %collective-permute-start = (f32[32,1664]{1,0:T(8,128)S(1)}, f32[32,1664]{1,0:T(8,128)S(1)}, u32[]{:S(2)}, u32[]{:S(2)}) collective-permute-start(f32[32,1664]{1,0:T(8,128)S(1)} %get-tuple-element.26), channel_id=1, source_target_pairs={{0,2},{2,0},{4,6},{6,4},{8,10},{10,8},{12,14},{14,12},{16,18},{18,... | collective-permute-start | bytes 638984 | tf_op jit(solution)/shard_map/ppermute | solution.py:343
  5.6 3.0 %collective-permute-start.1 = (f32[32,1664]{1,0:T(8,128)S(1)}, f32[32,1664]{1,0:T(8,128)S(1)}, u32[]{:S(2)}, u32[]{:S(2)}) collective-permute-start(f32[32,1664]{1,0:T(8,128)S(1)} %get-tuple-element.27), channel_id=1, source_target_pairs={{2,4},{4,2},{6,8},{8,6},{10,12},{12,10},{14,16},{16,14},{18,20},{2... | collective-permute-start | bytes 638984 | tf_op jit(solution)/shard_map/ppermute | solution.py:343
  8.6 1.3 %collective-permute-start.2 = (f32[16,1664]{1,0:T(8,128)S(1)}, f32[16,1664]{1,0:T(8,128)S(1)}, u32[]{:S(2)}, u32[]{:S(2)}) collective-permute-start(f32[16,1664]{1,0:T(8,128)S(1)} %get-tuple-element.28), channel_id=1, source_target_pairs={{0,1},{1,0},{2,3},{3,2},{4,5},{5,4},{6,7},{7,6},{8,9},{9,8},{10,11... | collective-permute-start | bytes 319496 | tf_op jit(solution)/shard_map/ppermute | solution.py:343
  9.9 0.0 copy-done.4
  9.9 0.0 copy-done.5
  9.9 0.0 copy-done.6
  9.9 0.0 copy-done.3
  9.9 0.0 copy-start
  9.9 2.5 %copy-done = bf16[1,1,2,1152,1152]{4,3,2,1,0:T(8,128)(2,1)S(1)} copy-done((bf16[1,1,2,1152,1152]{4,3,2,1,0:T(8,128)(2,1)S(1)}, bf16[1,1,2,1152,1152]{4,3,2,1,0:T(8,128)(2,1)}, u32[]{:S(2)}) %copy-start) | copy-done | bytes 5308440
  12.4 4.3 %advect_first.1 = (f32[9,512,128]{2,1,0:T(8,128)S(1)}, f32[512,128]{1,0:T(8,128)S(1)}, s32[512,128]{1,0:T(8,128)S(1)}, bf16[2,1152,1152]{2,1,0:T(8,128)(2,1)S(1)}, bf16[1152,256]{1,0:T(8,128)(2,1)S(1)}) custom-call(f32[9,544,128]{2,1,0:T(8,128)S(1)} %get-tuple-element.19.e_ref, f32[4,544,128]{2,1,0:T(8,128)S(1)} %get-tuple-element.20.o_ref.o_in, ...), custom_call_target="tpu_custom_call" | custom-call | tf_op jit(solution)/shard_map/advect_first/pallas_call | solution.py:388
  16.7 0.0 collective-permute-done.2.refs_2_
  16.7 0.0 collective-permute-done.refs_0_
  16.7 0.0 collective-permute-done.1.refs_1_
  16.7 8.4 %step.1 = (f32[9,512,128]{2,1,0:T(8,128)S(1)}, f32[9,544,128]{2,1,0:T(8,128)S(1)}, f32[4,544,128]{2,1,0:T(8,128)S(1)}, f32[32,1664]{1,0:T(8,128)S(1)}, f32[32,1664]{1,0:T(8,128)S(1)}, /*index=5*/f32[16,1664]{1,0:T(8,128)S(1)}) custom-call(s32[2]{0:T(128)S(1)} %pad_add_fusion.parity_ref, ...), custom_call_target="tpu_custom_call", output_to_operand_aliasing={{0}: (1, {})} | custom-call | tf_op jit(solution)/shard_map/step/pallas_call | solution.py:420
  25.2 0.7 %collective-permute-start.3 = (f32[32,1664]{1,0:T(8,128)S(1)}, f32[32,1664]{1,0:T(8,128)S(1)}, u32[]{:S(2)}, u32[]{:S(2)}) collective-permute-start(f32[32,1664]{1,0:T(8,128)S(1)} %get-tuple-element.31), channel_id=1, source_target_pairs={{0,2},{2,0},{4,6},{6,4},{8,10},{10,8},{12,14},{14,12},{16,18},{18,... | collective-permute-start | bytes 638984 | tf_op jit(solution)/shard_map/ppermute | solution.py:343
  25.9 2.2 %collective-permute-start.4 = (f32[32,1664]{1,0:T(8,128)S(1)}, f32[32,1664]{1,0:T(8,128)S(1)}, u32[]{:S(2)}, u32[]{:S(2)}) collective-permute-start(f32[32,1664]{1,0:T(8,128)S(1)} %get-tuple-element.32), channel_id=1, source_target_pairs={{2,4},{4,2},{6,8},{8,6},{10,12},{12,10},{14,16},{16,14},{18,20},{2... | collective-permute-start | bytes 638984 | tf_op jit(solution)/shard_map/ppermute | solution.py:343
  28.1 0.3 collective-permute-start.5
  28.4 3.5 %advect.1.adv_old = f32[9,512,128]{2,1,0:T(8,128)S(1)} custom-call(f32[9,544,128]{2,1,0:T(8,128)S(1)} %get-tuple-element.29.e_ref, f32[4,544,128]{2,1,0:T(8,128)S(1)} %get-tuple-element.30.o_ref.o_in, f32[512,128]{1,0:T(8,128)S(1)} %get-tuple-element.22.mask_ref, f32[2,1152]{1,0:T(2,128)S(1)} %copy-done.4), custom_call_target="tpu_custom_call" | custom-call | tf_op jit(solution)/shard_map/advect/pallas_call | solution.py:435
  31.8 0.2 collective-permute-done.5.refs_2_
  32.0 0.0 collective-permute-done.3.refs_0_
  32.0 3.3 %collective-permute-done.4.refs_1_ = f32[32,1664]{1,0:T(8,128)S(1)} collective-permute-done((f32[32,1664]{1,0:T(8,128)S(1)}, f32[32,1664]{1,0:T(8,128)S(1)}, u32[]{:S(2)}, u32[]{:S(2)}) %collective-permute-start.4) | collective-permute-done | bytes 213024 | tf_op jit(solution)/shard_map/ppermute | solution.py:343
  35.3 9.2 %step_last.1 = (f32[9,512,128]{2,1,0:T(8,128)S(1)}, f32[512,1152]{1,0:T(8,128)}, f32[4,512,128]{2,1,0:T(8,128)}) custom-call(s32[2]{0:T(128)S(1)} %pad_add_fusion.parity_ref, f32[9,512,128]{2,1,0:T(8,128)S(1)} %advect.1.adv_old, f32[4,544,128]{2,1,0:T(8,128)S(1)} %get-tuple-element.30.o_ref.o_in, ...), custom_call_target="tpu_custom_call", output_to_operand_aliasing={{0}: (1, {})} | custom-call | tf_op jit(solution)/shard_map/step_last/pallas_call | solution.py:420
Async XLA Ops:
  0.6 9.3 %copy-start.4 = (f32[2,1152]{1,0:T(2,128)S(1)}, f32[2,1152]{1,0:T(2,128)}, u32[]{:S(2)}) copy-start(f32[2,1152]{1,0:T(2,128)} %courant_ref.7) | copy-start | bytes 27652
  0.6 9.2 %copy-start.5 = (s32[32,16]{0,1:T(8,128)S(1)}, s32[32,16]{0,1:T(8,128)}, u32[]{:S(2)}) copy-start(s32[32,16]{0,1:T(8,128)} %param.10) | copy-start | bytes 6148
  0.7 9.2 %copy-start.6 = (s32[32,16]{0,1:T(8,128)S(1)}, s32[32,16]{0,1:T(8,128)}, u32[]{:S(2)}) copy-start(s32[32,16]{0,1:T(8,128)} %param.9) | copy-start | bytes 6148
  0.8 1.7 %copy-start.1 = (f32[1152,32,16]{0,2,1:T(8,128)S(1)}, f32[1152,32,16]{0,2,1:T(8,128)}, u32[]{:S(2)}) copy-start(f32[1152,32,16]{0,2,1:T(8,128)} %param.7) | copy-start | bytes 7077892
  2.4 1.2 %copy-start.2 = (f32[4,32,16,128]{3,2,1,0:T(8,128)S(1)}, f32[4,32,16,128]{3,2,1,0:T(8,128)}, u32[]{:S(2)}) copy-start(f32[4,32,16,128]{3,2,1,0:T(8,128)} %param.13) | copy-start | bytes 3145732
  3.6 6.2 %copy-start.3 = (bf16[1152,256]{1,0:T(8,128)(2,1)S(1)}, bf16[1152,256]{1,0:T(8,128)(2,1)}, u32[]{:S(2)}) copy-start(bf16[1152,256]{1,0:T(8,128)(2,1)} %w_hbm.1) | copy-start | bytes 1769476
  4.8 11.9 %collective-permute-start = (f32[32,1664]{1,0:T(8,128)S(1)}, f32[32,1664]{1,0:T(8,128)S(1)}, u32[]{:S(2)}, u32[]{:S(2)}) collective-permute-start(f32[32,1664]{1,0:T(8,128)S(1)} %get-tuple-element.26), channel_id=1, source_target_pairs={{0,2},{2,0},{4,6},{6,4},{8,10},{10,8},{12,14},{14,12},{16,18},{18,... | collective-permute-start | bytes 638984 | tf_op jit(solution)/shard_map/ppermute | solution.py:343
  5.6 11.2 %collective-permute-start.1 = (f32[32,1664]{1,0:T(8,128)S(1)}, f32[32,1664]{1,0:T(8,128)S(1)}, u32[]{:S(2)}, u32[]{:S(2)}) collective-permute-start(f32[32,1664]{1,0:T(8,128)S(1)} %get-tuple-element.27), channel_id=1, source_target_pairs={{2,4},{4,2},{6,8},{8,6},{10,12},{12,10},{14,16},{16,14},{18,20},{2... | collective-permute-start | bytes 638984 | tf_op jit(solution)/shard_map/ppermute | solution.py:343
  8.6 8.1 %collective-permute-start.2 = (f32[16,1664]{1,0:T(8,128)S(1)}, f32[16,1664]{1,0:T(8,128)S(1)}, u32[]{:S(2)}, u32[]{:S(2)}) collective-permute-start(f32[16,1664]{1,0:T(8,128)S(1)} %get-tuple-element.28), channel_id=1, source_target_pairs={{0,1},{1,0},{2,3},{3,2},{4,5},{5,4},{6,7},{7,6},{8,9},{9,8},{10,11... | collective-permute-start | bytes 319496 | tf_op jit(solution)/shard_map/ppermute | solution.py:343
  9.9 2.5 %copy-start = (bf16[1,1,2,1152,1152]{4,3,2,1,0:T(8,128)(2,1)S(1)}, bf16[1,1,2,1152,1152]{4,3,2,1,0:T(8,128)(2,1)}, u32[]{:S(2)}) copy-start(bf16[1,1,2,1152,1152]{4,3,2,1,0:T(8,128)(2,1)} %param.8) | copy-start | bytes 15925252
  25.2 6.8 %collective-permute-start.3 = (f32[32,1664]{1,0:T(8,128)S(1)}, f32[32,1664]{1,0:T(8,128)S(1)}, u32[]{:S(2)}, u32[]{:S(2)}) collective-permute-start(f32[32,1664]{1,0:T(8,128)S(1)} %get-tuple-element.31), channel_id=1, source_target_pairs={{0,2},{2,0},{4,6},{6,4},{8,10},{10,8},{12,14},{14,12},{16,18},{18,... | collective-permute-start | bytes 638984 | tf_op jit(solution)/shard_map/ppermute | solution.py:343
  25.9 9.4 %collective-permute-start.4 = (f32[32,1664]{1,0:T(8,128)S(1)}, f32[32,1664]{1,0:T(8,128)S(1)}, u32[]{:S(2)}, u32[]{:S(2)}) collective-permute-start(f32[32,1664]{1,0:T(8,128)S(1)} %get-tuple-element.32), channel_id=1, source_target_pairs={{2,4},{4,2},{6,8},{8,6},{10,12},{12,10},{14,16},{16,14},{18,20},{2... | collective-permute-start | bytes 638984 | tf_op jit(solution)/shard_map/ppermute | solution.py:343
  28.1 3.9 %collective-permute-start.5 = (f32[16,1664]{1,0:T(8,128)S(1)}, f32[16,1664]{1,0:T(8,128)S(1)}, u32[]{:S(2)}, u32[]{:S(2)}) collective-permute-start(f32[16,1664]{1,0:T(8,128)S(1)} %get-tuple-element.33), channel_id=1, source_target_pairs={{0,1},{1,0},{2,3},{3,2},{4,5},{5,4},{6,7},{7,6},{8,9},{9,8},{10,11... | collective-permute-start | bytes 319496 | tf_op jit(solution)/shard_map/ppermute | solution.py:343

commit v2 on v1

v2 whole, which is shorter than its diff:
```python
import functools

import jax
import jax.numpy as jnp
from jax import lax
from jax.experimental import pallas as pl
from jax.experimental.pallas import tpu as pltpu
from jax.sharding import PartitionSpec as P

STEPS = 2

current_gain = 0.2
source_gain = 0.5
mixing_side = 0.15
mixing_depth = 0.2
rotation = 0.3
transport = 0.5

LANES = 128
SUBLANES = 8
VMEM = pltpu.VMEM
F32 = jnp.float32
BF16 = jnp.bfloat16


def in_hbm(x):
    return pltpu.with_memory_space_constraint(x, pltpu.HBM)


def lane_chunks(width):
    return range(0, width, LANES)


def spread(columns, r, cols):
    return jnp.broadcast_to(columns[:, r : r + 1], (cols, LANES))


def pack_borders(dims, e_ref, o_ref, odd_col, odd_row, col_refs, row_refs):
    rows, cols, bins, levels, fields = dims

    def pack(spots, to_ref):
        for k in lane_chunks(bins):
            to_ref[:, k : k + LANES] = e_ref[k // LANES, spots, :]
        for q in range(fields):
            to_ref[:, bins + q * levels : bins + (q + 1) * levels] = o_ref[q, spots, :]

    for index, to_ref in enumerate(col_refs):
        near = odd_col if index == 0 else 1 - odd_col
        pack(pl.ds((cols - 1) * (1 - near), rows, stride=cols), to_ref)
    for index, to_ref in enumerate(row_refs):
        near = odd_row if index == 0 else 1 - odd_row
        pack(pl.ds(pl.multiple_of((rows - 1) * cols * (1 - near), cols), cols), to_ref)


def first_kernel(dims, n_col, n_row, parity_ref, e_hbm, o_hbm, e_ref, o_ref, *refs):
    rows, cols, bins, levels, fields = dims
    col_refs = refs[:n_col]
    row_refs = refs[n_col : n_col + n_row]
    sems = refs[-1]
    copies = []
    for k in range(bins // LANES):
        copies.append(
            pltpu.make_async_copy(
                e_hbm.at[:, pl.ds(k * LANES, LANES)], e_ref.at[k], sems.at[k]
            )
        )
    copies.append(pltpu.make_async_copy(o_hbm, o_ref, sems.at[bins // LANES]))
    for copy in copies:
        copy.start()
    for copy in copies:
        copy.wait()
    pack_borders(dims, e_ref, o_ref, parity_ref[0], parity_ref[1], col_refs, row_refs)


def shifted(parts, axis_ids, ahead):
    first, final = axis_ids
    out = []
    if ahead:
        turned = [pltpu.roll(x, SUBLANES - 1, axis=0) for x in parts]
        for i, x in enumerate(turned):
            out.append(jnp.where(final, turned[i + 1] if i + 1 < len(parts) else 0.0, x))
    else:
        turned = [pltpu.roll(x, 1, axis=0) for x in parts]
        for i, x in enumerate(turned):
            out.append(jnp.where(first, turned[i - 1] if i else 0.0, x))
    return out


def sublane_ends():
    ids = lax.broadcasted_iota(jnp.int32, (SUBLANES, LANES), 0)
    return ids == 0, ids == SUBLANES - 1


def advect_all(dims, e_ref, flow_ref, mask_ref, courant_ref, adv_ref):
    rows, cols, bins, levels, fields = dims
    ends = sublane_ends()
    per_row = cols // SUBLANES

    def body(k, _):
        lanes = pl.ds(pl.multiple_of(k * LANES, LANES), LANES)
        speeds = [
            jnp.broadcast_to(courant_ref[way : way + 1, lanes], (SUBLANES, LANES))
            for way in range(2)
        ]

        def load(r):
            if r >= rows:
                return None
            return [
                e_ref[k, r * cols + i * SUBLANES : r * cols + (i + 1) * SUBLANES, :]
                for i in range(per_row)
            ]

        mid = load(0)
        falls = mid
        for r in range(rows):
            following = load(r + 1)
            if following is None:
                falls_next = [-x for x in mid]
            else:
                falls_next = [b - a for a, b in zip(mid, following)]
            west = shifted(mid, ends, False)
            east = shifted(mid, ends, True)
            for i in range(per_row):
                at = slice(r * cols + i * SUBLANES, r * cols + (i + 1) * SUBLANES)
                speed_x = speeds[0] + flow_ref[0, at, :]
                speed_y = speeds[1] + flow_ref[1, at, :]
                flux = speed_x * jnp.where(speed_x > 0, mid[i] - west[i], east[i] - mid[i])
                flux = flux + speed_y * jnp.where(speed_y > 0, falls[i], falls_next[i])
                adv_ref[k, at, :] = mask_ref[at, :] * (mid[i] - flux)
            mid, falls = following, falls_next
        return 0

    lax.fori_loop(0, bins // LANES, body, 0)


def ocean_all(dims, o_ref, mask_ref, part_ref, grad_ref):
    rows, cols, bins, levels, fields = dims
    ends = sublane_ends()
    level_id = lax.broadcasted_iota(jnp.int32, (SUBLANES, levels), 1)
    top = level_id == 0
    bottom = level_id == levels - 1
    per_row = cols // SUBLANES

    def spots(r, i):
        return slice(r * cols + i * SUBLANES, r * cols + (i + 1) * SUBLANES)

    for q in range(fields):
        north = None
        mid = [o_ref[q, spots(0, i), :] for i in range(per_row)]
        for r in range(rows):
            south = None
            if r + 1 < rows:
                south = [o_ref[q, spots(r + 1, i), :] for i in range(per_row)]
            west = shifted(mid, ends, False)
            east = shifted(mid, ends, True)
            for i in range(per_row):
                at = spots(r, i)
                own = mid[i]
                if north is None:
                    across, slope = south[i], south[i]
                elif south is None:
                    across, slope = north[i], -north[i]
                else:
                    across, slope = north[i] + south[i], south[i] - north[i]
                above = jnp.where(top, 0.0, pltpu.roll(own, 1, axis=1))
                below = jnp.where(bottom, 0.0, pltpu.roll(own, levels - 1, axis=1))
                tend = mixing_side * (across + (west[i] + east[i])) + mixing_depth * (above + below)
                tend = tend - (4 * mixing_side + 2 * mixing_depth) * own
                if q == 0:
                    tend = tend + rotation * o_ref[1, at, :]
                elif q == 1:
                    tend = tend - rotation * o_ref[0, at, :]
                else:
                    grad_ref[2 * (q - 2), at, :] = east[i] - west[i]
                    grad_ref[2 * (q - 2) + 1, at, :] = slope
                part_ref[q, at, :] = own + mask_ref[at, :] * tend
            north, mid = mid, south


def window_kernel(dims, first, e_ref, o_ref, *refs):
    rows, cols, bins, levels, fields = dims
    points = rows * cols
    if first:
        mask_t, owner_t, courant_ref, m_hbm, w_hbm = refs[:5]
        adv_ref, part_ref, grad_ref, mask_ref, owner_ref, m_ref, w_ref, flow_ref, sems = refs[5:]
        copies = [
            pltpu.make_async_copy(m_hbm, m_ref, sems.at[0]),
            pltpu.make_async_copy(w_hbm, w_ref, sems.at[1]),
        ]
        for copy in copies:
            copy.start()
        mask = mask_t[...].astype(F32)
        owner = owner_t[...]
        for r in range(rows):
            mask_ref[r * cols : (r + 1) * cols, :] = spread(mask, r, cols)
            owner_ref[r * cols : (r + 1) * cols, :] = spread(owner, r, cols)
    else:
        mask_ref, courant_ref, adv_ref, part_ref, grad_ref, flow_ref = refs
        copies = []
    for way in range(2):
        flow_ref[way] = jnp.broadcast_to(current_gain * o_ref[way, :, 0:1], (points, LANES))
    advect_all(dims, e_ref, flow_ref, mask_ref, courant_ref, adv_ref)
    ocean_all(dims, o_ref, mask_ref, part_ref, grad_ref)
    for copy in copies:
        copy.wait()


def fix_borders(dims, west, east, north, south, o_ref, mask_ref, courant_ref, adv_ref):
    rows, cols, bins, levels, fields = dims
    points = rows * cols

    def column(c, halo, sign):
        sea = mask_ref[pl.ds(c, rows, stride=cols), :]
        speed = o_ref[0, pl.ds(c, rows, stride=cols), :]
        speed = jnp.broadcast_to(current_gain * speed[:, 0:1], (rows, LANES))
        for k in lane_chunks(bins):
            lanes = slice(k, k + LANES)
            flow = jnp.maximum(sign * (courant_ref[0:1, lanes] + speed), 0.0)
            spots = pl.ds(c, rows, stride=cols)
            adv_ref[k // LANES, spots, :] = (
                adv_ref[k // LANES, spots, :] + sea * flow * halo(lanes)
            )

    def row(r, halo, sign):
        sea = mask_ref[r * cols : (r + 1) * cols, :]
        speed = o_ref[1, r * cols : (r + 1) * cols, 0:1]
        speed = jnp.broadcast_to(current_gain * speed, (cols, LANES))
        for k in lane_chunks(bins):
            lanes = slice(k, k + LANES)
            flow = jnp.maximum(sign * (courant_ref[1:2, lanes] + speed), 0.0)
            spots = slice(r * cols, (r + 1) * cols)
            adv_ref[k // LANES, spots, :] = (
                adv_ref[k // LANES, spots, :] + sea * flow * halo(lanes)
            )

    column(0, west, 1.0)
    column(cols - 1, east, -1.0)
    row(0, north, 1.0)
    row(rows - 1, south, -1.0)


def ocean_combine(dims, part_ref, grad_ref, mask_ref, drift_ref, out_ref):
    rows, cols, bins, levels, fields = dims
    sea = mask_ref[...]
    along = sea * drift_ref[0]
    across = sea * drift_ref[1]
    out_ref[0] = part_ref[0] + rotation * across
    out_ref[1] = part_ref[1] - rotation * along
    for q in range(2, fields):
        grad = along * grad_ref[2 * (q - 2)] + across * grad_ref[2 * (q - 2) + 1]
        out_ref[q] = part_ref[q] - (0.5 * transport) * grad


def ocean_borders(dims, west, east, north, south, mask_ref, drift_ref, out_ref):
    rows, cols, bins, levels, fields = dims

    def border(start, count, stride, halo, along, sign):
        spots = pl.ds(start, count, stride=stride)
        sea = mask_ref[spots, :]
        shear = (sign * 0.5 * transport) * drift_ref[along, spots, :]
        for q in range(fields):
            value = halo(slice(bins + q * levels, bins + (q + 1) * levels))
            gain = mixing_side if q < 2 else mixing_side + shear
            out_ref[q, spots, :] = out_ref[q, spots, :] + sea * (gain * value)

    border(0, rows, cols, west, 0, 1.0)
    border(cols - 1, rows, cols, east, 0, -1.0)
    border(0, cols, 1, north, 1, 1.0)
    border((rows - 1) * cols, cols, 1, south, 1, -1.0)


def step_kernel(dims, mats, n_col, n_row, last, parity_ref, adv_old, o_in, part_ref, grad_ref,
                mask_ref, owner_ref, courant_ref, m_ref, w_ref, *refs):
    rows, cols, bins, levels, fields = dims
    chunks = bins // LANES
    got_col = refs[:n_col]
    got_row = refs[n_col : n_col + n_row]
    adv_ref, *rest = refs[n_col + n_row :]
    if last:
        e_hbm, o_hbm, low_ref, drift_ref, e_ref, o_ref, sems = rest
    else:
        e_ref, o_ref = rest[:2]
        col_refs = rest[2 : 2 + n_col]
        row_refs = rest[2 + n_col : 2 + n_col + n_row]
        low_ref, drift_ref = rest[2 + n_col + n_row :]
    odd_col = parity_ref[0] == 1
    odd_row = parity_ref[1] == 1

    def halo(got, odd, before):
        first = got[0]
        second = got[1] if len(got) > 1 else None

        def read(lanes):
            def take(ref):
                return 0.0 if ref is None else ref[:, lanes]

            if before:
                return jnp.where(odd, take(first), take(second))
            return jnp.where(odd, take(second), take(first))

        return read

    west = halo(got_col, odd_col, True)
    east = halo(got_col, odd_col, False)
    north = halo(got_row, odd_row, True)
    south = halo(got_row, odd_row, False)

    fix_borders(dims, west, east, north, south, o_in, mask_ref, courant_ref, adv_ref)
    owner = owner_ref[...]
    low = jnp.concatenate(
        [
            jnp.where(owner == m, adv_ref[k], 0.0).astype(BF16)
            for m in range(mats)
            for k in range(chunks)
        ],
        axis=1,
    )
    weights = jnp.concatenate([m_ref[m] for m in range(mats)], axis=1)
    source = lax.dot_general(
        low, weights, (((1,), (1,)), ((), ())), preferred_element_type=F32
    )
    sea = mask_ref[...]
    for k in range(chunks):
        lanes = slice(k * LANES, (k + 1) * LANES)
        energy = sea * (adv_ref[k] + source_gain * source[:, lanes])
        if last:
            e_ref[:, lanes] = energy
        else:
            e_ref[k] = energy
        low_ref[:, lanes] = energy.astype(BF16)
    if last:
        e_copy = pltpu.make_async_copy(e_ref, e_hbm, sems.at[0])
        e_copy.start()
    drift = jnp.dot(low_ref[...], w_ref[...], preferred_element_type=F32)
    for k in range(2):
        drift_ref[k] = drift[:, k * levels : (k + 1) * levels]
    ocean_combine(dims, part_ref, grad_ref, mask_ref, drift_ref, o_ref)
    ocean_borders(dims, west, east, north, south, mask_ref, drift_ref, o_ref)
    if last:
        o_copy = pltpu.make_async_copy(o_ref, o_hbm, sems.at[1])
        o_copy.start()
        e_copy.wait()
        o_copy.wait()
    else:
        pack_borders(dims, e_ref, o_ref, parity_ref[0], parity_ref[1], col_refs, row_refs)


def swap_pairs(values, axis):
    count = lax.axis_size(axis)
    got = []
    for index, value in enumerate(values):
        pairs = []
        for i in range(index, count - 1, 2):
            pairs += [(i, i + 1), (i + 1, i)]
        got.append(lax.ppermute(value, axis, pairs))
    return got


def local(spectrum, matrices, ownership, land_mask, courant, stokes_weight, ocean):
    bins, rows, cols = spectrum.shape
    fields, _, _, levels = ocean.shape
    mats = matrices.shape[2]
    points = rows * cols
    dims = (rows, cols, bins, levels, fields)
    n_col = 2 if lax.axis_size("grp") > 2 else 1
    n_row = 2 if lax.axis_size("tile") > 2 else 1
    e0 = jnp.transpose(spectrum, (1, 2, 0)).reshape(points, bins)
    o0 = ocean.reshape(fields, points, levels)
    m0 = matrices.reshape(mats, bins, bins)
    mask_t = land_mask.T
    owner_t = ownership.T
    parity = jnp.stack([lax.axis_index("grp") % 2, lax.axis_index("tile") % 2]).astype(jnp.int32)

    vmem = pl.BlockSpec(memory_space=VMEM)
    smem = pl.BlockSpec(memory_space=pltpu.SMEM)
    hbm = pl.BlockSpec(memory_space=pltpu.HBM)
    chunks = bins // LANES
    e_shape = VMEM((chunks, points, LANES), F32)
    o_shape = VMEM((fields, points, levels), F32)
    part_shapes = [e_shape, o_shape, VMEM((2 * (fields - 2), points, levels), F32)]
    wide = bins + fields * levels
    borders = [VMEM((rows, wide), F32)] * n_col + [VMEM((cols, wide), F32)] * n_row
    flow = VMEM((2, points, LANES), F32)
    n_all = n_col + n_row

    def params(mib):
        return pltpu.CompilerParams(vmem_limit_bytes=mib * 2**20)

    def exchange(sent):
        return swap_pairs(sent[:n_col], "grp") + swap_pairs(sent[n_col:], "tile")

    e, o, *sent = pl.pallas_call(
        functools.partial(first_kernel, dims, n_col, n_row),
        out_shape=[e_shape, o_shape] + borders,
        in_specs=[smem, hbm, hbm],
        out_specs=[vmem] * (2 + n_all),
        scratch_shapes=[pltpu.SemaphoreType.DMA((chunks + 1,))],
        compiler_params=params(8),
        name="first",
    )(parity, in_hbm(e0), in_hbm(o0))
    for step in range(STEPS):
        got = exchange(sent)
        if step == 0:
            adv, part, grad, mask, owner, m, w = pl.pallas_call(
                functools.partial(window_kernel, dims, True),
                out_shape=part_shapes
                + [
                    VMEM((points, LANES), F32),
                    VMEM((points, LANES), jnp.int32),
                    VMEM((mats, bins, bins), BF16),
                    VMEM(stokes_weight.shape, BF16),
                ],
                in_specs=[vmem] * 5 + [hbm] * 2,
                out_specs=[vmem] * 7,
                scratch_shapes=[flow, pltpu.SemaphoreType.DMA((2,))],
                compiler_params=params(16),
                name="window_first",
            )(e, o, mask_t, owner_t, courant, in_hbm(m0), in_hbm(stokes_weight))
        else:
            adv, part, grad = pl.pallas_call(
                functools.partial(window_kernel, dims, False),
                out_shape=part_shapes,
                in_specs=[vmem] * 4,
                out_specs=[vmem] * 3,
                scratch_shapes=[flow],
                compiler_params=params(16),
                name="window",
            )(e, o, mask, courant)
        last = step == STEPS - 1
        scratch = [VMEM((points, bins), BF16), VMEM((2, points, levels), F32)]
        if last:
            out_shape = [
                jax.ShapeDtypeStruct((points, bins), F32),
                jax.ShapeDtypeStruct((fields, points, levels), F32),
            ]
            out_specs = [hbm, hbm]
            scratch += [
                VMEM((points, bins), F32),
                VMEM((fields, points, levels), F32),
                pltpu.SemaphoreType.DMA((2,)),
            ]
        else:
            out_shape = [e_shape, o_shape] + borders
            out_specs = [vmem] * (2 + n_all)
        out = pl.pallas_call(
            functools.partial(step_kernel, dims, mats, n_col, n_row, last),
            out_shape=[e_shape] + out_shape,
            in_specs=[smem] + [vmem] * (9 + n_all),
            out_specs=[vmem] + out_specs,
            scratch_shapes=scratch,
            input_output_aliases={1: 0},
            compiler_params=params(32),
            name="step_last" if last else "step",
        )(parity, adv, o, part, grad, mask, owner, courant, m, w, *got)
        if last:
            _, energy, fields_out = out
        else:
            _, e, o, *sent = out
    energy = jnp.transpose(energy.reshape(rows, cols, bins), (2, 0, 1))
    return energy, fields_out.reshape(ocean.shape)


def solution(mesh):
    in_specs = (
        P(None, "tile", "grp"),
        P("tile", "grp", None, None, None),
        P("tile", "grp"),
        P("tile", "grp"),
        P(),
        P(),
        P(None, "tile", "grp", None),
    )
    out_specs = (P(None, "tile", "grp"), P(None, "tile", "grp", None))
    return jax.shard_map(local, mesh=mesh, in_specs=in_specs, out_specs=out_specs, check_vma=False)
```

time: 44.7 us -> 34.8 us (0.78)
  Pallas kernels: 26.5 us -> 19.1 us
  local copies, waits for them, and re-layouts: 5.41 us -> 0.01 us
  waiting for transfers between devices: 3.51 us -> 6.34 us
    pallas_call x2, Pallas kernels: 17.6 us -> 11.3 us  [local(): pl.pallas_call(functools.partial(step_kernel, dims, mats, n_col, n_row, l...]
    unnamed x14 -> x6, local copies, waits for them, and re-layouts: 5.41 us -> 0.01 us
    ppermute x6, waiting for transfers between devices: 3.51 us -> 6.34 us  [swap_pairs(): got.append(lax.ppermute(value, axis, pairs))]
    pallas_call x2, Pallas kernels: 7.74 us -> 4.95 us  [the longest x1 2.66 us: local(): pl.pallas_call(functools.partial(window_kernel, dims, True), out_shape=pa...]
    pallas_call x1, Pallas kernels: 1.16 us -> 2.84 us  [local(): pl.pallas_call(functools.partial(first_kernel, dims, n_col, n_row), out_s...]
  transfers between devices with their start and end apart: 6 -> 6, of which waited for: 2 -> 3; matrix products, arithmetic and copies ran while one was open for 0% -> 0% of each run, Pallas kernels for 17% -> 14%
where the time goes in v2:
time: 34.8 us; the launch traced here: 34.6 us
  Pallas kernels  19.1 us (55%)
  starting transfers between devices  8.36 us (24%)
  waiting for transfers between devices  6.34 us (18%)
  between operations  0.73 us (2%)
    pallas_call x2, Pallas kernels, local(): pl.pallas_call(functools.partial(step_kernel, dims, mats, n_col, n_row, l...  11.3 us
    ppermute x6, starting transfers between devices, swap_pairs(): got.append(lax.ppermute(value, axis, pairs))  8.36 us
    ppermute x6, waiting for transfers between devices, swap_pairs(): got.append(lax.ppermute(value, axis, pairs))  6.34 us
    pallas_call x1, Pallas kernels, local(): pl.pallas_call(functools.partial(first_kernel, dims, n_col, n_row), out_s...  2.84 us
    pallas_call x1, Pallas kernels, local(): pl.pallas_call(functools.partial(window_kernel, dims, True), out_shape=pa...  2.66 us
    pallas_call x1, Pallas kernels, local(): pl.pallas_call(functools.partial(window_kernel, dims, False), out_shape=p...  2.3 us
  transfers between devices with their start and end apart: 6, of which 3 were waited for; matrix products, arithmetic and copies ran while one was open for 0% of the time, Pallas kernels for 14%

profile of v2, /device:TPU:25, one launch (start us, length us, event | category | flops | bytes accessed | tf_op | source)
XLA Modules:
  0.0 34.6 jit_solution(18107231010555507288)
XLA Ops:
  0.6 0.0 copy-start
  0.6 0.0 copy-start.1
  0.7 0.0 copy-start.2
  0.7 0.1 pad_add_fusion.parity_ref
  0.8 2.8 %first.1 = (f32[9,512,128]{2,1,0:T(8,128)S(1)}, f32[4,512,128]{2,1,0:T(8,128)S(1)}, f32[32,1664]{1,0:T(8,128)S(1)}, f32[32,1664]{1,0:T(8,128)S(1)}, f32[16,1664]{1,0:T(8,128)S(1)}) custom-call(s32[2]{0:T(128)S(1)} %pad_add_fusion.parity_ref, f32[512,1152]{1,0:T(8,128)} %bitcast.16, f32[4,512,128]{2,1,0:T(8,128)} %bitcast.17), custom_call_target="tpu_custom_call" | custom-call | tf_op jit(solution)/shard_map/first/pallas_call | solution.py:393
  3.6 0.7 %collective-permute-start = (f32[32,1664]{1,0:T(8,128)S(1)}, f32[32,1664]{1,0:T(8,128)S(1)}, u32[]{:S(2)}, u32[]{:S(2)}) collective-permute-start(f32[32,1664]{1,0:T(8,128)S(1)} %get-tuple-element.33), channel_id=1, source_target_pairs={{0,2},{2,0},{4,6},{6,4},{8,10},{10,8},{12,14},{14,12},{16,18},{18,... | collective-permute-start | bytes 638984 | tf_op jit(solution)/shard_map/ppermute | solution.py:356
  4.3 3.0 %collective-permute-start.1 = (f32[32,1664]{1,0:T(8,128)S(1)}, f32[32,1664]{1,0:T(8,128)S(1)}, u32[]{:S(2)}, u32[]{:S(2)}) collective-permute-start(f32[32,1664]{1,0:T(8,128)S(1)} %get-tuple-element.34), channel_id=1, source_target_pairs={{2,4},{4,2},{6,8},{8,6},{10,12},{12,10},{14,16},{16,14},{18,20},{2... | collective-permute-start | bytes 638984 | tf_op jit(solution)/shard_map/ppermute | solution.py:356
  7.4 1.3 %collective-permute-start.2 = (f32[16,1664]{1,0:T(8,128)S(1)}, f32[16,1664]{1,0:T(8,128)S(1)}, u32[]{:S(2)}, u32[]{:S(2)}) collective-permute-start(f32[16,1664]{1,0:T(8,128)S(1)} %get-tuple-element.35), channel_id=1, source_target_pairs={{0,1},{1,0},{2,3},{3,2},{4,5},{5,4},{6,7},{7,6},{8,9},{9,8},{10,11... | collective-permute-start | bytes 319496 | tf_op jit(solution)/shard_map/ppermute | solution.py:356
  8.7 0.0 copy-done
  8.7 0.0 copy-done.1
  8.7 0.0 copy-done.2
  8.7 2.7 %window_first.1 = (f32[9,512,128]{2,1,0:T(8,128)S(1)}, f32[4,512,128]{2,1,0:T(8,128)S(1)}, f32[4,512,128]{2,1,0:T(8,128)S(1)}, f32[512,128]{1,0:T(8,128)S(1)}, s...) custom-call(f32[9,512,128]{2,1,0:T(8,128)S(1)} %get-tuple-element.24.e_ref, ...), custom_call_target="tpu_custom_call" | custom-call | tf_op jit(solution)/shard_map/window_first/pallas_call | solution.py:405
  11.3 0.2 collective-permute-done.2.refs_2_
  11.6 0.0 collective-permute-done.refs_0_
  11.6 2.2 %collective-permute-done.1.refs_1_ = f32[32,1664]{1,0:T(8,128)S(1)} collective-permute-done((f32[32,1664]{1,0:T(8,128)S(1)}, f32[32,1664]{1,0:T(8,128)S(1)}, u32[]{:S(2)}, u32[]{:S(2)}) %collective-permute-start.1) | collective-permute-done | bytes 213024 | tf_op jit(solution)/shard_map/ppermute | solution.py:356
  13.8 5.0 %step.1 = (f32[9,512,128]{2,1,0:T(8,128)S(1)}, f32[9,512,128]{2,1,0:T(8,128)S(1)}, f32[4,512,128]{2,1,0:T(8,128)S(1)}, f32[32,1664]{1,0:T(8,128)S(1)}, f32[32,1664]{1,0:T(8,128)S(1)}, /*index=5*/f32[16,1664]{1,0:T(8,128)S(1)}) custom-call(s32[2]{0:T(128)S(1)} %pad_add_fusion.parity_ref, ...), custom_call_target="tpu_custom_call", output_to_operand_aliasing={{0}: (1, {})} | custom-call | tf_op jit(solution)/shard_map/step/pallas_call | solution.py:446
  18.8 0.1 collective-permute-start.3
  18.9 1.9 %collective-permute-start.4 = (f32[32,1664]{1,0:T(8,128)S(1)}, f32[32,1664]{1,0:T(8,128)S(1)}, u32[]{:S(2)}, u32[]{:S(2)}) collective-permute-start(f32[32,1664]{1,0:T(8,128)S(1)} %get-tuple-element.42), channel_id=1, source_target_pairs={{2,4},{4,2},{6,8},{8,6},{10,12},{12,10},{14,16},{16,14},{18,20},{2... | collective-permute-start | bytes 638984 | tf_op jit(solution)/shard_map/ppermute | solution.py:356
  20.8 1.3 %collective-permute-start.5 = (f32[16,1664]{1,0:T(8,128)S(1)}, f32[16,1664]{1,0:T(8,128)S(1)}, u32[]{:S(2)}, u32[]{:S(2)}) collective-permute-start(f32[16,1664]{1,0:T(8,128)S(1)} %get-tuple-element.43), channel_id=1, source_target_pairs={{0,1},{1,0},{2,3},{3,2},{4,5},{5,4},{6,7},{7,6},{8,9},{9,8},{10,11... | collective-permute-start | bytes 319496 | tf_op jit(solution)/shard_map/ppermute | solution.py:356
  22.1 2.3 %window.1 = (f32[9,512,128]{2,1,0:T(8,128)S(1)}, f32[4,512,128]{2,1,0:T(8,128)S(1)}, f32[4,512,128]{2,1,0:T(8,128)S(1)}) custom-call(f32[9,512,128]{2,1,0:T(8,128)S(1)} %get-tuple-element.36.e_ref, f32[4,512,128]{2,1,0:T(8,128)S(1)} %get-tuple-element.37.o_ref.o_in, f32[512,128]{1,0:T(8,128)S(1)} %get-tuple-element.29.mask_ref.refs_0_, f32[2,1152]{1,0:T(2,128)S(1)} %copy-done), custom_call_target="tpu_custom_call" | custom-call | tf_op jit(solution)/shard_map/window/pallas_call | solution.py:421
  24.4 0.0 collective-permute-done.5.refs_2_
  24.4 0.0 collective-permute-done.3.refs_0_
  24.4 3.9 %collective-permute-done.4.refs_1_ = f32[32,1664]{1,0:T(8,128)S(1)} collective-permute-done((f32[32,1664]{1,0:T(8,128)S(1)}, f32[32,1664]{1,0:T(8,128)S(1)}, u32[]{:S(2)}, u32[]{:S(2)}) %collective-permute-start.4) | collective-permute-done | bytes 213024 | tf_op jit(solution)/shard_map/ppermute | solution.py:356
  28.3 6.3 %step_last.1 = (f32[9,512,128]{2,1,0:T(8,128)S(1)}, f32[512,1152]{1,0:T(8,128)}, f32[4,512,128]{2,1,0:T(8,128)}) custom-call(s32[2]{0:T(128)S(1)} %pad_add_fusion.parity_ref, f32[9,512,128]{2,1,0:T(8,128)S(1)} %get-tuple-element.38.adv_old, f32[4,512,128]{2,1,0:T(8,128)S(1)} %get-tuple-element.37.o_ref.o_in, ...), custom_call_target="tpu_custom_call", output_to_operand_aliasing={{0}: (1, {})} | custom-call | tf_op jit(solution)/shard_map/step_last/pallas_call | solution.py:446
Async XLA Ops:
  0.6 8.0 %copy-start = (f32[2,1152]{1,0:T(2,128)S(1)}, f32[2,1152]{1,0:T(2,128)}, u32[]{:S(2)}) copy-start(f32[2,1152]{1,0:T(2,128)} %courant_ref.3) | copy-start | bytes 27652
  0.6 8.0 %copy-start.1 = (s32[32,16]{0,1:T(8,128)S(1)}, s32[32,16]{0,1:T(8,128)}, u32[]{:S(2)}) copy-start(s32[32,16]{0,1:T(8,128)} %param.10) | copy-start | bytes 6148
  0.7 8.0 %copy-start.2 = (s32[32,16]{0,1:T(8,128)S(1)}, s32[32,16]{0,1:T(8,128)}, u32[]{:S(2)}) copy-start(s32[32,16]{0,1:T(8,128)} %param.9) | copy-start | bytes 6148
  3.6 8.0 %collective-permute-start = (f32[32,1664]{1,0:T(8,128)S(1)}, f32[32,1664]{1,0:T(8,128)S(1)}, u32[]{:S(2)}, u32[]{:S(2)}) collective-permute-start(f32[32,1664]{1,0:T(8,128)S(1)} %get-tuple-element.33), channel_id=1, source_target_pairs={{0,2},{2,0},{4,6},{6,4},{8,10},{10,8},{12,14},{14,12},{16,18},{18,... | collective-permute-start | bytes 638984 | tf_op jit(solution)/shard_map/ppermute | solution.py:356
  4.3 9.4 %collective-permute-start.1 = (f32[32,1664]{1,0:T(8,128)S(1)}, f32[32,1664]{1,0:T(8,128)S(1)}, u32[]{:S(2)}, u32[]{:S(2)}) collective-permute-start(f32[32,1664]{1,0:T(8,128)S(1)} %get-tuple-element.34), channel_id=1, source_target_pairs={{2,4},{4,2},{6,8},{8,6},{10,12},{12,10},{14,16},{16,14},{18,20},{2... | collective-permute-start | bytes 638984 | tf_op jit(solution)/shard_map/ppermute | solution.py:356
  7.4 4.2 %collective-permute-start.2 = (f32[16,1664]{1,0:T(8,128)S(1)}, f32[16,1664]{1,0:T(8,128)S(1)}, u32[]{:S(2)}, u32[]{:S(2)}) collective-permute-start(f32[16,1664]{1,0:T(8,128)S(1)} %get-tuple-element.35), channel_id=1, source_target_pairs={{0,1},{1,0},{2,3},{3,2},{4,5},{5,4},{6,7},{7,6},{8,9},{9,8},{10,11... | collective-permute-start | bytes 319496 | tf_op jit(solution)/shard_map/ppermute | solution.py:356
  18.8 5.6 %collective-permute-start.3 = (f32[32,1664]{1,0:T(8,128)S(1)}, f32[32,1664]{1,0:T(8,128)S(1)}, u32[]{:S(2)}, u32[]{:S(2)}) collective-permute-start(f32[32,1664]{1,0:T(8,128)S(1)} %get-tuple-element.41), channel_id=1, source_target_pairs={{0,2},{2,0},{4,6},{6,4},{8,10},{10,8},{12,14},{14,12},{16,18},{18,... | collective-permute-start | bytes 638984 | tf_op jit(solution)/shard_map/ppermute | solution.py:356
  18.9 9.4 %collective-permute-start.4 = (f32[32,1664]{1,0:T(8,128)S(1)}, f32[32,1664]{1,0:T(8,128)S(1)}, u32[]{:S(2)}, u32[]{:S(2)}) collective-permute-start(f32[32,1664]{1,0:T(8,128)S(1)} %get-tuple-element.42), channel_id=1, source_target_pairs={{2,4},{4,2},{6,8},{8,6},{10,12},{12,10},{14,16},{16,14},{18,20},{2... | collective-permute-start | bytes 638984 | tf_op jit(solution)/shard_map/ppermute | solution.py:356
  20.8 3.6 %collective-permute-start.5 = (f32[16,1664]{1,0:T(8,128)S(1)}, f32[16,1664]{1,0:T(8,128)S(1)}, u32[]{:S(2)}, u32[]{:S(2)}) collective-permute-start(f32[16,1664]{1,0:T(8,128)S(1)} %get-tuple-element.43), channel_id=1, source_target_pairs={{0,1},{1,0},{2,3},{3,2},{4,5},{5,4},{6,7},{7,6},{8,9},{9,8},{10,11... | collective-permute-start | bytes 319496 | tf_op jit(solution)/shard_map/ppermute | solution.py:356

commit v3 on v2

v3 whole, which is shorter than its diff:
```python
import functools

import jax
import jax.numpy as jnp
from jax import lax
from jax.experimental import pallas as pl
from jax.experimental.pallas import tpu as pltpu
from jax.sharding import PartitionSpec as P

STEPS = 2

current_gain = 0.2
source_gain = 0.5
mixing_side = 0.15
mixing_depth = 0.2
rotation = 0.3
transport = 0.5

LANES = 128
SUBLANES = 8
VMEM = pltpu.VMEM
F32 = jnp.float32
BF16 = jnp.bfloat16


def in_hbm(x):
    return pltpu.with_memory_space_constraint(x, pltpu.HBM)


def lane_chunks(width):
    return range(0, width, LANES)


def spread(columns, r, cols):
    return jnp.broadcast_to(columns[:, r : r + 1], (cols, LANES))


def low_side(parity, index):
    return parity if index == 0 else 1 - parity


def column_place(dims, parity, index):
    rows, cols, bins, levels, fields = dims
    high = 1 - low_side(parity, index)
    tile = high * (cols // SUBLANES - 1)
    return tile, pl.ds(high * (SUBLANES - 1), rows, stride=SUBLANES)


def row_place(dims, parity, index):
    high = 1 - low_side(parity, index)
    return pl.ds(pl.multiple_of(high * (dims[0] - 1) * SUBLANES, SUBLANES), SUBLANES)


def side_sign(parity, index):
    return jnp.where(low_side(parity, index) == 1, 1.0, -1.0).astype(F32)


def first_kernel(dims, n_col, n_row, parity_ref, e_hbm, o_hbm, *refs):
    rows, cols, bins, levels, fields = dims
    col_refs = refs[:n_col]
    row_refs = refs[n_col : n_col + n_row]
    sems = refs[-1]

    def pieces(to_ref, e_from, o_from, slot):
        copies = [pltpu.make_async_copy(e_from, to_ref.at[..., 0:bins], sems.at[slot, 0])]
        for q in range(fields):
            lanes = pl.ds(bins + q * levels, levels)
            copies.append(
                pltpu.make_async_copy(o_from(q), to_ref.at[..., lanes], sems.at[slot, 1 + q])
            )
        return copies

    def column(index, high):
        tile = high * (cols // SUBLANES - 1)
        place = high * (SUBLANES - 1)
        return pieces(
            col_refs[index],
            e_hbm.at[:, tile, place, :],
            lambda q: o_hbm.at[q, :, tile, place, :],
            index,
        )

    def row(index):
        r = (1 - low_side(parity_ref[1], index)) * (rows - 1)
        return pieces(row_refs[index], e_hbm.at[r], lambda q: o_hbm.at[q, r], n_col + index)

    for odd in range(2):

        @pl.when(parity_ref[0] == odd)
        def _(odd=odd):
            for index in reversed(range(n_col)):
                for copy in column(index, 1 - low_side(odd, index)):
                    copy.start()

    for index in range(n_row):
        for copy in row(index):
            copy.start()
    for index in range(n_col):
        for copy in column(index, 0):
            copy.wait()
    for index in range(n_row):
        for copy in row(index):
            copy.wait()


def shifted(parts, axis_ids, ahead):
    first, final = axis_ids
    out = []
    if ahead:
        turned = [pltpu.roll(x, SUBLANES - 1, axis=0) for x in parts]
        for i, x in enumerate(turned):
            out.append(jnp.where(final, turned[i + 1] if i + 1 < len(parts) else 0.0, x))
    else:
        turned = [pltpu.roll(x, 1, axis=0) for x in parts]
        for i, x in enumerate(turned):
            out.append(jnp.where(first, turned[i - 1] if i else 0.0, x))
    return out


def sublane_ends():
    ids = lax.broadcasted_iota(jnp.int32, (SUBLANES, LANES), 0)
    return ids == 0, ids == SUBLANES - 1


def span(r):
    return slice(r * SUBLANES, (r + 1) * SUBLANES)


def tile_at(ref, lead, i, r):
    if ref.ndim == 5:
        return ref[lead, i, r]
    return ref[lead, i, span(r), :]


def advect_all(dims, e_ref, arrived, flow_ref, mask_ref, courant_ref, adv_ref):
    rows, cols, bins, levels, fields = dims
    ends = sublane_ends()
    tiles = cols // SUBLANES

    def body(k, _):
        arrived(k)
        lanes = pl.ds(pl.multiple_of(k * LANES, LANES), LANES)
        speeds = [
            jnp.broadcast_to(courant_ref[way : way + 1, lanes], (SUBLANES, LANES))
            for way in range(2)
        ]

        def load(r):
            if r >= rows:
                return None
            return [tile_at(e_ref, k, i, r) for i in range(tiles)]

        mid = load(0)
        falls = mid
        for r in range(rows):
            following = load(r + 1)
            if following is None:
                falls_next = [-x for x in mid]
            else:
                falls_next = [b - a for a, b in zip(mid, following)]
            west = shifted(mid, ends, False)
            east = shifted(mid, ends, True)
            for i in range(tiles):
                speed_x = speeds[0] + flow_ref[0, i, span(r), :]
                speed_y = speeds[1] + flow_ref[1, i, span(r), :]
                flux = speed_x * jnp.where(speed_x > 0, mid[i] - west[i], east[i] - mid[i])
                flux = flux + speed_y * jnp.where(speed_y > 0, falls[i], falls_next[i])
                adv_ref[k, i, span(r), :] = mask_ref[i, span(r), :] * (mid[i] - flux)
            mid, falls = following, falls_next
        return 0

    lax.fori_loop(0, bins // LANES, body, 0)


def ocean_all(dims, o_ref, mask_ref, part_ref, grad_ref):
    rows, cols, bins, levels, fields = dims
    ends = sublane_ends()
    level_id = lax.broadcasted_iota(jnp.int32, (SUBLANES, levels), 1)
    top = level_id == 0
    bottom = level_id == levels - 1
    tiles = cols // SUBLANES

    for q in range(fields):
        north = None
        mid = [tile_at(o_ref, q, i, 0) for i in range(tiles)]
        for r in range(rows):
            south = None
            if r + 1 < rows:
                south = [tile_at(o_ref, q, i, r + 1) for i in range(tiles)]
            west = shifted(mid, ends, False)
            east = shifted(mid, ends, True)
            for i in range(tiles):
                own = mid[i]
                if north is None:
                    across, slope = south[i], south[i]
                elif south is None:
                    across, slope = north[i], -north[i]
                else:
                    across, slope = north[i] + south[i], south[i] - north[i]
                above = jnp.where(top, 0.0, pltpu.roll(own, 1, axis=1))
                below = jnp.where(bottom, 0.0, pltpu.roll(own, levels - 1, axis=1))
                tend = mixing_side * (across + (west[i] + east[i])) + mixing_depth * (above + below)
                tend = tend - (4 * mixing_side + 2 * mixing_depth) * own
                if q == 0:
                    tend = tend + rotation * tile_at(o_ref, 1, i, r)
                elif q == 1:
                    tend = tend - rotation * tile_at(o_ref, 0, i, r)
                else:
                    grad_ref[2 * (q - 2), i, span(r), :] = east[i] - west[i]
                    grad_ref[2 * (q - 2) + 1, i, span(r), :] = slope
                part_ref[q, i, span(r), :] = own + mask_ref[i, span(r), :] * tend
            north, mid = mid, south


def window_kernel(dims, first, e_in, o_in, *refs):
    rows, cols, bins, levels, fields = dims
    tiles = cols // SUBLANES
    if first:
        mask_t, owner_t, courant_ref, m_hbm, w_hbm = refs[:5]
        adv_ref, part_ref, grad_ref, flow_ref, mask_ref, owner_ref, m_ref, w_ref = refs[5:13]
        e_ref, o_ref, e_sems, o_sems, m_sems = refs[13:]

        def e_copies(k):
            lanes = pl.ds(pl.multiple_of(k * LANES, LANES), LANES)
            return [
                pltpu.make_async_copy(
                    e_in.at[:, i, :, lanes], e_ref.at[k, i], e_sems.at[k, i]
                )
                for i in range(tiles)
            ]

        o_copies = [
            pltpu.make_async_copy(o_in.at[q, :, i], o_ref.at[q, i], o_sems.at[q, i])
            for q in range(fields)
            for i in range(tiles)
        ]
        m_copies = [
            pltpu.make_async_copy(m_hbm, m_ref, m_sems.at[0]),
            pltpu.make_async_copy(w_hbm, w_ref, m_sems.at[1]),
        ]
        for copy in o_copies:
            copy.start()
        for k in range(bins // LANES):
            for copy in e_copies(k):
                copy.start()
        for copy in m_copies:
            copy.start()
        mask = mask_t[...].astype(F32)
        owner = owner_t[...]
        for i in range(tiles):
            for r in range(rows):
                for to_ref, values in ((mask_ref, mask), (owner_ref, owner)):
                    to_ref[i, span(r), :] = jnp.broadcast_to(
                        values[span(i), r : r + 1], (SUBLANES, LANES)
                    )
        for copy in o_copies:
            copy.wait()
    else:
        mask_ref, courant_ref, adv_ref, part_ref, grad_ref, flow_ref = refs
        e_ref, o_ref = e_in, o_in
        m_copies = []

    def arrived(k):
        if first:
            for copy in e_copies(k):
                copy.wait()

    for way in range(2):
        for i in range(tiles):
            for r in range(rows):
                current = tile_at(o_ref, way, i, r)
                flow_ref[way, i, span(r), :] = jnp.broadcast_to(
                    current_gain * current[:, 0:1], (SUBLANES, LANES)
                )
    ocean_all(dims, o_ref, mask_ref, part_ref, grad_ref)
    advect_all(dims, e_ref, arrived, flow_ref, mask_ref, courant_ref, adv_ref)
    for copy in m_copies:
        copy.wait()


def fix_column(dims, parity, index, halo_ref, flow_ref, mask_ref, courant_ref, adv_ref):
    tile, spots = column_place(dims, parity, index)
    sign = side_sign(parity, index)
    sea = mask_ref[tile, spots, :]
    speed = flow_ref[0, tile, spots, :]
    for k in range(dims[2] // LANES):
        lanes = slice(k * LANES, (k + 1) * LANES)
        inward = jnp.maximum(sign * (courant_ref[0:1, lanes] + speed), 0.0)
        adv_ref[k, tile, spots, :] = (
            adv_ref[k, tile, spots, :] + sea * inward * halo_ref[:, lanes]
        )


def fix_row(dims, parity, index, halo_ref, flow_ref, mask_ref, courant_ref, adv_ref):
    spots = row_place(dims, parity, index)
    sign = side_sign(parity, index)
    for i in range(dims[1] // SUBLANES):
        sea = mask_ref[i, spots, :]
        speed = flow_ref[1, i, spots, :]
        for k in range(dims[2] // LANES):
            lanes = slice(k * LANES, (k + 1) * LANES)
            inward = jnp.maximum(sign * (courant_ref[1:2, lanes] + speed), 0.0)
            adv_ref[k, i, spots, :] = (
                adv_ref[k, i, spots, :] + sea * inward * halo_ref[i, :, lanes]
            )


def ocean_border(dims, sign, along, tile, spots, halo, mask_ref, drift_ref, out_ref):
    rows, cols, bins, levels, fields = dims
    sea = mask_ref[tile, spots, :]
    shear = (sign * (0.5 * transport)) * drift_ref[along, spots, :]
    for q in range(fields):
        value = halo(slice(bins + q * levels, bins + (q + 1) * levels))
        gain = mixing_side if q < 2 else mixing_side + shear
        out_ref[q, spots, :] = out_ref[q, spots, :] + sea * (gain * value)


def source_of(dims, mats, tile, adv_ref, owner_ref, m_ref):
    chunks = dims[2] // LANES
    owner = owner_ref[tile]
    low = jnp.concatenate(
        [
            jnp.where(owner == m, adv_ref[k, tile], 0.0).astype(BF16)
            for m in range(mats)
            for k in range(chunks)
        ],
        axis=1,
    )
    weights = jnp.concatenate([m_ref[m] for m in range(mats)], axis=1)
    return lax.dot_general(low, weights, (((1,), (1,)), ((), ())), preferred_element_type=F32)


def ocean_tile(dims, tile, col_border, row_borders, parity, part_ref, grad_ref, mask_ref,
               w_ref, low_ref, drift_ref, out_ref):
    rows, cols, bins, levels, fields = dims
    drift = jnp.dot(low_ref[...], w_ref[...], preferred_element_type=F32)
    for k in range(2):
        drift_ref[k] = drift[:, k * levels : (k + 1) * levels]
    sea = mask_ref[tile]
    along = sea * drift[:, 0:levels]
    across = sea * drift[:, levels : 2 * levels]
    out_ref[0] = part_ref[0, tile] + rotation * across
    out_ref[1] = part_ref[1, tile] - rotation * along
    for q in range(2, fields):
        grad = along * grad_ref[2 * (q - 2), tile] + across * grad_ref[2 * (q - 2) + 1, tile]
        out_ref[q] = part_ref[q, tile] - (0.5 * transport) * grad
    if col_border is not None:
        index, halo_ref = col_border
        _, spots = column_place(dims, parity[0], index)
        ocean_border(
            dims, side_sign(parity[0], index), 0, tile, spots, lambda lanes: halo_ref[:, lanes],
            mask_ref, drift_ref, out_ref,
        )
    for index, halo_ref in enumerate(row_borders):
        ocean_border(
            dims, side_sign(parity[1], index), 1, tile, row_place(dims, parity[1], index),
            lambda lanes: halo_ref[tile, :, lanes], mask_ref, drift_ref, out_ref,
        )


def step_kernel(dims, mats, late, last, n_col, n_row, *refs):
    rows, cols, bins, levels, fields = dims
    tiles = cols // SUBLANES
    parity_ref, courant_ref, adv_in, part_ref, grad_ref, flow_ref = refs[:6]
    mask_ref, owner_ref, m_ref, w_ref = refs[6:10]
    refs = refs[10:]
    got_col, got_row, refs = refs[0], refs[1 : 1 + n_row], refs[1 + n_row :]
    if late:
        refs = refs[2:]
    adv_ref, e_out, o_out, *refs = refs
    if late and not last:
        col_refs, row_refs, refs = refs[:n_col], refs[n_col : n_col + n_row], refs[n_col + n_row :]
    if last:
        low_ref, drift_ref, e_tile, o_tile, sems = refs
    else:
        low_ref, drift_ref = refs
    parity = parity_ref[0], parity_ref[1]
    index = 1 if late else 0
    fixed = (flow_ref, mask_ref, courant_ref, adv_ref)
    if not late:
        for row_index in range(n_row):
            fix_row(dims, parity[1], row_index, got_row[row_index], *fixed)
    fix_column(dims, parity[0], index, got_col, *fixed)
    late_tile = (1 - low_side(parity[0], 1)) * (tiles - 1)
    if late:
        todo = [late_tile]
    else:
        walk = parity[0]
        todo = [walk * i + (1 - walk) * (tiles - 1 - i) for i in range(tiles - 1)]
    for number, tile in enumerate(todo):
        source = source_of(dims, mats, tile, adv_ref, owner_ref, m_ref)
        sea = mask_ref[tile]
        for k in range(bins // LANES):
            lanes = slice(k * LANES, (k + 1) * LANES)
            energy = sea * (adv_ref[k, tile] + source_gain * source[:, lanes])
            if last:
                e_tile[:, :, lanes] = energy.reshape(rows, SUBLANES, LANES)
            else:
                e_out[k, tile] = energy
            low_ref[:, lanes] = energy.astype(BF16)
        if last:
            e_copy = pltpu.make_async_copy(e_tile, e_out.at[:, tile], sems.at[0])
            e_copy.start()
        out_ref = o_tile if last else o_out.at[:, tile]
        ocean_tile(
            dims, tile, (index, got_col) if number == 0 else None, got_row, parity, part_ref, grad_ref, mask_ref,
            w_ref, low_ref, drift_ref, out_ref,
        )
        if last:
            o_copies = [
                pltpu.make_async_copy(
                    o_tile.at[q].reshape(rows, SUBLANES, levels), o_out.at[q, :, tile], sems.at[1 + q]
                )
                for q in range(fields)
            ]
            for copy in o_copies:
                copy.start()
            e_copy.wait()
            for copy in o_copies:
                copy.wait()
    if late and not last:

        def pack(to_ref, take):
            for k in lane_chunks(bins):
                to_ref[..., k : k + LANES] = take(e_out.at[k // LANES])
            for q in range(fields):
                to_ref[..., bins + q * levels : bins + (q + 1) * levels] = take(o_out.at[q])

        for i, to_ref in enumerate(col_refs):
            tile, spots = column_place(dims, parity[0], i)
            pack(to_ref, lambda ref: ref[tile, spots, :])
        for i, to_ref in enumerate(row_refs):
            spots = row_place(dims, parity[1], i)
            pack(to_ref, lambda ref: ref[:, spots, :])


def swap_pairs(values, axis):
    count = lax.axis_size(axis)
    got = []
    for index, value in enumerate(values):
        pairs = []
        for i in range(index, count - 1, 2):
            pairs += [(i, i + 1), (i + 1, i)]
        got.append(lax.ppermute(value, axis, pairs))
    return got


def local(spectrum, matrices, ownership, land_mask, courant, stokes_weight, ocean):
    bins, rows, cols = spectrum.shape
    fields, _, _, levels = ocean.shape
    mats = matrices.shape[2]
    tiles = cols // SUBLANES
    chunks = bins // LANES
    dims = (rows, cols, bins, levels, fields)
    n_col = 2
    n_row = 2 if lax.axis_size("tile") > 2 else 1
    e0 = jnp.transpose(spectrum, (1, 2, 0)).reshape(rows, tiles, SUBLANES, bins)
    o0 = ocean.reshape(fields, rows, tiles, SUBLANES, levels)
    m0 = matrices.reshape(mats, bins, bins)
    mask_t = land_mask.T
    owner_t = ownership.T
    parity = jnp.stack([lax.axis_index("grp") % 2, lax.axis_index("tile") % 2]).astype(jnp.int32)

    vmem = pl.BlockSpec(memory_space=VMEM)
    smem = pl.BlockSpec(memory_space=pltpu.SMEM)
    hbm = pl.BlockSpec(memory_space=pltpu.HBM)

    def points(lead, width=LANES, dtype=F32):
        return VMEM((*lead, tiles, rows * SUBLANES, width), dtype)

    adv_shape = points((chunks,))
    o_shape = points((fields,), levels)
    window_shapes = [adv_shape, o_shape, points((2 * (fields - 2),), levels), points((2,))]
    wide = bins + fields * levels
    borders = [VMEM((rows, wide), F32)] * n_col + [VMEM((tiles, SUBLANES, wide), F32)] * n_row
    dma = pltpu.SemaphoreType.DMA

    def params(mib):
        return pltpu.CompilerParams(vmem_limit_bytes=mib * 2**20)

    def exchange(sent):
        return swap_pairs(sent[:n_col], "grp") + swap_pairs(sent[n_col:], "tile")

    sent = pl.pallas_call(
        functools.partial(first_kernel, dims, n_col, n_row),
        out_shape=borders,
        in_specs=[smem, hbm, hbm],
        out_specs=[vmem] * len(borders),
        scratch_shapes=[dma((n_col + n_row, 1 + fields))],
        compiler_params=params(8),
        name="first",
    )(parity, in_hbm(e0), in_hbm(o0))
    e = o = None
    for step in range(STEPS):
        got = exchange(sent)
        if step == 0:
            adv, part, grad, flow, mask, owner, m, w = pl.pallas_call(
                functools.partial(window_kernel, dims, True),
                out_shape=window_shapes
                + [
                    points(()),
                    points((), LANES, jnp.int32),
                    VMEM((mats, bins, bins), BF16),
                    VMEM(stokes_weight.shape, BF16),
                ],
                in_specs=[hbm] * 2 + [vmem] * 3 + [hbm] * 2,
                out_specs=[vmem] * 8,
                scratch_shapes=[
                    VMEM((chunks, tiles, rows, SUBLANES, LANES), F32),
                    VMEM((fields, tiles, rows, SUBLANES, levels), F32),
                    dma((chunks, tiles)),
                    dma((fields, tiles)),
                    dma((2,)),
                ],
                compiler_params=params(16),
                name="window_first",
            )(
                in_hbm(e0), in_hbm(o0), mask_t, owner_t, courant, in_hbm(m0),
                in_hbm(stokes_weight),
            )
        else:
            adv, part, grad, flow = pl.pallas_call(
                functools.partial(window_kernel, dims, False),
                out_shape=window_shapes,
                in_specs=[vmem] * 4,
                out_specs=[vmem] * 4,
                compiler_params=params(16),
                name="window",
            )(e, o, mask, courant)
        last = step == STEPS - 1
        scratch = [VMEM((rows * SUBLANES, bins), BF16), VMEM((2, rows * SUBLANES, levels), F32)]
        if last:
            out_shape = [
                adv_shape,
                pltpu.HBM(e0.shape, F32),
                pltpu.HBM(o0.shape, F32),
            ]
            out_specs = [vmem, hbm, hbm]
            scratch += [
                VMEM((rows, SUBLANES, bins), F32),
                VMEM((fields, rows * SUBLANES, levels), F32),
                dma((1 + fields,)),
            ]
        else:
            out_shape = [adv_shape, adv_shape, o_shape]
            out_specs = [vmem] * 3
        common = (mask, owner, m, w)
        adv, e, o = pl.pallas_call(
            functools.partial(step_kernel, dims, mats, False, last, n_col, n_row),
            out_shape=out_shape,
            in_specs=[smem] + [vmem] * (10 + n_row),
            out_specs=out_specs,
            scratch_shapes=scratch,
            input_output_aliases={2: 0},
            compiler_params=params(24),
            name="early_last" if last else "early",
        )(parity, courant, adv, part, grad, flow, *common, got[0], *got[n_col:])
        extra = [] if last else borders
        e_at = 11 + n_row
        _, e, o, *sent = pl.pallas_call(
            functools.partial(step_kernel, dims, mats, True, last, n_col, n_row),
            out_shape=out_shape + extra,
            in_specs=[smem] + [vmem] * (10 + n_row) + out_specs[1:],
            out_specs=out_specs + [vmem] * len(extra),
            scratch_shapes=scratch,
            input_output_aliases={2: 0, e_at: 1, e_at + 1: 2},
            compiler_params=params(24),
            name="late_last" if last else "late",
        )(parity, courant, adv, part, grad, flow, *common, got[1], *got[n_col:], e, o)
    energy = jnp.transpose(e.reshape(rows, cols, bins), (2, 0, 1))
    return energy, o.reshape(ocean.shape)


def solution(mesh):
    in_specs = (
        P(None, "tile", "grp"),
        P("tile", "grp", None, None, None),
        P("tile", "grp"),
        P("tile", "grp"),
        P(),
        P(),
        P(None, "tile", "grp", None),
    )
    out_specs = (P(None, "tile", "grp"), P(None, "tile", "grp", None))
    return jax.shard_map(local, mesh=mesh, in_specs=in_specs, out_specs=out_specs, check_vma=False)
```

time: 34.8 us -> 36 us (1.034)
  the two profiles are of different devices: /device:TPU:25 before, /device:TPU:11 now
where the time goes in v3:
time: 36 us; the launch traced here: 35.8 us
  Pallas kernels  23.4 us (65%)
  starting transfers between devices  9.1 us (25%)
  waiting for transfers between devices  2.47 us (7%)
  between operations  0.78 us (2%)
    ppermute x6, starting transfers between devices, swap_pairs(): got.append(lax.ppermute(value, axis, pairs))  9.1 us
    pallas_call x2, Pallas kernels, local(): pl.pallas_call(functools.partial(step_kernel, dims, mats, True, last, n_c...  6.65 us
    pallas_call x2, Pallas kernels, local(): pl.pallas_call(functools.partial(step_kernel, dims, mats, False, last, n_...  6.57 us
    pallas_call x1, Pallas kernels, local(): pl.pallas_call(functools.partial(window_kernel, dims, True), out_shape=wi...  6 us
    ppermute x6, waiting for transfers between devices, swap_pairs(): got.append(lax.ppermute(value, axis, pairs))  2.47 us
    pallas_call x1, Pallas kernels, local(): pl.pallas_call(functools.partial(window_kernel, dims, False), out_shape=w...  2.23 us
    pallas_call x1, Pallas kernels, local(): pl.pallas_call(functools.partial(first_kernel, dims, n_col, n_row), out_s...  1.91 us
  transfers between devices with their start and end apart: 6, of which 1 were waited for; matrix products, arithmetic and copies ran while one was open for 0% of the time, Pallas kernels for 41%

profile of v3, /device:TPU:11, one launch (start us, length us, event | category | flops | bytes accessed | tf_op | source)
XLA Modules:
  0.0 35.8 jit_solution(3676570173137919480)
XLA Ops:
  0.6 0.0 copy-start
  0.6 0.0 copy-start.1
  0.7 0.0 copy-start.2
  0.7 0.1 pad_add_fusion.parity_ref.refs_0_
  0.8 1.9 %first.1 = (f32[32,1664]{1,0:T(8,128)S(1)}, f32[32,1664]{1,0:T(8,128)S(1)}, f32[2,8,1664]{2,1,0:T(8,128)S(1)}) custom-call(s32[2]{0:T(128)S(1)} %pad_add_fusion.parity_ref.refs_0_, f32[32,2,8,1152]{3,2,1,0:T(8,128)} %bitcast.15, f32[4,32,2,8,128]{4,3,2,1,0:T(8,128)} %bitcast.18), custom_call_target="tpu_custom_call" | custom-call | tf_op jit(solution)/shard_map/first/pallas_call | solution.py:484
  2.7 0.7 %collective-permute-start = (f32[32,1664]{1,0:T(8,128)S(1)}, f32[32,1664]{1,0:T(8,128)S(1)}, u32[]{:S(2)}, u32[]{:S(2)}) collective-permute-start(f32[32,1664]{1,0:T(8,128)S(1)} %get-tuple-element.38), channel_id=1, source_target_pairs={{0,2},{2,0},{4,6},{6,4},{8,10},{10,8},{12,14},{14,12},{16,18},{18,... | collective-permute-start | bytes 638984 | tf_op jit(solution)/shard_map/ppermute | solution.py:444
  3.4 3.1 %collective-permute-start.2 = (f32[32,1664]{1,0:T(8,128)S(1)}, f32[32,1664]{1,0:T(8,128)S(1)}, u32[]{:S(2)}, u32[]{:S(2)}) collective-permute-start(f32[32,1664]{1,0:T(8,128)S(1)} %get-tuple-element.41), channel_id=1, source_target_pairs={{2,4},{4,2},{6,8},{8,6},{10,12},{12,10},{14,16},{16,14},{18,20},{2... | collective-permute-start | bytes 638984 | tf_op jit(solution)/shard_map/ppermute | solution.py:444
  6.5 1.3 %collective-permute-start.1 = (f32[2,8,1664]{2,1,0:T(8,128)S(1)}, f32[2,8,1664]{2,1,0:T(8,128)S(1)}, u32[]{:S(2)}, u32[]{:S(2)}) collective-permute-start(f32[2,8,1664]{2,1,0:T(8,128)S(1)} %get-tuple-element.39), channel_id=1, source_target_pairs={{0,1},{1,0},{2,3},{3,2},{4,5},{5,4},{6,7},{7,6},{8,9},{9,8},{10,11... | collective-permute-start | bytes 319496 | tf_op jit(solution)/shard_map/ppermute | solution.py:444
  7.8 0.0 copy-done
  7.8 0.0 copy-done.1
  7.8 0.0 copy-done.2
  7.8 6.0 %window_first.1 = (f32[9,2,256,128]{3,2,1,0:T(8,128)S(1)}, f32[4,2,256,128]{3,2,1,0:T(8,128)S(1)}, f32[4,2,256,128]{3,2,1,0:T(8,128)S(1)}, f32[2,2,256,128]{3,2,...) custom-call(f32[32,2,8,1152]{3,2,1,0:T(8,128)} %bitcast.16, ...), custom_call_target="tpu_custom_call" | custom-call | tf_op jit(solution)/shard_map/window_first/pallas_call | solution.py:497
  13.8 0.0 collective-permute-done.1.refs_11_
  13.8 0.0 collective-permute-done.refs_10_
  13.8 2.8 %early.1 = (f32[9,2,256,128]{3,2,1,0:T(8,128)S(1)}, f32[9,2,256,128]{3,2,1,0:T(8,128)S(1)}, f32[4,2,256,128]{3,2,1,0:T(8,128)S(1)}) custom-call(s32[2]{0:T(128)S(1)} %pad_add_fusion.parity_ref.refs_0_, f32[2,1152]{1,0:T(2,128)S(1)} %copy-done, f32[9,2,256,128]{3,2,1,0:T(8,128)S(1)} %get-tuple-element.30.refs_2_, ...), custom_call_target="tpu_custom_call", output_to_operand_aliasing={{0}: (2, {})} | custom-call | tf_op jit(solution)/shard_map/early/pallas_call | solution.py:548
  16.6 0.0 collective-permute-done.2.refs_10_
  16.6 2.8 %late.1 = (f32[9,2,256,128]{3,2,1,0:T(8,128)S(1)}, f32[9,2,256,128]{3,2,1,0:T(8,128)S(1)}, f32[4,2,256,128]{3,2,1,0:T(8,128)S(1)}, f32[32,1664]{1,0:T(8,128)S(1)...) custom-call(s32[2]{0:T(128)S(1)} %pad_add_fusion.parity_ref.refs_0_,, ...), custom_call_target="tpu_custom_call", output_to_operand_aliasing={{0}: (2, {}), {1}: (12, {}), {2}: (13, {})} | custom-call | tf_op jit(solution)/shard_map/late/pallas_call | solution.py:560
  19.4 0.1 collective-permute-start.3
  19.5 3.7 %collective-permute-start.5 = (f32[32,1664]{1,0:T(8,128)S(1)}, f32[32,1664]{1,0:T(8,128)S(1)}, u32[]{:S(2)}, u32[]{:S(2)}) collective-permute-start(f32[32,1664]{1,0:T(8,128)S(1)} %get-tuple-element.53), channel_id=1, source_target_pairs={{2,4},{4,2},{6,8},{8,6},{10,12},{12,10},{14,16},{16,14},{18,20},{2... | collective-permute-start | bytes 638984 | tf_op jit(solution)/shard_map/ppermute | solution.py:444
  23.2 0.3 collective-permute-start.4
  23.5 2.2 %window.1 = (f32[9,2,256,128]{3,2,1,0:T(8,128)S(1)}, f32[4,2,256,128]{3,2,1,0:T(8,128)S(1)}, f32[4,2,256,128]{3,2,1,0:T(8,128)S(1)}, f32[2,2,256,128]{3,2,1,0:T(8,128)S(1)}) custom-call(f32[9,2,256,128]{3,2,1,0:T(8,128)S(1)} %get-tuple-element.44.e_in, f32[4,2,256,128]{3,2,1,0:T(8,128)S(1)} %get-tuple-element.45.o_in, ...), custom_call_target="tpu_custom_call" | custom-call | tf_op jit(solution)/shard_map/window/pallas_call | solution.py:522
  25.7 2.5 %collective-permute-done.4.refs_11_ = f32[2,8,1664]{2,1,0:T(8,128)S(1)} collective-permute-done((f32[2,8,1664]{2,1,0:T(8,128)S(1)}, f32[2,8,1664]{2,1,0:T(8,128)S(1)}, u32[]{:S(2)}, u32[]{:S(2)}) %collective-permute-start.4) | collective-permute-done | bytes 106528 | tf_op jit(solution)/shard_map/ppermute | solution.py:444
  28.2 0.0 collective-permute-done.3.refs_10_
  28.2 3.8 %early_last.1 = (f32[9,2,256,128]{3,2,1,0:T(8,128)S(1)}, f32[32,2,8,1152]{3,2,1,0:T(8,128)}, f32[4,32,2,8,128]{4,3,2,1,0:T(8,128)}) custom-call(s32[2]{0:T(128)S(1)} %pad_add_fusion.parity_ref.refs_0_, f32[2,1152]{1,0:T(2,128)S(1)} %copy-done, f32[9,2,256,128]{3,2,1,0:T(8,128)S(1)} %get-tuple-element.46.refs_2_, ...), custom_call_target="tpu_custom_call", output_to_operand_aliasing={{0}: (2, {})} | custom-call | tf_op jit(solution)/shard_map/early_last/pallas_call | solution.py:548
  32.0 0.0 collective-permute-done.5.refs_10_
  32.0 3.8 %late_last.1 = (f32[9,2,256,128]{3,2,1,0:T(8,128)S(1)}, f32[32,2,8,1152]{3,2,1,0:T(8,128)}, f32[4,32,2,8,128]{4,3,2,1,0:T(8,128)}) custom-call(s32[2]{0:T(128)S(1)} %pad_add_fusion.parity_ref.refs_0_, f32[2,1152]{1,0:T(2,128)S(1)} %copy-done, ...), custom_call_target="tpu_custom_call", output_to_operand_aliasing={{0}: (2, {}), {1}: (12, {}), {2}: (13, {})} | custom-call | tf_op jit(solution)/shard_map/late_last/pallas_call | solution.py:560
Async XLA Ops:
  0.6 7.1 %copy-start = (f32[2,1152]{1,0:T(2,128)S(1)}, f32[2,1152]{1,0:T(2,128)}, u32[]{:S(2)}) copy-start(f32[2,1152]{1,0:T(2,128)} %refs_1_.9) | copy-start | bytes 27652
  0.6 7.1 %copy-start.1 = (s32[32,16]{0,1:T(8,128)S(1)}, s32[32,16]{0,1:T(8,128)}, u32[]{:S(2)}) copy-start(s32[32,16]{0,1:T(8,128)} %param.10) | copy-start | bytes 6148
  0.7 7.1 %copy-start.2 = (s32[32,16]{0,1:T(8,128)S(1)}, s32[32,16]{0,1:T(8,128)}, u32[]{:S(2)}) copy-start(s32[32,16]{0,1:T(8,128)} %param.9) | copy-start | bytes 6148
  2.7 11.1 %collective-permute-start = (f32[32,1664]{1,0:T(8,128)S(1)}, f32[32,1664]{1,0:T(8,128)S(1)}, u32[]{:S(2)}, u32[]{:S(2)}) collective-permute-start(f32[32,1664]{1,0:T(8,128)S(1)} %get-tuple-element.38), channel_id=1, source_target_pairs={{0,2},{2,0},{4,6},{6,4},{8,10},{10,8},{12,14},{14,12},{16,18},{18,... | collective-permute-start | bytes 638984 | tf_op jit(solution)/shard_map/ppermute | solution.py:444
  3.4 13.2 %collective-permute-start.2 = (f32[32,1664]{1,0:T(8,128)S(1)}, f32[32,1664]{1,0:T(8,128)S(1)}, u32[]{:S(2)}, u32[]{:S(2)}) collective-permute-start(f32[32,1664]{1,0:T(8,128)S(1)} %get-tuple-element.41), channel_id=1, source_target_pairs={{2,4},{4,2},{6,8},{8,6},{10,12},{12,10},{14,16},{16,14},{18,20},{2... | collective-permute-start | bytes 638984 | tf_op jit(solution)/shard_map/ppermute | solution.py:444
  6.5 7.3 %collective-permute-start.1 = (f32[2,8,1664]{2,1,0:T(8,128)S(1)}, f32[2,8,1664]{2,1,0:T(8,128)S(1)}, u32[]{:S(2)}, u32[]{:S(2)}) collective-permute-start(f32[2,8,1664]{2,1,0:T(8,128)S(1)} %get-tuple-element.39), channel_id=1, source_target_pairs={{0,1},{1,0},{2,3},{3,2},{4,5},{5,4},{6,7},{7,6},{8,9},{9,8},{10,11... | collective-permute-start | bytes 319496 | tf_op jit(solution)/shard_map/ppermute | solution.py:444
  19.4 8.7 %collective-permute-start.3 = (f32[32,1664]{1,0:T(8,128)S(1)}, f32[32,1664]{1,0:T(8,128)S(1)}, u32[]{:S(2)}, u32[]{:S(2)}) collective-permute-start(f32[32,1664]{1,0:T(8,128)S(1)} %get-tuple-element.50), channel_id=1, source_target_pairs={{0,2},{2,0},{4,6},{6,4},{8,10},{10,8},{12,14},{14,12},{16,18},{18,... | collective-permute-start | bytes 638984 | tf_op jit(solution)/shard_map/ppermute | solution.py:444
  19.5 12.5 %collective-permute-start.5 = (f32[32,1664]{1,0:T(8,128)S(1)}, f32[32,1664]{1,0:T(8,128)S(1)}, u32[]{:S(2)}, u32[]{:S(2)}) collective-permute-start(f32[32,1664]{1,0:T(8,128)S(1)} %get-tuple-element.53), channel_id=1, source_target_pairs={{2,4},{4,2},{6,8},{8,6},{10,12},{12,10},{14,16},{16,14},{18,20},{2... | collective-permute-start | bytes 638984 | tf_op jit(solution)/shard_map/ppermute | solution.py:444
  23.2 5.0 %collective-permute-start.4 = (f32[2,8,1664]{2,1,0:T(8,128)S(1)}, f32[2,8,1664]{2,1,0:T(8,128)S(1)}, u32[]{:S(2)}, u32[]{:S(2)}) collective-permute-start(f32[2,8,1664]{2,1,0:T(8,128)S(1)} %get-tuple-element.51), channel_id=1, source_target_pairs={{0,1},{1,0},{2,3},{3,2},{4,5},{5,4},{6,7},{7,6},{8,9},{9,8},{10,11... | collective-permute-start | bytes 319496 | tf_op jit(solution)/shard_map/ppermute | solution.py:444

commit v4 on v3

--- a/solution.py
+++ b/solution.py
@@ -7,6 +7,7 @@
 from jax.experimental.pallas import tpu as pltpu
 from jax.sharding import PartitionSpec as P
 
+
 STEPS = 2
 
 current_gain = 0.2
@@ -31,16 +32,12 @@
     return range(0, width, LANES)
 
 
-def spread(columns, r, cols):
-    return jnp.broadcast_to(columns[:, r : r + 1], (cols, LANES))
-
-
 def low_side(parity, index):
     return parity if index == 0 else 1 - parity
 
 
 def column_place(dims, parity, index):
-    rows, cols, bins, levels, fields = dims
+    rows, cols, _, _, _ = dims
     high = 1 - low_side(parity, index)
     tile = high * (cols // SUBLANES - 1)
     return tile, pl.ds(high * (SUBLANES - 1), rows, stride=SUBLANES)
@@ -126,14 +123,8 @@
     return slice(r * SUBLANES, (r + 1) * SUBLANES)
 
 
-def tile_at(ref, lead, i, r):
-    if ref.ndim == 5:
-        return ref[lead, i, r]
-    return ref[lead, i, span(r), :]
-
-
-def advect_all(dims, e_ref, arrived, flow_ref, mask_ref, courant_ref, adv_ref):
-    rows, cols, bins, levels, fields = dims
+def advect_all(dims, energy_at, arrived, flow_ref, mask_ref, courant_ref, adv_ref):
+    rows, cols, bins, _, _ = dims
     ends = sublane_ends()
     tiles = cols // SUBLANES
 
@@ -148,7 +139,7 @@
         def load(r):
             if r >= rows:
                 return None
-            return [tile_at(e_ref, k, i, r) for i in range(tiles)]
+            return [energy_at(k, i, r) for i in range(tiles)]
 
         mid = load(0)
         falls = mid
@@ -172,8 +163,8 @@
     lax.fori_loop(0, bins // LANES, body, 0)
 
 
-def ocean_all(dims, o_ref, mask_ref, part_ref, grad_ref):
-    rows, cols, bins, levels, fields = dims
+def ocean_all(dims, ocean_at, mask_ref, part_ref, grad_ref):
+    rows, cols, _, levels, fields = dims
     ends = sublane_ends()
     level_id = lax.broadcasted_iota(jnp.int32, (SUBLANES, levels), 1)
     top = level_id == 0
@@ -182,11 +173,11 @@
 
     for q in range(fields):
         north = None
-        mid = [tile_at(o_ref, q, i, 0) for i in range(tiles)]
+        mid = [ocean_at(q, i, 0) for i in range(tiles)]
         for r in range(rows):
             south = None
             if r + 1 < rows:
-                south = [tile_at(o_ref, q, i, r + 1) for i in range(tiles)]
+                south = [ocean_at(q, i, r + 1) for i in range(tiles)]
             west = shifted(mid, ends, False)
             east = shifted(mid, ends, True)
             for i in range(tiles):
@@ -202,9 +193,9 @@
                 tend = mixing_side * (across + (west[i] + east[i])) + mixing_depth * (above + below)
                 tend = tend - (4 * mixing_side + 2 * mixing_depth) * own
                 if q == 0:
-                    tend = tend + rotation * tile_at(o_ref, 1, i, r)
+                    tend = tend + rotation * ocean_at(1, i, r)
                 elif q == 1:
-                    tend = tend - rotation * tile_at(o_ref, 0, i, r)
+                    tend = tend - rotation * ocean_at(0, i, r)
                 else:
                     grad_ref[2 * (q - 2), i, span(r), :] = east[i] - west[i]
                     grad_ref[2 * (q - 2) + 1, i, span(r), :] = slope
@@ -212,39 +203,21 @@
             north, mid = mid, south
 
 
-def window_kernel(dims, first, e_in, o_in, *refs):
-    rows, cols, bins, levels, fields = dims
+def window_kernel(dims, first, e_ref, o_ref, *refs):
+    rows, cols, bins, _, _ = dims
     tiles = cols // SUBLANES
     if first:
-        mask_t, owner_t, courant_ref, m_hbm, w_hbm = refs[:5]
-        adv_ref, part_ref, grad_ref, flow_ref, mask_ref, owner_ref, m_ref, w_ref = refs[5:13]
-        e_ref, o_ref, e_sems, o_sems, m_sems = refs[13:]
-
-        def e_copies(k):
+        mask_t, owner_t, courant_ref, adv_ref, part_ref, grad_ref, flow_ref = refs[:7]
+        mask_ref, owner_ref, e_here, o_here, sems = refs[7:]
+
+        def e_copy(k):
             lanes = pl.ds(pl.multiple_of(k * LANES, LANES), LANES)
-            return [
-                pltpu.make_async_copy(
-                    e_in.at[:, i, :, lanes], e_ref.at[k, i], e_sems.at[k, i]
-                )
-                for i in range(tiles)
-            ]
-
-        o_copies = [
-            pltpu.make_async_copy(o_in.at[q, :, i], o_ref.at[q, i], o_sems.at[q, i])
-            for q in range(fields)
-            for i in range(tiles)
-        ]
-        m_copies = [
-            pltpu.make_async_copy(m_hbm, m_ref, m_sems.at[0]),
-            pltpu.make_async_copy(w_hbm, w_ref, m_sems.at[1]),
-        ]
-        for copy in o_copies:
-            copy.start()
+            return pltpu.make_async_copy(e_ref.at[..., lanes], e_here.at[k], sems.at[k])
+
+        o_copy = pltpu.make_async_copy(o_ref, o_here, sems.at[bins // LANES])
+        o_copy.start()
         for k in range(bins // LANES):
-            for copy in e_copies(k):
-                copy.start()
-        for copy in m_copies:
-            copy.start()
+            e_copy(k).start()
         mask = mask_t[...].astype(F32)
         owner = owner_t[...]
         for i in range(tiles):
@@ -253,29 +226,28 @@
                     to_ref[i, span(r), :] = jnp.broadcast_to(
                         values[span(i), r : r + 1], (SUBLANES, LANES)
                     )
-        for copy in o_copies:
-            copy.wait()
+        o_copy.wait()
     else:
         mask_ref, courant_ref, adv_ref, part_ref, grad_ref, flow_ref = refs
-        e_ref, o_ref = e_in, o_in
-        m_copies = []
 
     def arrived(k):
         if first:
-            for copy in e_copies(k):
-                copy.wait()
+            e_copy(k).wait()
+
+    def energy_at(k, i, r):
+        return e_here[k, r, i] if first else e_ref[k, i, span(r), :]
+
+    def ocean_at(q, i, r):
+        return o_here[q, r, i] if first else o_ref[q, i, span(r), :]
 
     for way in range(2):
         for i in range(tiles):
             for r in range(rows):
-                current = tile_at(o_ref, way, i, r)
                 flow_ref[way, i, span(r), :] = jnp.broadcast_to(
-                    current_gain * current[:, 0:1], (SUBLANES, LANES)
+                    current_gain * ocean_at(way, i, r)[:, 0:1], (SUBLANES, LANES)
                 )
-    ocean_all(dims, o_ref, mask_ref, part_ref, grad_ref)
-    advect_all(dims, e_ref, arrived, flow_ref, mask_ref, courant_ref, adv_ref)
-    for copy in m_copies:
-        copy.wait()
+    ocean_all(dims, ocean_at, mask_ref, part_ref, grad_ref)
+    advect_all(dims, energy_at, arrived, flow_ref, mask_ref, courant_ref, adv_ref)
 
 
 def fix_column(dims, parity, index, halo_ref, flow_ref, mask_ref, courant_ref, adv_ref):
@@ -306,7 +278,7 @@
 
 
 def ocean_border(dims, sign, along, tile, spots, halo, mask_ref, drift_ref, out_ref):
-    rows, cols, bins, levels, fields = dims
+    _, _, bins, levels, fields = dims
     sea = mask_ref[tile, spots, :]
     shear = (sign * (0.5 * transport)) * drift_ref[along, spots, :]
     for q in range(fields):
@@ -332,7 +304,7 @@
 
 def ocean_tile(dims, tile, col_border, row_borders, parity, part_ref, grad_ref, mask_ref,
                w_ref, low_ref, drift_ref, out_ref):
-    rows, cols, bins, levels, fields = dims
+    _, _, _, levels, fields = dims
     drift = jnp.dot(low_ref[...], w_ref[...], preferred_element_type=F32)
     for k in range(2):
         drift_ref[k] = drift[:, k * levels : (k + 1) * levels]
@@ -361,64 +333,79 @@
 def step_kernel(dims, mats, late, last, n_col, n_row, *refs):
     rows, cols, bins, levels, fields = dims
     tiles = cols // SUBLANES
-    parity_ref, courant_ref, adv_in, part_ref, grad_ref, flow_ref = refs[:6]
+    parity_ref, courant_ref, _, part_ref, grad_ref, flow_ref = refs[:6]
     mask_ref, owner_ref, m_ref, w_ref = refs[6:10]
     refs = refs[10:]
     got_col, got_row, refs = refs[0], refs[1 : 1 + n_row], refs[1 + n_row :]
     if late:
-        refs = refs[2:]
+        e_early, o_early, *refs = refs
     adv_ref, e_out, o_out, *refs = refs
     if late and not last:
         col_refs, row_refs, refs = refs[:n_col], refs[n_col : n_col + n_row], refs[n_col + n_row :]
-    if last:
-        low_ref, drift_ref, e_tile, o_tile, sems = refs
-    else:
-        low_ref, drift_ref = refs
+    low_ref, drift_ref, *refs = refs
     parity = parity_ref[0], parity_ref[1]
     index = 1 if late else 0
+    walk = parity[0]
+    todo = [walk * i + (1 - walk) * (tiles - 1 - i) for i in range(tiles)]
+    copies = []
+    if late and last:
+        e_tile, o_tile, sems = refs
+
+        def store(number, e_from, o_from):
+            tile = todo[number]
+            made = [pltpu.make_async_copy(e_from, e_out.at[:, tile], sems.at[number, 0])]
+            for q in range(fields):
+                made.append(
+                    pltpu.make_async_copy(
+                        o_from.at[q].reshape(rows, SUBLANES, levels),
+                        o_out.at[q, :, tile],
+                        sems.at[number, 1 + q],
+                    )
+                )
+            return made
+
+        for number in range(tiles - 1):
+            copies += store(number, e_early.at[number], o_early.at[number])
+        for copy in copies:
+            copy.start()
     fixed = (flow_ref, mask_ref, courant_ref, adv_ref)
     if not late:
         for row_index in range(n_row):
             fix_row(dims, parity[1], row_index, got_row[row_index], *fixed)
     fix_column(dims, parity[0], index, got_col, *fixed)
-    late_tile = (1 - low_side(parity[0], 1)) * (tiles - 1)
-    if late:
-        todo = [late_tile]
-    else:
-        walk = parity[0]
-        todo = [walk * i + (1 - walk) * (tiles - 1 - i) for i in range(tiles - 1)]
     for number, tile in enumerate(todo):
+        if late != (number == tiles - 1):
+            continue
         source = source_of(dims, mats, tile, adv_ref, owner_ref, m_ref)
         sea = mask_ref[tile]
         for k in range(bins // LANES):
             lanes = slice(k * LANES, (k + 1) * LANES)
             energy = sea * (adv_ref[k, tile] + source_gain * source[:, lanes])
-            if last:
+            if not last:
+                e_out[k, tile] = energy
+            elif late:
                 e_tile[:, :, lanes] = energy.reshape(rows, SUBLANES, LANES)
             else:
-                e_out[k, tile] = energy
+                e_out[number, :, :, lanes] = energy.reshape(rows, SUBLANES, LANES)
             low_ref[:, lanes] = energy.astype(BF16)
-        if last:
-            e_copy = pltpu.make_async_copy(e_tile, e_out.at[:, tile], sems.at[0])
+        if not last:
+            out_ref = o_out.at[:, tile]
+        elif late:
+            out_ref = o_tile
+            e_copy, *o_copies = store(number, e_tile, o_tile)
             e_copy.start()
-        out_ref = o_tile if last else o_out.at[:, tile]
+        else:
+            out_ref = o_out.at[number]
         ocean_tile(
-            dims, tile, (index, got_col) if number == 0 else None, got_row, parity, part_ref, grad_ref, mask_ref,
-            w_ref, low_ref, drift_ref, out_ref,
+            dims, tile, (index, got_col) if late or number == 0 else None, got_row, parity,
+            part_ref, grad_ref, mask_ref, w_ref, low_ref, drift_ref, out_ref,
         )
-        if last:
-            o_copies = [
-                pltpu.make_async_copy(
-                    o_tile.at[q].reshape(rows, SUBLANES, levels), o_out.at[q, :, tile], sems.at[1 + q]
-                )
-                for q in range(fields)
-            ]
-            for copy in o_copies:
-                copy.start()
-            e_copy.wait()
-            for copy in o_copies:
-                copy.wait()
-    if late and not last:
+    if late and last:
+        for copy in o_copies:
+            copy.start()
+        for copy in copies + [e_copy] + o_copies:
+            copy.wait()
+    elif late:
 
         def pack(to_ref, take):
             for k in lane_chunks(bins):
@@ -451,6 +438,7 @@
     mats = matrices.shape[2]
     tiles = cols // SUBLANES
     chunks = bins // LANES
+    points_count = rows * cols
     dims = (rows, cols, bins, levels, fields)
     n_col = 2
     n_row = 2 if lax.axis_size("tile") > 2 else 1
@@ -474,6 +462,8 @@
     wide = bins + fields * levels
     borders = [VMEM((rows, wide), F32)] * n_col + [VMEM((tiles, SUBLANES, wide), F32)] * n_row
     dma = pltpu.SemaphoreType.DMA
+    moved = 4 * points_count * (chunks * LANES + fields * levels)
+    cost = pl.CostEstimate(flops=0, transcendentals=0, bytes_accessed=4 * moved)
 
     def params(mib):
         return pltpu.CompilerParams(vmem_limit_bytes=mib * 2**20)
@@ -488,82 +478,78 @@
         out_specs=[vmem] * len(borders),
         scratch_shapes=[dma((n_col + n_row, 1 + fields))],
         compiler_params=params(8),
+        cost_estimate=cost,
         name="first",
     )(parity, in_hbm(e0), in_hbm(o0))
     e = o = None
     for step in range(STEPS):
         got = exchange(sent)
         if step == 0:
-            adv, part, grad, flow, mask, owner, m, w = pl.pallas_call(
+            adv, part, grad, flow, mask, owner = pl.pallas_call(
                 functools.partial(window_kernel, dims, True),
-                out_shape=window_shapes
-                + [
-                    points(()),
-                    points((), LANES, jnp.int32),
-                    VMEM((mats, bins, bins), BF16),
-                    VMEM(stokes_weight.shape, BF16),
+                out_shape=window_shapes + [points(()), points((), LANES, jnp.int32)],
+                in_specs=[hbm] * 2 + [vmem] * 3,
+                out_specs=[vmem] * 6,
+                scratch_shapes=[
+                    VMEM((chunks, rows, tiles, SUBLANES, LANES), F32),
+                    VMEM((fields, rows, tiles, SUBLANES, levels), F32),
+                    dma((chunks + 1,)),
                 ],
-                in_specs=[hbm] * 2 + [vmem] * 3 + [hbm] * 2,
-                out_specs=[vmem] * 8,
-                scratch_shapes=[
-                    VMEM((chunks, tiles, rows, SUBLANES, LANES), F32),
-                    VMEM((fields, tiles, rows, SUBLANES, levels), F32),
-                    dma((chunks, tiles)),
-                    dma((fields, tiles)),
-                    dma((2,)),
-                ],
-                compiler_params=params(16),
+                compiler_params=params(12),
+                cost_estimate=cost,
                 name="window_first",
-            )(
-                in_hbm(e0), in_hbm(o0), mask_t, owner_t, courant, in_hbm(m0),
-                in_hbm(stokes_weight),
-            )
+            )(in_hbm(e0), in_hbm(o0), mask_t, owner_t, courant)
         else:
             adv, part, grad, flow = pl.pallas_call(
                 functools.partial(window_kernel, dims, False),
                 out_shape=window_shapes,
                 in_specs=[vmem] * 4,
                 out_specs=[vmem] * 4,
-                compiler_params=params(16),
+                compiler_params=params(8),
+                cost_estimate=cost,
                 name="window",
             )(e, o, mask, courant)
         last = step == STEPS - 1
         scratch = [VMEM((rows * SUBLANES, bins), BF16), VMEM((2, rows * SUBLANES, levels), F32)]
         if last:
-            out_shape = [
-                adv_shape,
-                pltpu.HBM(e0.shape, F32),
-                pltpu.HBM(o0.shape, F32),
-            ]
-            out_specs = [vmem, hbm, hbm]
-            scratch += [
-                VMEM((rows, SUBLANES, bins), F32),
-                VMEM((fields, rows * SUBLANES, levels), F32),
-                dma((1 + fields,)),
+            early_shape = [
+                VMEM((tiles - 1, rows, SUBLANES, bins), F32),
+                VMEM((tiles - 1, fields, rows * SUBLANES, levels), F32),
             ]
         else:
-            out_shape = [adv_shape, adv_shape, o_shape]
-            out_specs = [vmem] * 3
-        common = (mask, owner, m, w)
+            early_shape = [adv_shape, o_shape]
+        common = (mask, owner, m0, stokes_weight)
         adv, e, o = pl.pallas_call(
             functools.partial(step_kernel, dims, mats, False, last, n_col, n_row),
-            out_shape=out_shape,
+            out_shape=[adv_shape] + early_shape,
             in_specs=[smem] + [vmem] * (10 + n_row),
-            out_specs=out_specs,
+            out_specs=[vmem] * 3,
             scratch_shapes=scratch,
             input_output_aliases={2: 0},
             compiler_params=params(24),
             name="early_last" if last else "early",
         )(parity, courant, adv, part, grad, flow, *common, got[0], *got[n_col:])
-        extra = [] if last else borders
         e_at = 11 + n_row
+        aliases = {2: 0}
+        if last:
+            late_shape = [pltpu.HBM(e0.shape, F32), pltpu.HBM(o0.shape, F32)]
+            late_specs = [vmem, hbm, hbm]
+            scratch += [
+                VMEM((rows, SUBLANES, bins), F32),
+                VMEM((fields, rows * SUBLANES, levels), F32),
+                dma((tiles, 1 + fields)),
+            ]
+        else:
+            late_shape = early_shape + borders
+            late_specs = [vmem] * (1 + len(late_shape))
+            aliases.update({e_at: 1, e_at + 1: 2})
         _, e, o, *sent = pl.pallas_call(
             functools.partial(step_kernel, dims, mats, True, last, n_col, n_row),
-            out_shape=out_shape + extra,
-            in_specs=[smem] + [vmem] * (10 + n_row) + out_specs[1:],
-            out_specs=out_specs + [vmem] * len(extra),
+            out_shape=[adv_shape] + late_shape,
+            in_specs=[smem] + [vmem] * (12 + n_row),
+            out_specs=late_specs,
             scratch_shapes=scratch,
-            input_output_aliases={2: 0, e_at: 1, e_at + 1: 2},
+            input_output_aliases=aliases,
             compiler_params=params(24),
             name="late_last" if last else "late",
         )(parity, courant, adv, part, grad, flow, *common, got[1], *got[n_col:], e, o)

time: 36 us -> 33 us (0.917)
  the two profiles are of different devices: /device:TPU:11 before, /device:TPU:19 now
where the time goes in v4:
time: 33 us; the launch traced here: 32.8 us
  Pallas kernels  20.4 us (62%)
  starting transfers between devices  10.1 us (31%)
  waiting for transfers between devices  1.47 us (4%)
  between operations  0.79 us (2%)
    ppermute x6, starting transfers between devices, swap_pairs(): got.append(lax.ppermute(value, axis, pairs))  10.1 us
    pallas_call x2, Pallas kernels, local(): pl.pallas_call(functools.partial(step_kernel, dims, mats, True, last, n_c...  6.95 us
    pallas_call x2, Pallas kernels, local(): pl.pallas_call(functools.partial(step_kernel, dims, mats, False, last, n_...  5.41 us
    pallas_call x1, Pallas kernels, local(): pl.pallas_call(functools.partial(window_kernel, dims, True), out_shape=wi...  3.6 us
    pallas_call x1, Pallas kernels, local(): pl.pallas_call(functools.partial(window_kernel, dims, False), out_shape=w...  2.23 us
    pallas_call x1, Pallas kernels, local(): pl.pallas_call(functools.partial(first_kernel, dims, n_col, n_row), out_s...  2.18 us
    ppermute x6, waiting for transfers between devices, swap_pairs(): got.append(lax.ppermute(value, axis, pairs))  1.47 us
  transfers between devices with their start and end apart: 6, of which 1 were waited for; matrix products, arithmetic and copies ran while one was open for 0% of the time, Pallas kernels for 34%

profile of v4, /device:TPU:19, one launch (start us, length us, event | category | flops | bytes accessed | tf_op | source)
XLA Modules:
  0.0 32.8 jit_solution(11014670196013033601)
XLA Ops:
  0.6 0.0 copy-start.2
  0.6 0.0 copy-start.3
  0.7 0.0 copy-start.4
  0.7 0.1 pad_add_fusion.parity_ref.refs_0_
  0.8 0.0 copy-start
  0.8 2.2 %first.1 = (f32[32,1664]{1,0:T(8,128)S(1)}, f32[32,1664]{1,0:T(8,128)S(1)}, f32[2,8,1664]{2,1,0:T(8,128)S(1)}) custom-call(s32[2]{0:T(128)S(1)} %pad_add_fusion.parity_ref.refs_0_, f32[32,2,8,1152]{3,2,1,0:T(8,128)} %bitcast.19, f32[4,32,2,8,128]{4,3,2,1,0:T(8,128)} %bitcast.21), custom_call_target="tpu_custom_call" | custom-call | bytes 13631488 | tf_op jit(solution)/shard_map/first/pallas_call | solution.py:474
  2.9 0.0 copy-start.1
  3.0 0.7 %collective-permute-start = (f32[32,1664]{1,0:T(8,128)S(1)}, f32[32,1664]{1,0:T(8,128)S(1)}, u32[]{:S(2)}, u32[]{:S(2)}) collective-permute-start(f32[32,1664]{1,0:T(8,128)S(1)} %get-tuple-element.34), channel_id=1, source_target_pairs={{0,2},{2,0},{4,6},{6,4},{8,10},{10,8},{12,14},{14,12},{16,18},{18,... | collective-permute-start | bytes 638984 | tf_op jit(solution)/shard_map/ppermute | solution.py:431
  3.6 3.2 %collective-permute-start.2 = (f32[32,1664]{1,0:T(8,128)S(1)}, f32[32,1664]{1,0:T(8,128)S(1)}, u32[]{:S(2)}, u32[]{:S(2)}) collective-permute-start(f32[32,1664]{1,0:T(8,128)S(1)} %get-tuple-element.37), channel_id=1, source_target_pairs={{2,4},{4,2},{6,8},{8,6},{10,12},{12,10},{14,16},{16,14},{18,20},{2... | collective-permute-start | bytes 638984 | tf_op jit(solution)/shard_map/ppermute | solution.py:431
  6.8 1.3 %collective-permute-start.1 = (f32[2,8,1664]{2,1,0:T(8,128)S(1)}, f32[2,8,1664]{2,1,0:T(8,128)S(1)}, u32[]{:S(2)}, u32[]{:S(2)}) collective-permute-start(f32[2,8,1664]{2,1,0:T(8,128)S(1)} %get-tuple-element.35), channel_id=1, source_target_pairs={{0,1},{1,0},{2,3},{3,2},{4,5},{5,4},{6,7},{7,6},{8,9},{9,8},{10,11... | collective-permute-start | bytes 319496 | tf_op jit(solution)/shard_map/ppermute | solution.py:431
  8.1 0.0 copy-done.2
  8.1 0.0 copy-done.3
  8.1 0.0 copy-done.4
  8.1 3.6 %window_first.1 = (f32[9,2,256,128]{3,2,1,0:T(8,128)S(1)}, f32[4,2,256,128]{3,2,1,0:T(8,128)S(1)}, f32[4,2,256,128]{3,2,1,0:T(8,128)S(1)}, f32[2,2,256,128]{3,2,...) custom-call(f32[32,2,8,1152]{3,2,1,0:T(8,128)} %bitcast.20, f32[4,32,2,8,128]{4,3,2,1,0:T(8,128)} %bitcast.22, ...), custom_call_target="tpu_custom_call" | custom-call | bytes 13631488 | tf_op jit(solution)/shard_map/window_first/pallas_call | solution.py:488
  11.8 0.0 collective-permute-done.1.refs_11_
  11.8 0.0 collective-permute-done.refs_10_
  11.8 0.0 copy-done
  11.8 0.0 copy-done.1
  11.8 2.7 %early.1 = (f32[9,2,256,128]{3,2,1,0:T(8,128)S(1)}, f32[9,2,256,128]{3,2,1,0:T(8,128)S(1)}, f32[4,2,256,128]{3,2,1,0:T(8,128)S(1)}) custom-call(s32[2]{0:T(128)S(1)} %pad_add_fusion.parity_ref.refs_0_, f32[2,1152]{1,0:T(2,128)S(1)} %copy-done.2, f32[9,2,256,128]{3,2,1,0:T(8,128)S(1)} %get-tuple-element.28.refs_2_, ...), custom_call_target="tpu_custom_call", output_to_operand_aliasing={{0}: (2, {})} | custom-call | tf_op jit(solution)/shard_map/early/pallas_call | solution.py:522
  14.5 0.0 collective-permute-done.2.refs_10_
  14.5 2.8 %late.1 = (f32[9,2,256,128]{3,2,1,0:T(8,128)S(1)}, f32[9,2,256,128]{3,2,1,0:T(8,128)S(1)}, f32[4,2,256,128]{3,2,1,0:T(8,128)S(1)}, f32[32,1664]{1,0:T(8,128)S(1)...) custom-call(s32[2]{0:T(128)S(1)} %pad_add_fusion.parity_ref.refs_0_,, ...), custom_call_target="tpu_custom_call", output_to_operand_aliasing={{0}: (2, {}), {1}: (12, {}), {2}: (13, {})} | custom-call | tf_op jit(solution)/shard_map/late/pallas_call | solution.py:546
  17.3 0.2 collective-permute-start.3
  17.5 3.4 %collective-permute-start.5 = (f32[32,1664]{1,0:T(8,128)S(1)}, f32[32,1664]{1,0:T(8,128)S(1)}, u32[]{:S(2)}, u32[]{:S(2)}) collective-permute-start(f32[32,1664]{1,0:T(8,128)S(1)} %get-tuple-element.49), channel_id=1, source_target_pairs={{2,4},{4,2},{6,8},{8,6},{10,12},{12,10},{14,16},{16,14},{18,20},{2... | collective-permute-start | bytes 638984 | tf_op jit(solution)/shard_map/ppermute | solution.py:431
  20.9 1.3 %collective-permute-start.4 = (f32[2,8,1664]{2,1,0:T(8,128)S(1)}, f32[2,8,1664]{2,1,0:T(8,128)S(1)}, u32[]{:S(2)}, u32[]{:S(2)}) collective-permute-start(f32[2,8,1664]{2,1,0:T(8,128)S(1)} %get-tuple-element.47), channel_id=1, source_target_pairs={{0,1},{1,0},{2,3},{3,2},{4,5},{5,4},{6,7},{7,6},{8,9},{9,8},{10,11... | collective-permute-start | bytes 319496 | tf_op jit(solution)/shard_map/ppermute | solution.py:431
  22.2 2.2 %window.1 = (f32[9,2,256,128]{3,2,1,0:T(8,128)S(1)}, f32[4,2,256,128]{3,2,1,0:T(8,128)S(1)}, f32[4,2,256,128]{3,2,1,0:T(8,128)S(1)}, f32[2,2,256,128]{3,2,1,0:T(8,128)S(1)}) custom-call(f32[9,2,256,128]{3,2,1,0:T(8,128)S(1)} %get-tuple-element.40.e_ref, f32[4,2,256,128]{3,2,1,0:T(8,128)S(1)} %get-tuple-element.41.o_ref, ...), custom_call_target="tpu_custom_call" | custom-call | bytes 13631488 | tf_op jit(solution)/shard_map/window/pallas_call | solution.py:503
  24.5 1.5 %collective-permute-done.4.refs_11_ = f32[2,8,1664]{2,1,0:T(8,128)S(1)} collective-permute-done((f32[2,8,1664]{2,1,0:T(8,128)S(1)}, f32[2,8,1664]{2,1,0:T(8,128)S(1)}, u32[]{:S(2)}, u32[]{:S(2)}) %collective-permute-start.4) | collective-permute-done | bytes 106528 | tf_op jit(solution)/shard_map/ppermute | solution.py:431
  25.9 0.0 collective-permute-done.3.refs_10_
  25.9 2.7 %early_last.1 = (f32[9,2,256,128]{3,2,1,0:T(8,128)S(1)}, f32[1,32,8,1152]{3,2,1,0:T(8,128)S(1)}, f32[1,4,256,128]{3,2,1,0:T(8,128)S(1)}) custom-call(s32[2]{0:T(128)S(1)} %pad_add_fusion.parity_ref.refs_0_, f32[2,1152]{1,0:T(2,128)S(1)} %copy-done.2, f32[9,2,256,128]{3,2,1,0:T(8,128)S(1)} %get-tuple-element.42.refs_2_, ...), custom_call_target="tpu_custom_call", output_to_operand_aliasing={{0}: (2, {})} | custom-call | tf_op jit(solution)/shard_map/early_last/pallas_call | solution.py:522
  28.6 0.0 collective-permute-done.5.refs_10_
  28.6 4.1 %late_last.1 = (f32[9,2,256,128]{3,2,1,0:T(8,128)S(1)}, f32[32,2,8,1152]{3,2,1,0:T(8,128)}, f32[4,32,2,8,128]{4,3,2,1,0:T(8,128)}) custom-call(s32[2]{0:T(128)S(1)} %pad_add_fusion.parity_ref.refs_0_, f32[2,1152]{1,0:T(2,128)S(1)} %copy-done.2, f32[9,2,256,128]{3,2,1,0:T(8,128)S(1)} %get-tuple-element.48.refs_2_, ...), custom_call_target="tpu_custom_call", output_to_operand_aliasing={{0}: (2, {})} | custom-call | tf_op jit(solution)/shard_map/late_last/pallas_call | solution.py:546
Async XLA Ops:
  0.6 7.5 %copy-start.2 = (f32[2,1152]{1,0:T(2,128)S(1)}, f32[2,1152]{1,0:T(2,128)}, u32[]{:S(2)}) copy-start(f32[2,1152]{1,0:T(2,128)} %refs_1_.9) | copy-start | bytes 27652
  0.6 7.5 %copy-start.3 = (s32[32,16]{0,1:T(8,128)S(1)}, s32[32,16]{0,1:T(8,128)}, u32[]{:S(2)}) copy-start(s32[32,16]{0,1:T(8,128)} %param.10) | copy-start | bytes 6148
  0.7 7.5 %copy-start.4 = (s32[32,16]{0,1:T(8,128)S(1)}, s32[32,16]{0,1:T(8,128)}, u32[]{:S(2)}) copy-start(s32[32,16]{0,1:T(8,128)} %param.9) | copy-start | bytes 6148
  0.8 11.0 %copy-start = (bf16[1,1,2,1152,1152]{4,3,2,1,0:T(8,128)(2,1)S(1)}, bf16[1,1,2,1152,1152]{4,3,2,1,0:T(8,128)(2,1)}, u32[]{:S(2)}) copy-start(bf16[1,1,2,1152,1152]{4,3,2,1,0:T(8,128)(2,1)} %param.8) | copy-start | bytes 15925252
  2.9 8.8 %copy-start.1 = (bf16[1152,256]{1,0:T(8,128)(2,1)S(1)}, bf16[1152,256]{1,0:T(8,128)(2,1)}, u32[]{:S(2)}) copy-start(bf16[1152,256]{1,0:T(8,128)(2,1)} %refs_9_.7) | copy-start | bytes 1769476
  3.0 8.8 %collective-permute-start = (f32[32,1664]{1,0:T(8,128)S(1)}, f32[32,1664]{1,0:T(8,128)S(1)}, u32[]{:S(2)}, u32[]{:S(2)}) collective-permute-start(f32[32,1664]{1,0:T(8,128)S(1)} %get-tuple-element.34), channel_id=1, source_target_pairs={{0,2},{2,0},{4,6},{6,4},{8,10},{10,8},{12,14},{14,12},{16,18},{18,... | collective-permute-start | bytes 638984 | tf_op jit(solution)/shard_map/ppermute | solution.py:431
  3.6 10.9 %collective-permute-start.2 = (f32[32,1664]{1,0:T(8,128)S(1)}, f32[32,1664]{1,0:T(8,128)S(1)}, u32[]{:S(2)}, u32[]{:S(2)}) collective-permute-start(f32[32,1664]{1,0:T(8,128)S(1)} %get-tuple-element.37), channel_id=1, source_target_pairs={{2,4},{4,2},{6,8},{8,6},{10,12},{12,10},{14,16},{16,14},{18,20},{2... | collective-permute-start | bytes 638984 | tf_op jit(solution)/shard_map/ppermute | solution.py:431
  6.8 4.9 %collective-permute-start.1 = (f32[2,8,1664]{2,1,0:T(8,128)S(1)}, f32[2,8,1664]{2,1,0:T(8,128)S(1)}, u32[]{:S(2)}, u32[]{:S(2)}) collective-permute-start(f32[2,8,1664]{2,1,0:T(8,128)S(1)} %get-tuple-element.35), channel_id=1, source_target_pairs={{0,1},{1,0},{2,3},{3,2},{4,5},{5,4},{6,7},{7,6},{8,9},{9,8},{10,11... | collective-permute-start | bytes 319496 | tf_op jit(solution)/shard_map/ppermute | solution.py:431
  17.3 8.6 %collective-permute-start.3 = (f32[32,1664]{1,0:T(8,128)S(1)}, f32[32,1664]{1,0:T(8,128)S(1)}, u32[]{:S(2)}, u32[]{:S(2)}) collective-permute-start(f32[32,1664]{1,0:T(8,128)S(1)} %get-tuple-element.46), channel_id=1, source_target_pairs={{0,2},{2,0},{4,6},{6,4},{8,10},{10,8},{12,14},{14,12},{16,18},{18,... | collective-permute-start | bytes 638984 | tf_op jit(solution)/shard_map/ppermute | solution.py:431
  17.5 11.1 %collective-permute-start.5 = (f32[32,1664]{1,0:T(8,128)S(1)}, f32[32,1664]{1,0:T(8,128)S(1)}, u32[]{:S(2)}, u32[]{:S(2)}) collective-permute-start(f32[32,1664]{1,0:T(8,128)S(1)} %get-tuple-element.49), channel_id=1, source_target_pairs={{2,4},{4,2},{6,8},{8,6},{10,12},{12,10},{14,16},{16,14},{18,20},{2... | collective-permute-start | bytes 638984 | tf_op jit(solution)/shard_map/ppermute | solution.py:431
  20.9 5.0 %collective-permute-start.4 = (f32[2,8,1664]{2,1,0:T(8,128)S(1)}, f32[2,8,1664]{2,1,0:T(8,128)S(1)}, u32[]{:S(2)}, u32[]{:S(2)}) collective-permute-start(f32[2,8,1664]{2,1,0:T(8,128)S(1)} %get-tuple-element.47), channel_id=1, source_target_pairs={{0,1},{1,0},{2,3},{3,2},{4,5},{5,4},{6,7},{7,6},{8,9},{9,8},{10,11... | collective-permute-start | bytes 319496 | tf_op jit(solution)/shard_map/ppermute | solution.py:431

commit v5 on v4

--- a/solution.py
+++ b/solution.py
@@ -19,6 +19,7 @@
 
 LANES = 128
 SUBLANES = 8
+BLOCK = 512
 VMEM = pltpu.VMEM
 F32 = jnp.float32
 BF16 = jnp.bfloat16
@@ -52,11 +53,13 @@
     return jnp.where(low_side(parity, index) == 1, 1.0, -1.0).astype(F32)
 
 
-def first_kernel(dims, n_col, n_row, parity_ref, e_hbm, o_hbm, *refs):
+def first_kernel(dims, n_col, n_row, place_ref, e_hbm, o_hbm, *refs):
     rows, cols, bins, levels, fields = dims
     col_refs = refs[:n_col]
     row_refs = refs[n_col : n_col + n_row]
-    sems = refs[-1]
+    e_all, o_all = refs[n_col + n_row : n_col + n_row + 2]
+    sems, all_sems = refs[-2:]
+    parity_ref = lax.rem(place_ref[0], 2), lax.rem(place_ref[1], 2)
 
     def pieces(to_ref, e_from, o_from, slot):
         copies = [pltpu.make_async_copy(e_from, to_ref.at[..., 0:bins], sems.at[slot, 0])]
@@ -92,6 +95,14 @@
     for index in range(n_row):
         for copy in row(index):
             copy.start()
+    loads = [
+        pltpu.make_async_copy(o_hbm, o_all, all_sems.at[0]),
+        pltpu.make_async_copy(e_hbm, e_all, all_sems.at[1]),
+    ]
+    for copy in loads:
+        copy.start()
+    for copy in loads:
+        copy.wait()
     for index in range(n_col):
         for copy in column(index, 0):
             copy.wait()
@@ -123,13 +134,12 @@
     return slice(r * SUBLANES, (r + 1) * SUBLANES)
 
 
-def advect_all(dims, energy_at, arrived, flow_ref, mask_ref, courant_ref, adv_ref):
+def advect_all(dims, energy_at, flow_ref, mask_ref, courant_ref, adv_ref):
     rows, cols, bins, _, _ = dims
     ends = sublane_ends()
     tiles = cols // SUBLANES
 
     def body(k, _):
-        arrived(k)
         lanes = pl.ds(pl.multiple_of(k * LANES, LANES), LANES)
         speeds = [
             jnp.broadcast_to(courant_ref[way : way + 1, lanes], (SUBLANES, LANES))
@@ -204,20 +214,17 @@
 
 
 def window_kernel(dims, first, e_ref, o_ref, *refs):
-    rows, cols, bins, _, _ = dims
+    rows, cols, _, _, _ = dims
     tiles = cols // SUBLANES
     if first:
-        mask_t, owner_t, courant_ref, adv_ref, part_ref, grad_ref, flow_ref = refs[:7]
-        mask_ref, owner_ref, e_here, o_here, sems = refs[7:]
-
-        def e_copy(k):
-            lanes = pl.ds(pl.multiple_of(k * LANES, LANES), LANES)
-            return pltpu.make_async_copy(e_ref.at[..., lanes], e_here.at[k], sems.at[k])
-
-        o_copy = pltpu.make_async_copy(o_ref, o_here, sems.at[bins // LANES])
-        o_copy.start()
-        for k in range(bins // LANES):
-            e_copy(k).start()
+        mask_t, owner_t, courant_ref, m_hbm, w_hbm, adv_ref, part_ref, grad_ref, flow_ref = refs[:9]
+        mask_ref, owner_ref, m_ref, w_ref, sems = refs[9:]
+        copies = [
+            pltpu.make_async_copy(m_hbm, m_ref, sems.at[0]),
+            pltpu.make_async_copy(w_hbm, w_ref, sems.at[1]),
+        ]
+        for copy in copies:
+            copy.start()
         mask = mask_t[...].astype(F32)
         owner = owner_t[...]
         for i in range(tiles):
@@ -226,19 +233,17 @@
                     to_ref[i, span(r), :] = jnp.broadcast_to(
                         values[span(i), r : r + 1], (SUBLANES, LANES)
                     )
-        o_copy.wait()
     else:
         mask_ref, courant_ref, adv_ref, part_ref, grad_ref, flow_ref = refs
-
-    def arrived(k):
+        copies = []
+
+    def energy_at(k, i, r):
         if first:
-            e_copy(k).wait()
-
-    def energy_at(k, i, r):
-        return e_here[k, r, i] if first else e_ref[k, i, span(r), :]
+            return e_ref[r, i, :, pl.ds(pl.multiple_of(k * LANES, LANES), LANES)]
+        return e_ref[k, i, span(r), :]
 
     def ocean_at(q, i, r):
-        return o_here[q, r, i] if first else o_ref[q, i, span(r), :]
+        return o_ref[q, r, i] if first else o_ref[q, i, span(r), :]
 
     for way in range(2):
         for i in range(tiles):
@@ -247,10 +252,25 @@
                     current_gain * ocean_at(way, i, r)[:, 0:1], (SUBLANES, LANES)
                 )
     ocean_all(dims, ocean_at, mask_ref, part_ref, grad_ref)
-    advect_all(dims, energy_at, arrived, flow_ref, mask_ref, courant_ref, adv_ref)
-
-
-def fix_column(dims, parity, index, halo_ref, flow_ref, mask_ref, courant_ref, adv_ref):
+    advect_all(dims, energy_at, flow_ref, mask_ref, courant_ref, adv_ref)
+    for copy in copies:
+        copy.wait()
+
+
+def real(spot, index):
+    place, count = spot
+    if index == 0 and count % 2 == 0:
+        return None
+    low = low_side(lax.rem(place, 2), index)
+    partner = place + 1 - 2 * low
+    return jnp.logical_and(partner >= 0, partner < count)
+
+
+def kept(valid, value):
+    return value if valid is None else jnp.where(valid, value, 0.0)
+
+
+def fix_column(dims, parity, index, valid, halo_ref, flow_ref, mask_ref, courant_ref, adv_ref):
     tile, spots = column_place(dims, parity, index)
     sign = side_sign(parity, index)
     sea = mask_ref[tile, spots, :]
@@ -259,11 +279,11 @@
         lanes = slice(k * LANES, (k + 1) * LANES)
         inward = jnp.maximum(sign * (courant_ref[0:1, lanes] + speed), 0.0)
         adv_ref[k, tile, spots, :] = (
-            adv_ref[k, tile, spots, :] + sea * inward * halo_ref[:, lanes]
+            adv_ref[k, tile, spots, :] + sea * inward * kept(valid, halo_ref[:, lanes])
         )
 
 
-def fix_row(dims, parity, index, halo_ref, flow_ref, mask_ref, courant_ref, adv_ref):
+def fix_row(dims, parity, index, valid, halo_ref, flow_ref, mask_ref, courant_ref, adv_ref):
     spots = row_place(dims, parity, index)
     sign = side_sign(parity, index)
     for i in range(dims[1] // SUBLANES):
@@ -273,7 +293,7 @@
             lanes = slice(k * LANES, (k + 1) * LANES)
             inward = jnp.maximum(sign * (courant_ref[1:2, lanes] + speed), 0.0)
             adv_ref[k, i, spots, :] = (
-                adv_ref[k, i, spots, :] + sea * inward * halo_ref[i, :, lanes]
+                adv_ref[k, i, spots, :] + sea * inward * kept(valid, halo_ref[i, :, lanes])
             )
 
 
@@ -287,18 +307,20 @@
         out_ref[q, spots, :] = out_ref[q, spots, :] + sea * (gain * value)
 
 
-def source_of(dims, mats, tile, adv_ref, owner_ref, m_ref):
-    chunks = dims[2] // LANES
+def low_of(dims, mats, tile, adv_ref, owner_ref):
     owner = owner_ref[tile]
-    low = jnp.concatenate(
+    return jnp.concatenate(
         [
             jnp.where(owner == m, adv_ref[k, tile], 0.0).astype(BF16)
             for m in range(mats)
-            for k in range(chunks)
+            for k in range(dims[2] // LANES)
         ],
         axis=1,
     )
-    weights = jnp.concatenate([m_ref[m] for m in range(mats)], axis=1)
+
+
+def source_of(mats, low, m_ref, begin, end):
+    weights = jnp.concatenate([m_ref[m, begin:end, :] for m in range(mats)], axis=1)
     return lax.dot_general(low, weights, (((1,), (1,)), ((), ())), preferred_element_type=F32)
 
 
@@ -317,23 +339,23 @@
         grad = along * grad_ref[2 * (q - 2), tile] + across * grad_ref[2 * (q - 2) + 1, tile]
         out_ref[q] = part_ref[q, tile] - (0.5 * transport) * grad
     if col_border is not None:
-        index, halo_ref = col_border
+        index, valid, col_ref = col_border
         _, spots = column_place(dims, parity[0], index)
         ocean_border(
-            dims, side_sign(parity[0], index), 0, tile, spots, lambda lanes: halo_ref[:, lanes],
-            mask_ref, drift_ref, out_ref,
+            dims, side_sign(parity[0], index), 0, tile, spots,
+            lambda lanes: kept(valid, col_ref[:, lanes]), mask_ref, drift_ref, out_ref,
         )
-    for index, halo_ref in enumerate(row_borders):
+    for index, (valid, row_ref) in enumerate(row_borders):
         ocean_border(
             dims, side_sign(parity[1], index), 1, tile, row_place(dims, parity[1], index),
-            lambda lanes: halo_ref[tile, :, lanes], mask_ref, drift_ref, out_ref,
+            lambda lanes: kept(valid, row_ref[tile, :, lanes]), mask_ref, drift_ref, out_ref,
         )
 
 
-def step_kernel(dims, mats, late, last, n_col, n_row, *refs):
+def step_kernel(dims, mats, counts, late, last, n_col, n_row, *refs):
     rows, cols, bins, levels, fields = dims
     tiles = cols // SUBLANES
-    parity_ref, courant_ref, _, part_ref, grad_ref, flow_ref = refs[:6]
+    place_ref, courant_ref, _, part_ref, grad_ref, flow_ref = refs[:6]
     mask_ref, owner_ref, m_ref, w_ref = refs[6:10]
     refs = refs[10:]
     got_col, got_row, refs = refs[0], refs[1 : 1 + n_row], refs[1 + n_row :]
@@ -343,8 +365,10 @@
     if late and not last:
         col_refs, row_refs, refs = refs[:n_col], refs[n_col : n_col + n_row], refs[n_col + n_row :]
     low_ref, drift_ref, *refs = refs
-    parity = parity_ref[0], parity_ref[1]
+    parity = lax.rem(place_ref[0], 2), lax.rem(place_ref[1], 2)
     index = 1 if late else 0
+    col_valid = real((place_ref[0], counts[0]), index)
+    row_valid = [real((place_ref[1], counts[1]), i) for i in range(n_row)]
     walk = parity[0]
     todo = [walk * i + (1 - walk) * (tiles - 1 - i) for i in range(tiles)]
     copies = []
@@ -371,16 +395,22 @@
     fixed = (flow_ref, mask_ref, courant_ref, adv_ref)
     if not late:
         for row_index in range(n_row):
-            fix_row(dims, parity[1], row_index, got_row[row_index], *fixed)
-    fix_column(dims, parity[0], index, got_col, *fixed)
+            fix_row(
+                dims, parity[1], row_index, row_valid[row_index], got_row[row_index], *fixed
+            )
+    fix_column(dims, parity[0], index, col_valid, got_col, *fixed)
     for number, tile in enumerate(todo):
         if late != (number == tiles - 1):
             continue
-        source = source_of(dims, mats, tile, adv_ref, owner_ref, m_ref)
+        low = low_of(dims, mats, tile, adv_ref, owner_ref)
         sea = mask_ref[tile]
         for k in range(bins // LANES):
             lanes = slice(k * LANES, (k + 1) * LANES)
-            energy = sea * (adv_ref[k, tile] + source_gain * source[:, lanes])
+            begin = k * LANES // BLOCK * BLOCK
+            if k * LANES == begin:
+                source = source_of(mats, low, m_ref, begin, min(begin + BLOCK, bins))
+            gain = source[:, k * LANES - begin : (k + 1) * LANES - begin]
+            energy = sea * (adv_ref[k, tile] + source_gain * gain)
             if not last:
                 e_out[k, tile] = energy
             elif late:
@@ -397,7 +427,8 @@
         else:
             out_ref = o_out.at[number]
         ocean_tile(
-            dims, tile, (index, got_col) if late or number == 0 else None, got_row, parity,
+            dims, tile, (index, col_valid, got_col) if late or number == 0 else None,
+            list(zip(row_valid, got_row)), parity,
             part_ref, grad_ref, mask_ref, w_ref, low_ref, drift_ref, out_ref,
         )
     if late and last:
@@ -421,14 +452,25 @@
             pack(to_ref, lambda ref: ref[:, spots, :])
 
 
-def swap_pairs(values, axis):
-    count = lax.axis_size(axis)
+def swap_pairs(values, axis, other):
+    size = {name: lax.axis_size(name) for name in (axis, other)}
+    names = ("grp", "tile")
+
+    def device(along, across):
+        spot = {axis: along, other: across}
+        return spot[names[0]] * lax.axis_size(names[1]) + spot[names[1]]
+
     got = []
     for index, value in enumerate(values):
         pairs = []
-        for i in range(index, count - 1, 2):
-            pairs += [(i, i + 1), (i + 1, i)]
-        got.append(lax.ppermute(value, axis, pairs))
+        for i in range(size[axis]):
+            partner = i + 1 if (i - index) % 2 == 0 else i - 1
+            for j in range(size[other]):
+                if 0 <= partner < size[axis]:
+                    pairs.append((device(i, j), device(partner, j)))
+                elif j ^ 1 < size[other]:
+                    pairs.append((device(i, j), device(i, j ^ 1)))
+        got.append(lax.ppermute(value, names, pairs))
     return got
 
 
@@ -438,7 +480,6 @@
     mats = matrices.shape[2]
     tiles = cols // SUBLANES
     chunks = bins // LANES
-    points_count = rows * cols
     dims = (rows, cols, bins, levels, fields)
     n_col = 2
     n_row = 2 if lax.axis_size("tile") > 2 else 1
@@ -447,7 +488,8 @@
     m0 = matrices.reshape(mats, bins, bins)
     mask_t = land_mask.T
     owner_t = ownership.T
-    parity = jnp.stack([lax.axis_index("grp") % 2, lax.axis_index("tile") % 2]).astype(jnp.int32)
+    place = jnp.stack([lax.axis_index("grp"), lax.axis_index("tile")])
+    counts = lax.axis_size("grp"), lax.axis_size("tile")
 
     vmem = pl.BlockSpec(memory_space=VMEM)
     smem = pl.BlockSpec(memory_space=pltpu.SMEM)
@@ -462,43 +504,42 @@
     wide = bins + fields * levels
     borders = [VMEM((rows, wide), F32)] * n_col + [VMEM((tiles, SUBLANES, wide), F32)] * n_row
     dma = pltpu.SemaphoreType.DMA
-    moved = 4 * points_count * (chunks * LANES + fields * levels)
-    cost = pl.CostEstimate(flops=0, transcendentals=0, bytes_accessed=4 * moved)
 
     def params(mib):
         return pltpu.CompilerParams(vmem_limit_bytes=mib * 2**20)
 
     def exchange(sent):
-        return swap_pairs(sent[:n_col], "grp") + swap_pairs(sent[n_col:], "tile")
+        return swap_pairs(sent[:n_col], "grp", "tile") + swap_pairs(sent[n_col:], "tile", "grp")
 
     sent = pl.pallas_call(
         functools.partial(first_kernel, dims, n_col, n_row),
-        out_shape=borders,
+        out_shape=borders + [VMEM(e0.shape, F32), VMEM(o0.shape, F32)],
         in_specs=[smem, hbm, hbm],
-        out_specs=[vmem] * len(borders),
-        scratch_shapes=[dma((n_col + n_row, 1 + fields))],
+        out_specs=[vmem] * (len(borders) + 2),
+        scratch_shapes=[dma((n_col + n_row, 1 + fields)), dma((2,))],
         compiler_params=params(8),
-        cost_estimate=cost,
         name="first",
-    )(parity, in_hbm(e0), in_hbm(o0))
-    e = o = None
+    )(place, in_hbm(e0), in_hbm(o0))
+    e, o = sent[-2:]
+    sent = sent[:-2]
     for step in range(STEPS):
         got = exchange(sent)
         if step == 0:
-            adv, part, grad, flow, mask, owner = pl.pallas_call(
+            adv, part, grad, flow, mask, owner, m, w = pl.pallas_call(
                 functools.partial(window_kernel, dims, True),
-                out_shape=window_shapes + [points(()), points((), LANES, jnp.int32)],
-                in_specs=[hbm] * 2 + [vmem] * 3,
-                out_specs=[vmem] * 6,
-                scratch_shapes=[
-                    VMEM((chunks, rows, tiles, SUBLANES, LANES), F32),
-                    VMEM((fields, rows, tiles, SUBLANES, levels), F32),
-                    dma((chunks + 1,)),
+                out_shape=window_shapes
+                + [
+                    points(()),
+                    points((), LANES, jnp.int32),
+                    VMEM(m0.shape, BF16),
+                    VMEM(stokes_weight.shape, BF16),
                 ],
-                compiler_params=params(12),
-                cost_estimate=cost,
+                in_specs=[vmem] * 5 + [hbm] * 2,
+                out_specs=[vmem] * 8,
+                scratch_shapes=[dma((2,))],
+                compiler_params=params(8),
                 name="window_first",
-            )(in_hbm(e0), in_hbm(o0), mask_t, owner_t, courant)
+            )(e, o, mask_t, owner_t, courant, in_hbm(m0), in_hbm(stokes_weight))
         else:
             adv, part, grad, flow = pl.pallas_call(
                 functools.partial(window_kernel, dims, False),
@@ -506,7 +547,6 @@
                 in_specs=[vmem] * 4,
                 out_specs=[vmem] * 4,
                 compiler_params=params(8),
-                cost_estimate=cost,
                 name="window",
             )(e, o, mask, courant)
         last = step == STEPS - 1
@@ -518,9 +558,9 @@
             ]
         else:
             early_shape = [adv_shape, o_shape]
-        common = (mask, owner, m0, stokes_weight)
+        common = (mask, owner, m, w)
         adv, e, o = pl.pallas_call(
-            functools.partial(step_kernel, dims, mats, False, last, n_col, n_row),
+            functools.partial(step_kernel, dims, mats, counts, False, last, n_col, n_row),
             out_shape=[adv_shape] + early_shape,
             in_specs=[smem] + [vmem] * (10 + n_row),
             out_specs=[vmem] * 3,
@@ -528,7 +568,7 @@
             input_output_aliases={2: 0},
             compiler_params=params(24),
             name="early_last" if last else "early",
-        )(parity, courant, adv, part, grad, flow, *common, got[0], *got[n_col:])
+        )(place, courant, adv, part, grad, flow, *common, got[0], *got[n_col:])
         e_at = 11 + n_row
         aliases = {2: 0}
         if last:
@@ -544,7 +584,7 @@
             late_specs = [vmem] * (1 + len(late_shape))
             aliases.update({e_at: 1, e_at + 1: 2})
         _, e, o, *sent = pl.pallas_call(
-            functools.partial(step_kernel, dims, mats, True, last, n_col, n_row),
+            functools.partial(step_kernel, dims, mats, counts, True, last, n_col, n_row),
             out_shape=[adv_shape] + late_shape,
             in_specs=[smem] + [vmem] * (12 + n_row),
             out_specs=late_specs,
@@ -552,7 +592,7 @@
             input_output_aliases=aliases,
             compiler_params=params(24),
             name="late_last" if last else "late",
-        )(parity, courant, adv, part, grad, flow, *common, got[1], *got[n_col:], e, o)
+        )(place, courant, adv, part, grad, flow, *common, got[1], *got[n_col:], e, o)
     energy = jnp.transpose(e.reshape(rows, cols, bins), (2, 0, 1))
     return energy, o.reshape(ocean.shape)
 

time: 33 us -> 33.9 us (1.027)
  the two profiles are of different devices: /device:TPU:19 before, /device:TPU:0 now
where the time goes in v5:
time: 33.9 us; the launch traced here: 33.7 us
  Pallas kernels  20.6 us (61%)
  waiting for transfers between devices  6.9 us (20%)
  starting transfers between devices  5.44 us (16%)
  between operations  0.73 us (2%)
    pallas_call x2, Pallas kernels, local(): pl.pallas_call(functools.partial(step_kernel, dims, mats, counts, True, l...  7.19 us
    ppermute x6, waiting for transfers between devices, swap_pairs(): got.append(lax.ppermute(value, names, pairs))  6.9 us
    ppermute x6, starting transfers between devices, swap_pairs(): got.append(lax.ppermute(value, names, pairs))  5.44 us
    pallas_call x2, Pallas kernels, local(): pl.pallas_call(functools.partial(step_kernel, dims, mats, counts, False,...  5.4 us
    pallas_call x1, Pallas kernels, local(): pl.pallas_call(functools.partial(first_kernel, dims, n_col, n_row), out_s...  3.08 us
    pallas_call x1, Pallas kernels, local(): pl.pallas_call(functools.partial(window_kernel, dims, True), out_shape=wi...  2.66 us
    pallas_call x1, Pallas kernels, local(): pl.pallas_call(functools.partial(window_kernel, dims, False), out_shape=w...  2.23 us
  transfers between devices with their start and end apart: 6, of which 2 were waited for; matrix products, arithmetic and copies ran while one was open for 0% of the time, Pallas kernels for 31%

profile of v5, /device:TPU:0, one launch (start us, length us, event | category | flops | bytes accessed | tf_op | source)
XLA Modules:
  0.0 33.7 jit_solution(3365648696822065991)
XLA Ops:
  0.6 0.0 copy-start
  0.6 0.0 copy-start.1
  0.7 0.0 copy-start.2
  0.7 0.1 pad_add_fusion.place_ref.refs_0_
  0.7 3.1 %first.1 = (f32[32,1664]{1,0:T(8,128)S(1)}, f32[32,1664]{1,0:T(8,128)S(1)}, f32[2,8,1664]{2,1,0:T(8,128)S(1)}, f32[32,2,8,1152]{3,2,1,0:T(8,128)S(1)}, f32[4,32,2,8,128]{4,3,2,1,0:T(8,128)S(1)}) custom-call(s32[2]{0:T(128)S(1)} %pad_add_fusion.place_ref.refs_0_, f32[32,2,8,1152]{3,2,1,0:T(8,128)} %bitcast.16, f32[4,32,2,8,128]{4,3,2,1,0:T(8,128)} %bitcast.17), custom_call_target="tpu_custom_call" | custom-call | tf_op jit(solution)/shard_map/first/pallas_call | solution.py:514
  3.8 0.6 %collective-permute-start = (f32[32,1664]{1,0:T(8,128)S(1)}, f32[32,1664]{1,0:T(8,128)S(1)}, u32[]{:S(2)}, u32[]{:S(2)}) collective-permute-start(f32[32,1664]{1,0:T(8,128)S(1)} %get-tuple-element.42), channel_id=1, source_target_pairs={{0,2},{1,3},{2,0},{3,1},{4,6},{5,7},{6,4},{7,5},{8,10},{9,11},{10,... | collective-permute-start | bytes 638984 | tf_op jit(solution)/shard_map/ppermute | solution.py:473
  4.4 2.5 %collective-permute-start.2 = (f32[32,1664]{1,0:T(8,128)S(1)}, f32[32,1664]{1,0:T(8,128)S(1)}, u32[]{:S(2)}, u32[]{:S(2)}) collective-permute-start(f32[32,1664]{1,0:T(8,128)S(1)} %get-tuple-element.45), channel_id=1, source_target_pairs={{0,1},{1,0},{2,4},{3,5},{4,2},{5,3},{6,8},{7,9},{8,6},{9,7},{10,12... | collective-permute-start | bytes 638984 | tf_op jit(solution)/shard_map/ppermute | solution.py:473
  7.0 0.1 collective-permute-start.1
  7.0 0.0 copy-done
  7.0 0.0 copy-done.1
  7.0 0.0 copy-done.2
  7.1 2.7 %window_first.1 = (f32[9,2,256,128]{3,2,1,0:T(8,128)S(1)}, f32[4,2,256,128]{3,2,1,0:T(8,128)S(1)}, f32[4,2,256,128]{3,2,1,0:T(8,128)S(1)}, f32[2,2,256,128]{3,2,...) custom-call(f32[32,2,8,1152]{3,2,1,0:T(8,128)S(1)} %get-tuple-elemen, ...), custom_call_target="tpu_custom_call" | custom-call | tf_op jit(solution)/shard_map/window_first/pallas_call | solution.py:528
  9.7 3.4 %collective-permute-done.1.refs_11_ = f32[2,8,1664]{2,1,0:T(8,128)S(1)} collective-permute-done((f32[2,8,1664]{2,1,0:T(8,128)S(1)}, f32[2,8,1664]{2,1,0:T(8,128)S(1)}, u32[]{:S(2)}, u32[]{:S(2)}) %collective-permute-start.1) | collective-permute-done | bytes 106528 | tf_op jit(solution)/shard_map/ppermute | solution.py:473
  13.1 0.0 collective-permute-done.refs_10_
  13.1 2.7 %early.1 = (f32[9,2,256,128]{3,2,1,0:T(8,128)S(1)}, f32[9,2,256,128]{3,2,1,0:T(8,128)S(1)}, f32[4,2,256,128]{3,2,1,0:T(8,128)S(1)}) custom-call(s32[2]{0:T(128)S(1)} %pad_add_fusion.place_ref.refs_0_, f32[2,1152]{1,0:T(2,128)S(1)} %copy-done, f32[9,2,256,128]{3,2,1,0:T(8,128)S(1)} %get-tuple-element.34.refs_2_, ...), custom_call_target="tpu_custom_call", output_to_operand_aliasing={{0}: (2, {})} | custom-call | tf_op jit(solution)/shard_map/early/pallas_call | solution.py:562
  15.8 0.0 collective-permute-done.2.refs_10_
  15.8 2.8 %late.1 = (f32[9,2,256,128]{3,2,1,0:T(8,128)S(1)}, f32[9,2,256,128]{3,2,1,0:T(8,128)S(1)}, f32[4,2,256,128]{3,2,1,0:T(8,128)S(1)}, f32[32,1664]{1,0:T(8,128)S(1)...) custom-call(s32[2]{0:T(128)S(1)} %pad_add_fusion.place_ref.refs_0_, ...), custom_call_target="tpu_custom_call", output_to_operand_aliasing={{0}: (2, {}), {1}: (12, {}), {2}: (13, {})} | custom-call | tf_op jit(solution)/shard_map/late/pallas_call | solution.py:586
  18.6 0.1 collective-permute-start.3
  18.7 2.1 %collective-permute-start.5 = (f32[32,1664]{1,0:T(8,128)S(1)}, f32[32,1664]{1,0:T(8,128)S(1)}, u32[]{:S(2)}, u32[]{:S(2)}) collective-permute-start(f32[32,1664]{1,0:T(8,128)S(1)} %get-tuple-element.57), channel_id=1, source_target_pairs={{0,1},{1,0},{2,4},{3,5},{4,2},{5,3},{6,8},{7,9},{8,6},{9,7},{10,12... | collective-permute-start | bytes 638984 | tf_op jit(solution)/shard_map/ppermute | solution.py:473
  20.7 0.1 collective-permute-start.4
  20.8 2.2 %window.1 = (f32[9,2,256,128]{3,2,1,0:T(8,128)S(1)}, f32[4,2,256,128]{3,2,1,0:T(8,128)S(1)}, f32[4,2,256,128]{3,2,1,0:T(8,128)S(1)}, f32[2,2,256,128]{3,2,1,0:T(8,128)S(1)}) custom-call(f32[9,2,256,128]{3,2,1,0:T(8,128)S(1)} %get-tuple-element.48.e_ref, f32[4,2,256,128]{3,2,1,0:T(8,128)S(1)} %get-tuple-element.49.o_ref, ...), custom_call_target="tpu_custom_call" | custom-call | tf_op jit(solution)/shard_map/window/pallas_call | solution.py:544
  23.1 3.5 %collective-permute-done.4.refs_11_ = f32[2,8,1664]{2,1,0:T(8,128)S(1)} collective-permute-done((f32[2,8,1664]{2,1,0:T(8,128)S(1)}, f32[2,8,1664]{2,1,0:T(8,128)S(1)}, u32[]{:S(2)}, u32[]{:S(2)}) %collective-permute-start.4) | collective-permute-done | bytes 106528 | tf_op jit(solution)/shard_map/ppermute | solution.py:473
  26.6 0.0 collective-permute-done.3.refs_10_
  26.6 2.7 %early_last.1 = (f32[9,2,256,128]{3,2,1,0:T(8,128)S(1)}, f32[1,32,8,1152]{3,2,1,0:T(8,128)S(1)}, f32[1,4,256,128]{3,2,1,0:T(8,128)S(1)}) custom-call(s32[2]{0:T(128)S(1)} %pad_add_fusion.place_ref.refs_0_, f32[2,1152]{1,0:T(2,128)S(1)} %copy-done, f32[9,2,256,128]{3,2,1,0:T(8,128)S(1)} %get-tuple-element.50.refs_2_, ...), custom_call_target="tpu_custom_call", output_to_operand_aliasing={{0}: (2, {})} | custom-call | tf_op jit(solution)/shard_map/early_last/pallas_call | solution.py:562
  29.3 0.0 collective-permute-done.5.refs_10_
  29.3 4.4 %late_last.1 = (f32[9,2,256,128]{3,2,1,0:T(8,128)S(1)}, f32[32,2,8,1152]{3,2,1,0:T(8,128)}, f32[4,32,2,8,128]{4,3,2,1,0:T(8,128)}) custom-call(s32[2]{0:T(128)S(1)} %pad_add_fusion.place_ref.refs_0_, f32[2,1152]{1,0:T(2,128)S(1)} %copy-done, f32[9,2,256,128]{3,2,1,0:T(8,128)S(1)} %get-tuple-element.56.refs_2_, ...), custom_call_target="tpu_custom_call", output_to_operand_aliasing={{0}: (2, {})} | custom-call | tf_op jit(solution)/shard_map/late_last/pallas_call | solution.py:586
Async XLA Ops:
  0.6 6.4 %copy-start = (f32[2,1152]{1,0:T(2,128)S(1)}, f32[2,1152]{1,0:T(2,128)}, u32[]{:S(2)}) copy-start(f32[2,1152]{1,0:T(2,128)} %refs_1_.9) | copy-start | bytes 27652
  0.6 6.4 %copy-start.1 = (s32[32,16]{0,1:T(8,128)S(1)}, s32[32,16]{0,1:T(8,128)}, u32[]{:S(2)}) copy-start(s32[32,16]{0,1:T(8,128)} %param.10) | copy-start | bytes 6148
  0.7 6.4 %copy-start.2 = (s32[32,16]{0,1:T(8,128)S(1)}, s32[32,16]{0,1:T(8,128)}, u32[]{:S(2)}) copy-start(s32[32,16]{0,1:T(8,128)} %param.9) | copy-start | bytes 6148
  3.8 9.2 %collective-permute-start = (f32[32,1664]{1,0:T(8,128)S(1)}, f32[32,1664]{1,0:T(8,128)S(1)}, u32[]{:S(2)}, u32[]{:S(2)}) collective-permute-start(f32[32,1664]{1,0:T(8,128)S(1)} %get-tuple-element.42), channel_id=1, source_target_pairs={{0,2},{1,3},{2,0},{3,1},{4,6},{5,7},{6,4},{7,5},{8,10},{9,11},{10,... | collective-permute-start | bytes 638984 | tf_op jit(solution)/shard_map/ppermute | solution.py:473
  4.4 11.4 %collective-permute-start.2 = (f32[32,1664]{1,0:T(8,128)S(1)}, f32[32,1664]{1,0:T(8,128)S(1)}, u32[]{:S(2)}, u32[]{:S(2)}) collective-permute-start(f32[32,1664]{1,0:T(8,128)S(1)} %get-tuple-element.45), channel_id=1, source_target_pairs={{0,1},{1,0},{2,4},{3,5},{4,2},{5,3},{6,8},{7,9},{8,6},{9,7},{10,12... | collective-permute-start | bytes 638984 | tf_op jit(solution)/shard_map/ppermute | solution.py:473
  7.0 6.1 %collective-permute-start.1 = (f32[2,8,1664]{2,1,0:T(8,128)S(1)}, f32[2,8,1664]{2,1,0:T(8,128)S(1)}, u32[]{:S(2)}, u32[]{:S(2)}) collective-permute-start(f32[2,8,1664]{2,1,0:T(8,128)S(1)} %get-tuple-element.43), channel_id=1, source_target_pairs={{0,1},{2,3},{4,5},{6,7},{8,9},{10,11},{12,13},{14,15},{16,17},{18,... | collective-permute-start | bytes 319496 | tf_op jit(solution)/shard_map/ppermute | solution.py:473
  18.6 8.0 %collective-permute-start.3 = (f32[32,1664]{1,0:T(8,128)S(1)}, f32[32,1664]{1,0:T(8,128)S(1)}, u32[]{:S(2)}, u32[]{:S(2)}) collective-permute-start(f32[32,1664]{1,0:T(8,128)S(1)} %get-tuple-element.54), channel_id=1, source_target_pairs={{0,2},{1,3},{2,0},{3,1},{4,6},{5,7},{6,4},{7,5},{8,10},{9,11},{10,... | collective-permute-start | bytes 638984 | tf_op jit(solution)/shard_map/ppermute | solution.py:473
  18.7 10.6 %collective-permute-start.5 = (f32[32,1664]{1,0:T(8,128)S(1)}, f32[32,1664]{1,0:T(8,128)S(1)}, u32[]{:S(2)}, u32[]{:S(2)}) collective-permute-start(f32[32,1664]{1,0:T(8,128)S(1)} %get-tuple-element.57), channel_id=1, source_target_pairs={{0,1},{1,0},{2,4},{3,5},{4,2},{5,3},{6,8},{7,9},{8,6},{9,7},{10,12... | collective-permute-start | bytes 638984 | tf_op jit(solution)/shard_map/ppermute | solution.py:473
  20.7 5.8 %collective-permute-start.4 = (f32[2,8,1664]{2,1,0:T(8,128)S(1)}, f32[2,8,1664]{2,1,0:T(8,128)S(1)}, u32[]{:S(2)}, u32[]{:S(2)}) collective-permute-start(f32[2,8,1664]{2,1,0:T(8,128)S(1)} %get-tuple-element.55), channel_id=1, source_target_pairs={{0,1},{2,3},{4,5},{6,7},{8,9},{10,11},{12,13},{14,15},{16,17},{18,... | collective-permute-start | bytes 319496 | tf_op jit(solution)/shard_map/ppermute | solution.py:473

commit v6 on v5

--- a/solution.py
+++ b/solution.py
@@ -53,62 +53,44 @@
     return jnp.where(low_side(parity, index) == 1, 1.0, -1.0).astype(F32)
 
 
-def first_kernel(dims, n_col, n_row, place_ref, e_hbm, o_hbm, *refs):
+def spot():
+    return lax.axis_index("grp"), lax.axis_index("tile")
+
+
+def parities():
+    return tuple(lax.rem(i, 2) for i in spot())
+
+
+def first_kernel(dims, n_col, n_row, e_hbm, o_hbm, *refs):
     rows, cols, bins, levels, fields = dims
+    chunks = bins // LANES
     col_refs = refs[:n_col]
     row_refs = refs[n_col : n_col + n_row]
-    e_all, o_all = refs[n_col + n_row : n_col + n_row + 2]
-    sems, all_sems = refs[-2:]
-    parity_ref = lax.rem(place_ref[0], 2), lax.rem(place_ref[1], 2)
-
-    def pieces(to_ref, e_from, o_from, slot):
-        copies = [pltpu.make_async_copy(e_from, to_ref.at[..., 0:bins], sems.at[slot, 0])]
-        for q in range(fields):
-            lanes = pl.ds(bins + q * levels, levels)
-            copies.append(
-                pltpu.make_async_copy(o_from(q), to_ref.at[..., lanes], sems.at[slot, 1 + q])
-            )
-        return copies
-
-    def column(index, high):
-        tile = high * (cols // SUBLANES - 1)
-        place = high * (SUBLANES - 1)
-        return pieces(
-            col_refs[index],
-            e_hbm.at[:, tile, place, :],
-            lambda q: o_hbm.at[q, :, tile, place, :],
-            index,
-        )
-
-    def row(index):
-        r = (1 - low_side(parity_ref[1], index)) * (rows - 1)
-        return pieces(row_refs[index], e_hbm.at[r], lambda q: o_hbm.at[q, r], n_col + index)
-
-    for odd in range(2):
-
-        @pl.when(parity_ref[0] == odd)
-        def _(odd=odd):
-            for index in reversed(range(n_col)):
-                for copy in column(index, 1 - low_side(odd, index)):
-                    copy.start()
-
-    for index in range(n_row):
-        for copy in row(index):
-            copy.start()
+    e_ref, o_ref, sems = refs[n_col + n_row :]
     loads = [
-        pltpu.make_async_copy(o_hbm, o_all, all_sems.at[0]),
-        pltpu.make_async_copy(e_hbm, e_all, all_sems.at[1]),
+        pltpu.make_async_copy(e_hbm.at[:, pl.ds(k * LANES, LANES)], e_ref.at[k], sems.at[k])
+        for k in range(chunks)
     ]
+    loads.append(pltpu.make_async_copy(o_hbm, o_ref, sems.at[chunks]))
     for copy in loads:
         copy.start()
-    for copy in loads:
-        copy.wait()
-    for index in range(n_col):
-        for copy in column(index, 0):
-            copy.wait()
-    for index in range(n_row):
-        for copy in row(index):
-            copy.wait()
+    parity = parities()
+
+    def pack(lanes, ref):
+        for i, to_ref in enumerate(col_refs):
+            high = 1 - low_side(parity[0], i)
+            to_ref[:, lanes] = ref[pl.ds(high * (cols - 1), rows, stride=cols), :]
+        for i, to_ref in enumerate(row_refs):
+            high = 1 - low_side(parity[1], i)
+            begin = pl.multiple_of(high * (rows - 1) * cols, cols)
+            to_ref[:, :, lanes] = ref[pl.ds(begin, cols), :].reshape(-1, SUBLANES, LANES)
+
+    for k in range(chunks):
+        loads[k].wait()
+        pack(slice(k * LANES, (k + 1) * LANES), e_ref.at[k])
+    loads[chunks].wait()
+    for q in range(fields):
+        pack(slice(bins + q * levels, bins + (q + 1) * levels), o_ref.at[q])
 
 
 def shifted(parts, axis_ids, ahead):
@@ -238,12 +220,10 @@
         copies = []
 
     def energy_at(k, i, r):
-        if first:
-            return e_ref[r, i, :, pl.ds(pl.multiple_of(k * LANES, LANES), LANES)]
-        return e_ref[k, i, span(r), :]
+        return e_ref[k, span(r * tiles + i), :] if first else e_ref[k, i, span(r), :]
 
     def ocean_at(q, i, r):
-        return o_ref[q, r, i] if first else o_ref[q, i, span(r), :]
+        return o_ref[q, span(r * tiles + i), :] if first else o_ref[q, i, span(r), :]
 
     for way in range(2):
         for i in range(tiles):
@@ -355,9 +335,9 @@
 def step_kernel(dims, mats, counts, late, last, n_col, n_row, *refs):
     rows, cols, bins, levels, fields = dims
     tiles = cols // SUBLANES
-    place_ref, courant_ref, _, part_ref, grad_ref, flow_ref = refs[:6]
-    mask_ref, owner_ref, m_ref, w_ref = refs[6:10]
-    refs = refs[10:]
+    courant_ref, _, part_ref, grad_ref, flow_ref = refs[:5]
+    mask_ref, owner_ref, m_ref, w_ref = refs[5:9]
+    refs = refs[9:]
     got_col, got_row, refs = refs[0], refs[1 : 1 + n_row], refs[1 + n_row :]
     if late:
         e_early, o_early, *refs = refs
@@ -365,10 +345,10 @@
     if late and not last:
         col_refs, row_refs, refs = refs[:n_col], refs[n_col : n_col + n_row], refs[n_col + n_row :]
     low_ref, drift_ref, *refs = refs
-    parity = lax.rem(place_ref[0], 2), lax.rem(place_ref[1], 2)
+    here, parity = spot(), parities()
     index = 1 if late else 0
-    col_valid = real((place_ref[0], counts[0]), index)
-    row_valid = [real((place_ref[1], counts[1]), i) for i in range(n_row)]
+    col_valid = real((here[0], counts[0]), index)
+    row_valid = [real((here[1], counts[1]), i) for i in range(n_row)]
     walk = parity[0]
     todo = [walk * i + (1 - walk) * (tiles - 1 - i) for i in range(tiles)]
     copies = []
@@ -377,13 +357,22 @@
 
         def store(number, e_from, o_from):
             tile = todo[number]
-            made = [pltpu.make_async_copy(e_from, e_out.at[:, tile], sems.at[number, 0])]
+            made = []
+            for begin in range(0, bins, BLOCK):
+                lanes = pl.ds(begin, min(BLOCK, bins - begin))
+                made.append(
+                    pltpu.make_async_copy(
+                        e_from.at[:, :, lanes],
+                        e_out.at[:, tile, :, lanes],
+                        sems.at[number, fields + begin // BLOCK],
+                    )
+                )
             for q in range(fields):
                 made.append(
                     pltpu.make_async_copy(
                         o_from.at[q].reshape(rows, SUBLANES, levels),
                         o_out.at[q, :, tile],
-                        sems.at[number, 1 + q],
+                        sems.at[number, q],
                     )
                 )
             return made
@@ -404,6 +393,7 @@
             continue
         low = low_of(dims, mats, tile, adv_ref, owner_ref)
         sea = mask_ref[tile]
+        own_copies = store(number, e_tile, o_tile) if late and last else None
         for k in range(bins // LANES):
             lanes = slice(k * LANES, (k + 1) * LANES)
             begin = k * LANES // BLOCK * BLOCK
@@ -418,12 +408,12 @@
             else:
                 e_out[number, :, :, lanes] = energy.reshape(rows, SUBLANES, LANES)
             low_ref[:, lanes] = energy.astype(BF16)
+            if own_copies and (k + 1) * LANES in (begin + BLOCK, bins):
+                own_copies[begin // BLOCK].start()
         if not last:
             out_ref = o_out.at[:, tile]
         elif late:
             out_ref = o_tile
-            e_copy, *o_copies = store(number, e_tile, o_tile)
-            e_copy.start()
         else:
             out_ref = o_out.at[number]
         ocean_tile(
@@ -432,9 +422,9 @@
             part_ref, grad_ref, mask_ref, w_ref, low_ref, drift_ref, out_ref,
         )
     if late and last:
-        for copy in o_copies:
+        for copy in own_copies[-fields:]:
             copy.start()
-        for copy in copies + [e_copy] + o_copies:
+        for copy in copies + own_copies:
             copy.wait()
     elif late:
 
@@ -488,11 +478,9 @@
     m0 = matrices.reshape(mats, bins, bins)
     mask_t = land_mask.T
     owner_t = ownership.T
-    place = jnp.stack([lax.axis_index("grp"), lax.axis_index("tile")])
     counts = lax.axis_size("grp"), lax.axis_size("tile")
 
     vmem = pl.BlockSpec(memory_space=VMEM)
-    smem = pl.BlockSpec(memory_space=pltpu.SMEM)
     hbm = pl.BlockSpec(memory_space=pltpu.HBM)
 
     def points(lead, width=LANES, dtype=F32):
@@ -513,13 +501,14 @@
 
     sent = pl.pallas_call(
         functools.partial(first_kernel, dims, n_col, n_row),
-        out_shape=borders + [VMEM(e0.shape, F32), VMEM(o0.shape, F32)],
-        in_specs=[smem, hbm, hbm],
+        out_shape=borders
+        + [VMEM((chunks, rows * cols, LANES), F32), VMEM((fields, rows * cols, levels), F32)],
+        in_specs=[hbm, hbm],
         out_specs=[vmem] * (len(borders) + 2),
-        scratch_shapes=[dma((n_col + n_row, 1 + fields)), dma((2,))],
+        scratch_shapes=[dma((chunks + 1,))],
         compiler_params=params(8),
         name="first",
-    )(place, in_hbm(e0), in_hbm(o0))
+    )(in_hbm(e0.reshape(-1, bins)), in_hbm(o0.reshape(fields, -1, levels)))
     e, o = sent[-2:]
     sent = sent[:-2]
     for step in range(STEPS):
@@ -562,22 +551,22 @@
         adv, e, o = pl.pallas_call(
             functools.partial(step_kernel, dims, mats, counts, False, last, n_col, n_row),
             out_shape=[adv_shape] + early_shape,
-            in_specs=[smem] + [vmem] * (10 + n_row),
+            in_specs=[vmem] * (10 + n_row),
             out_specs=[vmem] * 3,
             scratch_shapes=scratch,
-            input_output_aliases={2: 0},
+            input_output_aliases={1: 0},
             compiler_params=params(24),
             name="early_last" if last else "early",
-        )(place, courant, adv, part, grad, flow, *common, got[0], *got[n_col:])
-        e_at = 11 + n_row
-        aliases = {2: 0}
+        )(courant, adv, part, grad, flow, *common, got[0], *got[n_col:])
+        e_at = 10 + n_row
+        aliases = {1: 0}
         if last:
             late_shape = [pltpu.HBM(e0.shape, F32), pltpu.HBM(o0.shape, F32)]
             late_specs = [vmem, hbm, hbm]
             scratch += [
                 VMEM((rows, SUBLANES, bins), F32),
                 VMEM((fields, rows * SUBLANES, levels), F32),
-                dma((tiles, 1 + fields)),
+                dma((tiles, fields + pl.cdiv(bins, BLOCK))),
             ]
         else:
             late_shape = early_shape + borders
@@ -586,13 +575,13 @@
         _, e, o, *sent = pl.pallas_call(
             functools.partial(step_kernel, dims, mats, counts, True, last, n_col, n_row),
             out_shape=[adv_shape] + late_shape,
-            in_specs=[smem] + [vmem] * (12 + n_row),
+            in_specs=[vmem] * (12 + n_row),
             out_specs=late_specs,
             scratch_shapes=scratch,
             input_output_aliases=aliases,
             compiler_params=params(24),
             name="late_last" if last else "late",
-        )(place, courant, adv, part, grad, flow, *common, got[1], *got[n_col:], e, o)
+        )(courant, adv, part, grad, flow, *common, got[1], *got[n_col:], e, o)
     energy = jnp.transpose(e.reshape(rows, cols, bins), (2, 0, 1))
     return energy, o.reshape(ocean.shape)
 

time: 33.9 us -> 30 us (0.88)
  Pallas kernels: 20.6 us -> 16.9 us
    pallas_call x2, Pallas kernels: 7.19 us -> 5.4 us  [local(): pl.pallas_call(functools.partial(step_kernel, dims, mats, counts, True, l...]
    pallas_call x2, Pallas kernels: 5.4 us -> 4.39 us  [local(): pl.pallas_call(functools.partial(step_kernel, dims, mats, counts, False,...]
    pallas_call x1, Pallas kernels: 3.08 us -> 2.16 us  [local(): pl.pallas_call(functools.partial(first_kernel, dims, n_col, n_row), out_s...]
where the time goes in v6:
time: 30 us; the launch traced here: 29.9 us
  Pallas kernels  16.9 us (56%)
  waiting for transfers between devices  6.87 us (23%)
  starting transfers between devices  5.44 us (18%)
  between operations  0.73 us (2%)
    ppermute x6, waiting for transfers between devices, swap_pairs(): got.append(lax.ppermute(value, names, pairs))  6.87 us
    ppermute x6, starting transfers between devices, swap_pairs(): got.append(lax.ppermute(value, names, pairs))  5.44 us
    pallas_call x2, Pallas kernels, local(): pl.pallas_call(functools.partial(step_kernel, dims, mats, counts, True, l...  5.4 us
    pallas_call x2, Pallas kernels, local(): pl.pallas_call(functools.partial(step_kernel, dims, mats, counts, False,...  4.39 us
    pallas_call x1, Pallas kernels, local(): pl.pallas_call(functools.partial(window_kernel, dims, True), out_shape=wi...  2.66 us
    pallas_call x1, Pallas kernels, local(): pl.pallas_call(functools.partial(window_kernel, dims, False), out_shape=w...  2.26 us
    pallas_call x1, Pallas kernels, local(): pl.pallas_call(functools.partial(first_kernel, dims, n_col, n_row), out_s...  2.16 us
  transfers between devices with their start and end apart: 6, of which 2 were waited for; matrix products, arithmetic and copies ran while one was open for 0% of the time, Pallas kernels for 31%

profile of v6, /device:TPU:0, one launch (start us, length us, event | category | flops | bytes accessed | tf_op | source)
XLA Modules:
  0.0 29.9 jit_solution(2437500632502391874)
XLA Ops:
  0.6 0.0 copy-start
  0.6 0.0 copy-start.1
  0.7 0.0 copy-start.2
  0.7 2.2 %first.1 = (f32[32,1664]{1,0:T(8,128)S(1)}, f32[32,1664]{1,0:T(8,128)S(1)}, f32[2,8,1664]{2,1,0:T(8,128)S(1)}, f32[9,512,128]{2,1,0:T(8,128)S(1)}, f32[4,512,128]{2,1,0:T(8,128)S(1)}) custom-call(f32[512,1152]{1,0:T(8,128)} %bitcast.14, f32[4,512,128]{2,1,0:T(8,128)} %bitcast.15), custom_call_target="tpu_custom_call" | custom-call | tf_op jit(solution)/shard_map/first/pallas_call | solution.py:502
  2.8 0.6 %collective-permute-start = (f32[32,1664]{1,0:T(8,128)S(1)}, f32[32,1664]{1,0:T(8,128)S(1)}, u32[]{:S(2)}, u32[]{:S(2)}) collective-permute-start(f32[32,1664]{1,0:T(8,128)S(1)} %get-tuple-element.42), channel_id=1, source_target_pairs={{0,2},{1,3},{2,0},{3,1},{4,6},{5,7},{6,4},{7,5},{8,10},{9,11},{10,... | collective-permute-start | bytes 638984 | tf_op jit(solution)/shard_map/ppermute | solution.py:463
  3.4 2.6 %collective-permute-start.2 = (f32[32,1664]{1,0:T(8,128)S(1)}, f32[32,1664]{1,0:T(8,128)S(1)}, u32[]{:S(2)}, u32[]{:S(2)}) collective-permute-start(f32[32,1664]{1,0:T(8,128)S(1)} %get-tuple-element.45), channel_id=1, source_target_pairs={{0,1},{1,0},{2,4},{3,5},{4,2},{5,3},{6,8},{7,9},{8,6},{9,7},{10,12... | collective-permute-start | bytes 638984 | tf_op jit(solution)/shard_map/ppermute | solution.py:463
  6.0 0.1 collective-permute-start.1
  6.0 0.0 copy-done
  6.0 0.0 copy-done.1
  6.0 0.0 copy-done.2
  6.1 2.7 %window_first.1 = (f32[9,2,256,128]{3,2,1,0:T(8,128)S(1)}, f32[4,2,256,128]{3,2,1,0:T(8,128)S(1)}, f32[4,2,256,128]{3,2,1,0:T(8,128)S(1)}, f32[2,2,256,128]{3,2,...) custom-call(f32[9,512,128]{2,1,0:T(8,128)S(1)} %get-tuple-element.32, ...), custom_call_target="tpu_custom_call" | custom-call | tf_op jit(solution)/shard_map/window_first/pallas_call | solution.py:517
  8.7 3.4 %collective-permute-done.1.refs_10_ = f32[2,8,1664]{2,1,0:T(8,128)S(1)} collective-permute-done((f32[2,8,1664]{2,1,0:T(8,128)S(1)}, f32[2,8,1664]{2,1,0:T(8,128)S(1)}, u32[]{:S(2)}, u32[]{:S(2)}) %collective-permute-start.1) | collective-permute-done | bytes 106528 | tf_op jit(solution)/shard_map/ppermute | solution.py:463
  12.1 0.0 collective-permute-done.refs_9_
  12.1 2.2 %early.1 = (f32[9,2,256,128]{3,2,1,0:T(8,128)S(1)}, f32[9,2,256,128]{3,2,1,0:T(8,128)S(1)}, f32[4,2,256,128]{3,2,1,0:T(8,128)S(1)}) custom-call(f32[2,1152]{1,0:T(2,128)S(1)} %copy-done, f32[9,2,256,128]{3,2,1,0:T(8,128)S(1)} %get-tuple-element.34.refs_1_, f32[4,2,256,128]{3,2,1,0:T(8,128)S(1)} %get-tuple-element.35.refs_2_, ...), custom_call_target="tpu_custom_call", output_to_operand_aliasing={{0}: (1, {})} | custom-call | tf_op jit(solution)/shard_map/early/pallas_call | solution.py:551
  14.3 0.0 collective-permute-done.2.refs_9_
  14.3 2.3 %late.1 = (f32[9,2,256,128]{3,2,1,0:T(8,128)S(1)}, f32[9,2,256,128]{3,2,1,0:T(8,128)S(1)}, f32[4,2,256,128]{3,2,1,0:T(8,128)S(1)}, f32[32,1664]{1,0:T(8,128)S(1)...) custom-call(f32[2,1152]{1,0:T(2,128)S(1)} %copy-done, ...), custom_call_target="tpu_custom_call", output_to_operand_aliasing={{0}: (1, {}), {1}: (11, {}), {2}: (12, {})} | custom-call | tf_op jit(solution)/shard_map/late/pallas_call | solution.py:575
  16.6 0.1 collective-permute-start.3
  16.7 2.1 %collective-permute-start.5 = (f32[32,1664]{1,0:T(8,128)S(1)}, f32[32,1664]{1,0:T(8,128)S(1)}, u32[]{:S(2)}, u32[]{:S(2)}) collective-permute-start(f32[32,1664]{1,0:T(8,128)S(1)} %get-tuple-element.57), channel_id=1, source_target_pairs={{0,1},{1,0},{2,4},{3,5},{4,2},{5,3},{6,8},{7,9},{8,6},{9,7},{10,12... | collective-permute-start | bytes 638984 | tf_op jit(solution)/shard_map/ppermute | solution.py:463
  18.7 0.1 collective-permute-start.4
  18.8 2.3 %window.1 = (f32[9,2,256,128]{3,2,1,0:T(8,128)S(1)}, f32[4,2,256,128]{3,2,1,0:T(8,128)S(1)}, f32[4,2,256,128]{3,2,1,0:T(8,128)S(1)}, f32[2,2,256,128]{3,2,1,0:T(8,128)S(1)}) custom-call(f32[9,2,256,128]{3,2,1,0:T(8,128)S(1)} %get-tuple-element.48.e_ref, f32[4,2,256,128]{3,2,1,0:T(8,128)S(1)} %get-tuple-element.49.o_ref, ...), custom_call_target="tpu_custom_call" | custom-call | tf_op jit(solution)/shard_map/window/pallas_call | solution.py:533
  21.1 3.5 %collective-permute-done.4.refs_10_ = f32[2,8,1664]{2,1,0:T(8,128)S(1)} collective-permute-done((f32[2,8,1664]{2,1,0:T(8,128)S(1)}, f32[2,8,1664]{2,1,0:T(8,128)S(1)}, u32[]{:S(2)}, u32[]{:S(2)}) %collective-permute-start.4) | collective-permute-done | bytes 106528 | tf_op jit(solution)/shard_map/ppermute | solution.py:463
  24.6 0.0 collective-permute-done.3.refs_9_
  24.6 2.2 %early_last.1 = (f32[9,2,256,128]{3,2,1,0:T(8,128)S(1)}, f32[1,32,8,1152]{3,2,1,0:T(8,128)S(1)}, f32[1,4,256,128]{3,2,1,0:T(8,128)S(1)}) custom-call(f32[2,1152]{1,0:T(2,128)S(1)} %copy-done, f32[9,2,256,128]{3,2,1,0:T(8,128)S(1)} %get-tuple-element.50.refs_1_, f32[4,2,256,128]{3,2,1,0:T(8,128)S(1)} %get-tuple-element.51.refs_2_, ...), custom_call_target="tpu_custom_call", output_to_operand_aliasing={{0}: (1, {})} | custom-call | tf_op jit(solution)/shard_map/early_last/pallas_call | solution.py:551
  26.8 0.0 collective-permute-done.5.refs_9_
  26.8 3.1 %late_last.1 = (f32[9,2,256,128]{3,2,1,0:T(8,128)S(1)}, f32[32,2,8,1152]{3,2,1,0:T(8,128)}, f32[4,32,2,8,128]{4,3,2,1,0:T(8,128)}) custom-call(f32[2,1152]{1,0:T(2,128)S(1)} %copy-done, f32[9,2,256,128]{3,2,1,0:T(8,128)S(1)} %get-tuple-element.56.refs_1_, f32[4,2,256,128]{3,2,1,0:T(8,128)S(1)} %get-tuple-element.51.refs_2_, ...), custom_call_target="tpu_custom_call", output_to_operand_aliasing={{0}: (1, {})} | custom-call | tf_op jit(solution)/shard_map/late_last/pallas_call | solution.py:575
Async XLA Ops:
  0.6 5.4 %copy-start = (f32[2,1152]{1,0:T(2,128)S(1)}, f32[2,1152]{1,0:T(2,128)}, u32[]{:S(2)}) copy-start(f32[2,1152]{1,0:T(2,128)} %refs_0_.7) | copy-start | bytes 27652
  0.6 5.4 %copy-start.1 = (s32[32,16]{0,1:T(8,128)S(1)}, s32[32,16]{0,1:T(8,128)}, u32[]{:S(2)}) copy-start(s32[32,16]{0,1:T(8,128)} %param.10) | copy-start | bytes 6148
  0.7 5.4 %copy-start.2 = (s32[32,16]{0,1:T(8,128)S(1)}, s32[32,16]{0,1:T(8,128)}, u32[]{:S(2)}) copy-start(s32[32,16]{0,1:T(8,128)} %param.9) | copy-start | bytes 6148
  2.8 9.2 %collective-permute-start = (f32[32,1664]{1,0:T(8,128)S(1)}, f32[32,1664]{1,0:T(8,128)S(1)}, u32[]{:S(2)}, u32[]{:S(2)}) collective-permute-start(f32[32,1664]{1,0:T(8,128)S(1)} %get-tuple-element.42), channel_id=1, source_target_pairs={{0,2},{1,3},{2,0},{3,1},{4,6},{5,7},{6,4},{7,5},{8,10},{9,11},{10,... | collective-permute-start | bytes 638984 | tf_op jit(solution)/shard_map/ppermute | solution.py:463
  3.4 10.9 %collective-permute-start.2 = (f32[32,1664]{1,0:T(8,128)S(1)}, f32[32,1664]{1,0:T(8,128)S(1)}, u32[]{:S(2)}, u32[]{:S(2)}) collective-permute-start(f32[32,1664]{1,0:T(8,128)S(1)} %get-tuple-element.45), channel_id=1, source_target_pairs={{0,1},{1,0},{2,4},{3,5},{4,2},{5,3},{6,8},{7,9},{8,6},{9,7},{10,12... | collective-permute-start | bytes 638984 | tf_op jit(solution)/shard_map/ppermute | solution.py:463
  6.0 6.1 %collective-permute-start.1 = (f32[2,8,1664]{2,1,0:T(8,128)S(1)}, f32[2,8,1664]{2,1,0:T(8,128)S(1)}, u32[]{:S(2)}, u32[]{:S(2)}) collective-permute-start(f32[2,8,1664]{2,1,0:T(8,128)S(1)} %get-tuple-element.43), channel_id=1, source_target_pairs={{0,1},{2,3},{4,5},{6,7},{8,9},{10,11},{12,13},{14,15},{16,17},{18,... | collective-permute-start | bytes 319496 | tf_op jit(solution)/shard_map/ppermute | solution.py:463
  16.6 8.0 %collective-permute-start.3 = (f32[32,1664]{1,0:T(8,128)S(1)}, f32[32,1664]{1,0:T(8,128)S(1)}, u32[]{:S(2)}, u32[]{:S(2)}) collective-permute-start(f32[32,1664]{1,0:T(8,128)S(1)} %get-tuple-element.54), channel_id=1, source_target_pairs={{0,2},{1,3},{2,0},{3,1},{4,6},{5,7},{6,4},{7,5},{8,10},{9,11},{10,... | collective-permute-start | bytes 638984 | tf_op jit(solution)/shard_map/ppermute | solution.py:463
  16.7 10.1 %collective-permute-start.5 = (f32[32,1664]{1,0:T(8,128)S(1)}, f32[32,1664]{1,0:T(8,128)S(1)}, u32[]{:S(2)}, u32[]{:S(2)}) collective-permute-start(f32[32,1664]{1,0:T(8,128)S(1)} %get-tuple-element.57), channel_id=1, source_target_pairs={{0,1},{1,0},{2,4},{3,5},{4,2},{5,3},{6,8},{7,9},{8,6},{9,7},{10,12... | collective-permute-start | bytes 638984 | tf_op jit(solution)/shard_map/ppermute | solution.py:463
  18.7 5.8 %collective-permute-start.4 = (f32[2,8,1664]{2,1,0:T(8,128)S(1)}, f32[2,8,1664]{2,1,0:T(8,128)S(1)}, u32[]{:S(2)}, u32[]{:S(2)}) collective-permute-start(f32[2,8,1664]{2,1,0:T(8,128)S(1)} %get-tuple-element.55), channel_id=1, source_target_pairs={{0,1},{2,3},{4,5},{6,7},{8,9},{10,11},{12,13},{14,15},{16,17},{18,... | collective-permute-start | bytes 319496 | tf_op jit(solution)/shard_map/ppermute | solution.py:463

commit v7 on v6

--- a/solution.py
+++ b/solution.py
@@ -116,7 +116,7 @@
     return slice(r * SUBLANES, (r + 1) * SUBLANES)
 
 
-def advect_all(dims, energy_at, flow_ref, mask_ref, courant_ref, adv_ref):
+def advect_all(dims, energy_at, flow_ref, courant_ref, adv_ref):
     rows, cols, bins, _, _ = dims
     ends = sublane_ends()
     tiles = cols // SUBLANES
@@ -148,7 +148,7 @@
                 speed_y = speeds[1] + flow_ref[1, i, span(r), :]
                 flux = speed_x * jnp.where(speed_x > 0, mid[i] - west[i], east[i] - mid[i])
                 flux = flux + speed_y * jnp.where(speed_y > 0, falls[i], falls_next[i])
-                adv_ref[k, i, span(r), :] = mask_ref[i, span(r), :] * (mid[i] - flux)
+                adv_ref[k, i, span(r), :] = mid[i] - flux
             mid, falls = following, falls_next
         return 0
 
@@ -208,7 +208,7 @@
         for copy in copies:
             copy.start()
         mask = mask_t[...].astype(F32)
-        owner = owner_t[...]
+        owner = jnp.where(mask_t[...] == 1, owner_t[...], -1)
         for i in range(tiles):
             for r in range(rows):
                 for to_ref, values in ((mask_ref, mask), (owner_ref, owner)):
@@ -232,7 +232,7 @@
                     current_gain * ocean_at(way, i, r)[:, 0:1], (SUBLANES, LANES)
                 )
     ocean_all(dims, ocean_at, mask_ref, part_ref, grad_ref)
-    advect_all(dims, energy_at, flow_ref, mask_ref, courant_ref, adv_ref)
+    advect_all(dims, energy_at, flow_ref, courant_ref, adv_ref)
     for copy in copies:
         copy.wait()
 
@@ -250,30 +250,28 @@
     return value if valid is None else jnp.where(valid, value, 0.0)
 
 
-def fix_column(dims, parity, index, valid, halo_ref, flow_ref, mask_ref, courant_ref, adv_ref):
+def fix_column(dims, parity, index, valid, halo_ref, flow_ref, courant_ref, adv_ref):
     tile, spots = column_place(dims, parity, index)
     sign = side_sign(parity, index)
-    sea = mask_ref[tile, spots, :]
     speed = flow_ref[0, tile, spots, :]
     for k in range(dims[2] // LANES):
         lanes = slice(k * LANES, (k + 1) * LANES)
         inward = jnp.maximum(sign * (courant_ref[0:1, lanes] + speed), 0.0)
         adv_ref[k, tile, spots, :] = (
-            adv_ref[k, tile, spots, :] + sea * inward * kept(valid, halo_ref[:, lanes])
+            adv_ref[k, tile, spots, :] + inward * kept(valid, halo_ref[:, lanes])
         )
 
 
-def fix_row(dims, parity, index, valid, halo_ref, flow_ref, mask_ref, courant_ref, adv_ref):
+def fix_row(dims, parity, index, valid, halo_ref, flow_ref, courant_ref, adv_ref):
     spots = row_place(dims, parity, index)
     sign = side_sign(parity, index)
     for i in range(dims[1] // SUBLANES):
-        sea = mask_ref[i, spots, :]
         speed = flow_ref[1, i, spots, :]
         for k in range(dims[2] // LANES):
             lanes = slice(k * LANES, (k + 1) * LANES)
             inward = jnp.maximum(sign * (courant_ref[1:2, lanes] + speed), 0.0)
             adv_ref[k, i, spots, :] = (
-                adv_ref[k, i, spots, :] + sea * inward * kept(valid, halo_ref[i, :, lanes])
+                adv_ref[k, i, spots, :] + inward * kept(valid, halo_ref[i, :, lanes])
             )
 
 
@@ -381,7 +379,7 @@
             copies += store(number, e_early.at[number], o_early.at[number])
         for copy in copies:
             copy.start()
-    fixed = (flow_ref, mask_ref, courant_ref, adv_ref)
+    fixed = (flow_ref, courant_ref, adv_ref)
     if not late:
         for row_index in range(n_row):
             fix_row(

time: 30 us -> 30 us (level)
  no operation moved by 1% of the time
where the time goes in v7:
time: 30 us; the launch traced here: 29.9 us
  Pallas kernels  16.7 us (56%)
  waiting for transfers between devices  6.97 us (23%)
  starting transfers between devices  5.45 us (18%)
  between operations  0.73 us (2%)
    ppermute x6, waiting for transfers between devices, swap_pairs(): got.append(lax.ppermute(value, names, pairs))  6.97 us
    ppermute x6, starting transfers between devices, swap_pairs(): got.append(lax.ppermute(value, names, pairs))  5.45 us
    pallas_call x2, Pallas kernels, local(): pl.pallas_call(functools.partial(step_kernel, dims, mats, counts, True, l...  5.38 us
    pallas_call x2, Pallas kernels, local(): pl.pallas_call(functools.partial(step_kernel, dims, mats, counts, False,...  4.38 us
    pallas_call x1, Pallas kernels, local(): pl.pallas_call(functools.partial(window_kernel, dims, True), out_shape=wi...  2.66 us
    pallas_call x1, Pallas kernels, local(): pl.pallas_call(functools.partial(window_kernel, dims, False), out_shape=w...  2.16 us
    pallas_call x1, Pallas kernels, local(): pl.pallas_call(functools.partial(first_kernel, dims, n_col, n_row), out_s...  2.16 us
  transfers between devices with their start and end apart: 6, of which 2 were waited for; matrix products, arithmetic and copies ran while one was open for 0% of the time, Pallas kernels for 31%

profile of v7, /device:TPU:0, one launch (start us, length us, event | category | flops | bytes accessed | tf_op | source)
XLA Modules:
  0.0 29.9 jit_solution(18333473126681304243)
XLA Ops:
  0.6 0.0 copy-start
  0.6 0.0 copy-start.1
  0.7 0.0 copy-start.2
  0.7 2.2 %first.1 = (f32[32,1664]{1,0:T(8,128)S(1)}, f32[32,1664]{1,0:T(8,128)S(1)}, f32[2,8,1664]{2,1,0:T(8,128)S(1)}, f32[9,512,128]{2,1,0:T(8,128)S(1)}, f32[4,512,128]{2,1,0:T(8,128)S(1)}) custom-call(f32[512,1152]{1,0:T(8,128)} %bitcast.14, f32[4,512,128]{2,1,0:T(8,128)} %bitcast.15), custom_call_target="tpu_custom_call" | custom-call | tf_op jit(solution)/shard_map/first/pallas_call | solution.py:500
  2.8 0.6 %collective-permute-start = (f32[32,1664]{1,0:T(8,128)S(1)}, f32[32,1664]{1,0:T(8,128)S(1)}, u32[]{:S(2)}, u32[]{:S(2)}) collective-permute-start(f32[32,1664]{1,0:T(8,128)S(1)} %get-tuple-element.42), channel_id=1, source_target_pairs={{0,2},{1,3},{2,0},{3,1},{4,6},{5,7},{6,4},{7,5},{8,10},{9,11},{10,... | collective-permute-start | bytes 638984 | tf_op jit(solution)/shard_map/ppermute | solution.py:461
  3.4 2.6 %collective-permute-start.2 = (f32[32,1664]{1,0:T(8,128)S(1)}, f32[32,1664]{1,0:T(8,128)S(1)}, u32[]{:S(2)}, u32[]{:S(2)}) collective-permute-start(f32[32,1664]{1,0:T(8,128)S(1)} %get-tuple-element.45), channel_id=1, source_target_pairs={{0,1},{1,0},{2,4},{3,5},{4,2},{5,3},{6,8},{7,9},{8,6},{9,7},{10,12... | collective-permute-start | bytes 638984 | tf_op jit(solution)/shard_map/ppermute | solution.py:461
  6.0 0.1 collective-permute-start.1
  6.0 0.0 copy-done
  6.0 0.0 copy-done.1
  6.0 0.0 copy-done.2
  6.1 2.7 %window_first.1 = (f32[9,2,256,128]{3,2,1,0:T(8,128)S(1)}, f32[4,2,256,128]{3,2,1,0:T(8,128)S(1)}, f32[4,2,256,128]{3,2,1,0:T(8,128)S(1)}, f32[2,2,256,128]{3,2,...) custom-call(f32[9,512,128]{2,1,0:T(8,128)S(1)} %get-tuple-element.32, ...), custom_call_target="tpu_custom_call" | custom-call | tf_op jit(solution)/shard_map/window_first/pallas_call | solution.py:515
  8.7 3.4 %collective-permute-done.1.refs_10_ = f32[2,8,1664]{2,1,0:T(8,128)S(1)} collective-permute-done((f32[2,8,1664]{2,1,0:T(8,128)S(1)}, f32[2,8,1664]{2,1,0:T(8,128)S(1)}, u32[]{:S(2)}, u32[]{:S(2)}) %collective-permute-start.1) | collective-permute-done | bytes 106528 | tf_op jit(solution)/shard_map/ppermute | solution.py:461
  12.1 0.0 collective-permute-done.refs_9_
  12.1 2.2 %early.1 = (f32[9,2,256,128]{3,2,1,0:T(8,128)S(1)}, f32[9,2,256,128]{3,2,1,0:T(8,128)S(1)}, f32[4,2,256,128]{3,2,1,0:T(8,128)S(1)}) custom-call(f32[2,1152]{1,0:T(2,128)S(1)} %copy-done, f32[9,2,256,128]{3,2,1,0:T(8,128)S(1)} %get-tuple-element.34.refs_1_, f32[4,2,256,128]{3,2,1,0:T(8,128)S(1)} %get-tuple-element.35.refs_2_, ...), custom_call_target="tpu_custom_call", output_to_operand_aliasing={{0}: (1, {})} | custom-call | tf_op jit(solution)/shard_map/early/pallas_call | solution.py:549
  14.3 0.0 collective-permute-done.2.refs_9_
  14.3 2.3 %late.1 = (f32[9,2,256,128]{3,2,1,0:T(8,128)S(1)}, f32[9,2,256,128]{3,2,1,0:T(8,128)S(1)}, f32[4,2,256,128]{3,2,1,0:T(8,128)S(1)}, f32[32,1664]{1,0:T(8,128)S(1)...) custom-call(f32[2,1152]{1,0:T(2,128)S(1)} %copy-done, ...), custom_call_target="tpu_custom_call", output_to_operand_aliasing={{0}: (1, {}), {1}: (11, {}), {2}: (12, {})} | custom-call | tf_op jit(solution)/shard_map/late/pallas_call | solution.py:573
  16.6 0.1 collective-permute-start.3
  16.6 2.1 %collective-permute-start.5 = (f32[32,1664]{1,0:T(8,128)S(1)}, f32[32,1664]{1,0:T(8,128)S(1)}, u32[]{:S(2)}, u32[]{:S(2)}) collective-permute-start(f32[32,1664]{1,0:T(8,128)S(1)} %get-tuple-element.57), channel_id=1, source_target_pairs={{0,1},{1,0},{2,4},{3,5},{4,2},{5,3},{6,8},{7,9},{8,6},{9,7},{10,12... | collective-permute-start | bytes 638984 | tf_op jit(solution)/shard_map/ppermute | solution.py:461
  18.7 0.1 collective-permute-start.4
  18.8 2.2 %window.1 = (f32[9,2,256,128]{3,2,1,0:T(8,128)S(1)}, f32[4,2,256,128]{3,2,1,0:T(8,128)S(1)}, f32[4,2,256,128]{3,2,1,0:T(8,128)S(1)}, f32[2,2,256,128]{3,2,1,0:T(8,128)S(1)}) custom-call(f32[9,2,256,128]{3,2,1,0:T(8,128)S(1)} %get-tuple-element.48.e_ref, f32[4,2,256,128]{3,2,1,0:T(8,128)S(1)} %get-tuple-element.49.o_ref, ...), custom_call_target="tpu_custom_call" | custom-call | tf_op jit(solution)/shard_map/window/pallas_call | solution.py:531
  21.0 3.6 %collective-permute-done.4.refs_10_ = f32[2,8,1664]{2,1,0:T(8,128)S(1)} collective-permute-done((f32[2,8,1664]{2,1,0:T(8,128)S(1)}, f32[2,8,1664]{2,1,0:T(8,128)S(1)}, u32[]{:S(2)}, u32[]{:S(2)}) %collective-permute-start.4) | collective-permute-done | bytes 106528 | tf_op jit(solution)/shard_map/ppermute | solution.py:461
  24.6 0.0 collective-permute-done.3.refs_9_
  24.6 2.2 %early_last.1 = (f32[9,2,256,128]{3,2,1,0:T(8,128)S(1)}, f32[1,32,8,1152]{3,2,1,0:T(8,128)S(1)}, f32[1,4,256,128]{3,2,1,0:T(8,128)S(1)}) custom-call(f32[2,1152]{1,0:T(2,128)S(1)} %copy-done, f32[9,2,256,128]{3,2,1,0:T(8,128)S(1)} %get-tuple-element.50.refs_1_, f32[4,2,256,128]{3,2,1,0:T(8,128)S(1)} %get-tuple-element.51.refs_2_, ...), custom_call_target="tpu_custom_call", output_to_operand_aliasing={{0}: (1, {})} | custom-call | tf_op jit(solution)/shard_map/early_last/pallas_call | solution.py:549
  26.8 0.0 collective-permute-done.5.refs_9_
  26.8 3.1 %late_last.1 = (f32[9,2,256,128]{3,2,1,0:T(8,128)S(1)}, f32[32,2,8,1152]{3,2,1,0:T(8,128)}, f32[4,32,2,8,128]{4,3,2,1,0:T(8,128)}) custom-call(f32[2,1152]{1,0:T(2,128)S(1)} %copy-done, f32[9,2,256,128]{3,2,1,0:T(8,128)S(1)} %get-tuple-element.56.refs_1_, f32[4,2,256,128]{3,2,1,0:T(8,128)S(1)} %get-tuple-element.51.refs_2_, ...), custom_call_target="tpu_custom_call", output_to_operand_aliasing={{0}: (1, {})} | custom-call | tf_op jit(solution)/shard_map/late_last/pallas_call | solution.py:573
Async XLA Ops:
  0.6 5.4 %copy-start = (f32[2,1152]{1,0:T(2,128)S(1)}, f32[2,1152]{1,0:T(2,128)}, u32[]{:S(2)}) copy-start(f32[2,1152]{1,0:T(2,128)} %refs_0_.7) | copy-start | bytes 27652
  0.6 5.4 %copy-start.1 = (s32[32,16]{0,1:T(8,128)S(1)}, s32[32,16]{0,1:T(8,128)}, u32[]{:S(2)}) copy-start(s32[32,16]{0,1:T(8,128)} %param.10) | copy-start | bytes 6148
  0.7 5.4 %copy-start.2 = (s32[32,16]{0,1:T(8,128)S(1)}, s32[32,16]{0,1:T(8,128)}, u32[]{:S(2)}) copy-start(s32[32,16]{0,1:T(8,128)} %param.9) | copy-start | bytes 6148
  2.8 9.2 %collective-permute-start = (f32[32,1664]{1,0:T(8,128)S(1)}, f32[32,1664]{1,0:T(8,128)S(1)}, u32[]{:S(2)}, u32[]{:S(2)}) collective-permute-start(f32[32,1664]{1,0:T(8,128)S(1)} %get-tuple-element.42), channel_id=1, source_target_pairs={{0,2},{1,3},{2,0},{3,1},{4,6},{5,7},{6,4},{7,5},{8,10},{9,11},{10,... | collective-permute-start | bytes 638984 | tf_op jit(solution)/shard_map/ppermute | solution.py:461
  3.4 10.9 %collective-permute-start.2 = (f32[32,1664]{1,0:T(8,128)S(1)}, f32[32,1664]{1,0:T(8,128)S(1)}, u32[]{:S(2)}, u32[]{:S(2)}) collective-permute-start(f32[32,1664]{1,0:T(8,128)S(1)} %get-tuple-element.45), channel_id=1, source_target_pairs={{0,1},{1,0},{2,4},{3,5},{4,2},{5,3},{6,8},{7,9},{8,6},{9,7},{10,12... | collective-permute-start | bytes 638984 | tf_op jit(solution)/shard_map/ppermute | solution.py:461
  6.0 6.1 %collective-permute-start.1 = (f32[2,8,1664]{2,1,0:T(8,128)S(1)}, f32[2,8,1664]{2,1,0:T(8,128)S(1)}, u32[]{:S(2)}, u32[]{:S(2)}) collective-permute-start(f32[2,8,1664]{2,1,0:T(8,128)S(1)} %get-tuple-element.43), channel_id=1, source_target_pairs={{0,1},{2,3},{4,5},{6,7},{8,9},{10,11},{12,13},{14,15},{16,17},{18,... | collective-permute-start | bytes 319496 | tf_op jit(solution)/shard_map/ppermute | solution.py:461
  16.6 8.0 %collective-permute-start.3 = (f32[32,1664]{1,0:T(8,128)S(1)}, f32[32,1664]{1,0:T(8,128)S(1)}, u32[]{:S(2)}, u32[]{:S(2)}) collective-permute-start(f32[32,1664]{1,0:T(8,128)S(1)} %get-tuple-element.54), channel_id=1, source_target_pairs={{0,2},{1,3},{2,0},{3,1},{4,6},{5,7},{6,4},{7,5},{8,10},{9,11},{10,... | collective-permute-start | bytes 638984 | tf_op jit(solution)/shard_map/ppermute | solution.py:461
  16.6 10.1 %collective-permute-start.5 = (f32[32,1664]{1,0:T(8,128)S(1)}, f32[32,1664]{1,0:T(8,128)S(1)}, u32[]{:S(2)}, u32[]{:S(2)}) collective-permute-start(f32[32,1664]{1,0:T(8,128)S(1)} %get-tuple-element.57), channel_id=1, source_target_pairs={{0,1},{1,0},{2,4},{3,5},{4,2},{5,3},{6,8},{7,9},{8,6},{9,7},{10,12... | collective-permute-start | bytes 638984 | tf_op jit(solution)/shard_map/ppermute | solution.py:461
  18.7 5.8 %collective-permute-start.4 = (f32[2,8,1664]{2,1,0:T(8,128)S(1)}, f32[2,8,1664]{2,1,0:T(8,128)S(1)}, u32[]{:S(2)}, u32[]{:S(2)}) collective-permute-start(f32[2,8,1664]{2,1,0:T(8,128)S(1)} %get-tuple-element.55), channel_id=1, source_target_pairs={{0,1},{2,3},{4,5},{6,7},{8,9},{10,11},{12,13},{14,15},{16,17},{18,... | collective-permute-start | bytes 319496 | tf_op jit(solution)/shard_map/ppermute | solution.py:461
